TPU v7x, 128 devices: a whole 4x4x4 slice. The times are simulated.
128 devices in a mesh: ctx: 32 (over x_lo, y, z), tp: 4 (over x_hi, core).
Axes of the slice: x: 4 (x_hi: 2, x_lo: 2; x = x_hi * 2 + x_lo), y: 4, z: 4, core: 2. Of those that a mesh axis runs over, the one named last changes fastest.
Arguments:
- query_rows: bfloat16 [16384, 2048], P('ctx', 'tp'), may hold values from -5 to 5
- key_rows: bfloat16 [16384, 1024], P('ctx', 'tp'), may hold values from -5 to 5
- value_rows: bfloat16 [16384, 1024], P('ctx', 'tp'), may hold values from -6 to 6
Outputs:
- attended: bfloat16 [16384, 2048], P(('ctx', 'tp'))
All inputs are finite; a program needn't handle non-finite values.
Results may differ from a plain program's by a relative error of at most 0.009.
Values may be sent and summed in bfloat16 or wider, within the bound.
No kernel may reach another device: no remote copies, remote signals or barrier semaphores. Data moves between devices by JAX's collectives and lax.ppermute only.
A program may use at most 192 MiB of HBM per device.

v0:
```python
import functools

import jax
import jax.numpy as jnp
from jax import lax
from jax.experimental import pallas as pl
from jax.experimental.pallas import tpu as pltpu
from jax.sharding import Mesh, PartitionSpec as P

HEAD_DIM = 128
SCALAR = 168
SCALE = SCALAR ** (-0.5) * 1.4426950408889634
LOWEST = -1e30
BLOCK = 512
ROWS = 2 * BLOCK
EXT = HEAD_DIM + 16
STRIP = 256
STRIPS = ROWS // STRIP

CONTRACT_LAST = (((1,), (1,)), ((), ()))
PARAMS = pltpu.CompilerParams(vmem_limit_bytes=30 * 2**20)


def vmem(count):
    return [pl.BlockSpec(memory_space=pltpu.VMEM)] * count


def smem():
    return pl.BlockSpec(memory_space=pltpu.SMEM)


def pack_keys_kernel(place, key_ref, value_ref, kv_own, kv_other):
    half = place[0]
    for head, kv_out in ((1 - half, kv_other), (half, kv_own)):
        at = pl.multiple_of(head * 128, 128)
        kv_out[:BLOCK] = key_ref[:, pl.ds(at, 128)]
        for part in range(4):
            rows = value_ref[part * 128 : (part + 1) * 128, pl.ds(at, 128)]
            kv_out[BLOCK + part * 128 : BLOCK + (part + 1) * 128] = (
                rows.astype(jnp.float32).T.astype(jnp.bfloat16)
            )


def pack_queries_kernel(place, query_ref, after, q_own, q_other):
    half = place[0]
    for head, q_out in ((1 - half, q_other), (half, q_own)):
        for part in range(2):
            at = pl.multiple_of(head * 256 + part * 128, 128)
            q_out[part * BLOCK : (part + 1) * BLOCK] = query_ref[:, pl.ds(at, 128)]


def whole(shape):
    return pl.BlockSpec(shape, lambda _: (0,) * len(shape))


def attend_kernel(step, place, q_ref, kv_ref, out_ref, best, acc, held, peak, todo):
    half, y, z = place[0], place[1], place[2]
    own_row = 4 * half + y
    kv_rows = (own_row, 7 - own_row)
    back = lax.rem(y - step + 4, 4)
    q_rows = (4 * half + back, 4 * (1 - half) + back)

    def keys_of(tile):
        _, row, pair = tile
        at = 4 * row + 2 * pair
        return jnp.concatenate([kv_ref[at + part, :BLOCK] for part in range(2)], axis=0)

    def values_of(tile):
        _, row, pair = tile
        at = 4 * row + 2 * pair
        flipped = [
            kv_ref[at + part, BLOCK + piece * 128 : BLOCK + (piece + 1) * 128]
            for part in range(2)
            for piece in range(4)
        ]
        ones = jnp.ones((EXT - HEAD_DIM, 2 * BLOCK), jnp.bfloat16)
        return jnp.concatenate([jnp.concatenate(flipped, axis=1), ones], axis=0)

    def score(tile, keys, strip, mask=None):
        part = lax.dot_general(
            keys,
            q_ref[tile[0], strip * STRIP : (strip + 1) * STRIP],
            CONTRACT_LAST,
            preferred_element_type=jnp.float32,
        )
        if mask is not None:
            part = mask(part, strip)
        held[strip] = part
        peak[strip] = jnp.max(part, axis=0, keepdims=True)

    def update(tile, values, strip):
        slot = tile[0]
        old = best[slot, strip]
        new = jnp.maximum(old, peak[strip])
        weights = jnp.exp2(held[strip] * SCALE - new * SCALE)
        rescale = jnp.exp2((old - new) * SCALE)
        best[slot, strip] = new
        acc[slot, strip] = acc[slot, strip] * rescale + jnp.dot(
            values, weights.astype(jnp.bfloat16), preferred_element_type=jnp.float32
        )

    best[...] = jnp.full_like(best, LOWEST)
    acc[...] = jnp.zeros_like(acc)
    todo[0] = 0
    for slot in range(2):
        for row in range(2):

            @pl.when(kv_rows[row] < q_rows[slot])
            def _():
                count = todo[0]
                todo[1 + count] = 2 * slot + row
                todo[0] = count + 1

    def tile_at(at):
        entry = todo[1 + at // 2]
        return entry // 2, entry % 2, at % 2

    count = 2 * todo[0]

    @pl.when(count > 0)
    def _():
        start = tile_at(0)
        keys = keys_of(start)
        for strip in range(STRIPS):
            score(start, keys, strip)

        def step_on(at):
            now, later = tile_at(at), tile_at(at + 1)
            values, keys = values_of(now), keys_of(later)
            for strip in range(STRIPS):
                update(now, values, strip)
                score(later, keys, strip)

        def one(at, _):
            step_on(2 * at)
            step_on(2 * at + 1)
            return 0

        lax.fori_loop(0, todo[0] - 1, one, 0)
        step_on(count - 2)
        last = tile_at(count - 1)
        values = values_of(last)
        for strip in range(STRIPS):
            update(last, values, strip)

    def on_the_diagonal(slot, row):
        def causal(part, strip):
            key_at = lax.broadcasted_iota(jnp.int32, (BLOCK, STRIP), 0)
            token = lax.broadcasted_iota(jnp.int32, (BLOCK, STRIP), 1) + strip * STRIP % BLOCK
            near = jnp.where(key_at <= token, part[:BLOCK], LOWEST)
            return jnp.concatenate([near, jnp.where(z >= 1, part[BLOCK:], LOWEST)], axis=0)

        def far(part, strip):
            return jnp.concatenate(
                [part[:BLOCK], jnp.where(z >= 3, part[BLOCK:], LOWEST)], axis=0
            )

        def alone(pair, mask):
            tile = (slot, row, pair)
            keys, values = keys_of(tile), values_of(tile)
            for strip in range(STRIPS):
                score(tile, keys, strip, mask)
            for strip in range(STRIPS):
                update(tile, values, strip)

        alone(0, causal)
        pl.when(z >= 2)(lambda: alone(1, far))

    if step == 0:
        on_the_diagonal(0, 0)
    if step % 2 == 1:
        pl.when(kv_rows[1] == q_rows[1])(lambda: on_the_diagonal(1, 1))

    index = lax.broadcasted_iota(jnp.int32, (EXT - HEAD_DIM, STRIP), 0)
    for slot in range(2):
        for strip in range(STRIPS):
            at = slice(strip * STRIP, (strip + 1) * STRIP)
            total = acc[slot, strip, HEAD_DIM : HEAD_DIM + 1]
            empty = total == 0.0
            inverse = 1.0 / jnp.where(empty, 1.0, total)
            out_ref[slot, :HEAD_DIM, at] = (acc[slot, strip, :HEAD_DIM] * inverse).astype(
                jnp.bfloat16
            )
            level = best[slot, strip] * SCALE + jnp.log2(jnp.where(empty, 1.0, total))
            high = level.astype(jnp.bfloat16).astype(jnp.float32)
            middle = (level - high).astype(jnp.bfloat16).astype(jnp.float32)
            low = level - high - middle
            rows = jnp.where(index == 0, high, jnp.where(index == 1, middle, low))
            out_ref[slot, HEAD_DIM:, at] = rows.astype(jnp.bfloat16)


def attend(step, place, queries, blocks):
    return pl.pallas_call(
        functools.partial(attend_kernel, step),
        out_shape=jax.ShapeDtypeStruct((2, EXT, ROWS), jnp.bfloat16),
        in_specs=[smem()] + vmem(2),
        out_specs=vmem(1)[0],
        scratch_shapes=[
            pltpu.VMEM((2, STRIPS, 1, STRIP), jnp.float32),
            pltpu.VMEM((2, STRIPS, EXT, STRIP), jnp.float32),
            pltpu.VMEM((STRIPS, 2 * BLOCK, STRIP), jnp.float32),
            pltpu.VMEM((STRIPS, 1, STRIP), jnp.float32),
            pltpu.SMEM((8,), jnp.int32),
        ],
        compiler_params=PARAMS,
        name=f"attend{step}",
    )(place, queries, blocks)


def merge_kernel(place, *refs):
    parts, out_ref = refs[:4], refs[4]
    half = place[0]
    for slot in range(2):
        levels = []
        for part in parts:
            tail = part[slot, HEAD_DIM:].astype(jnp.float32)
            levels.append(tail[0:1] + tail[1:2] + tail[2:3])
        top = jnp.maximum(jnp.maximum(levels[0], levels[1]), jnp.maximum(levels[2], levels[3]))
        shares = [jnp.exp2(level - top) for level in levels]
        inverse = 1.0 / (shares[0] + shares[1] + shares[2] + shares[3])
        mixed = sum(
            part[slot, :HEAD_DIM].astype(jnp.float32) * (share * inverse)
            for part, share in zip(parts, shares)
        )
        row_half = half if slot == 0 else 1 - half
        for sub in range(2):
            for piece in range(4):
                at = sub * BLOCK + piece * 128
                out_ref[piece, row_half, :, sub * 128 : (sub + 1) * 128] = (
                    mixed[:, at : at + 128].T.astype(jnp.bfloat16)
                )


def ring(value, axis, steps):
    size = lax.axis_size(axis)
    return lax.ppermute(value, axis, [(at, (at + steps) % size) for at in range(size)])


def routed(value, target):
    pairs = []
    for half in range(2):
        for y in range(4):
            to_half, to_y = target(half, y)
            pairs.append((4 * half + y, 4 * to_half + to_y))
    return lax.ppermute(value, ("xl", "y"), pairs)


def on_device(query_rows, key_rows, value_rows):
    half, y, z = lax.axis_index("xl"), lax.axis_index("y"), lax.axis_index("z")
    place = jnp.stack([half, y, z]).astype(jnp.int32)
    message = jax.ShapeDtypeStruct((ROWS, 128), jnp.bfloat16)
    kv_own, kv_other = pl.pallas_call(
        pack_keys_kernel,
        grid=(1,),
        out_shape=(message,) * 2,
        in_specs=[smem(), whole((BLOCK, 256)), whole((BLOCK, 256))],
        out_specs=tuple(vmem(2)),
        compiler_params=PARAMS,
        name="pack_keys",
    )(place, key_rows, value_rows)
    q_own, q_other = pl.pallas_call(
        pack_queries_kernel,
        grid=(1,),
        out_shape=(message,) * 2,
        in_specs=[smem(), whole((BLOCK, 512)), pl.BlockSpec(memory_space=pl.ANY)],
        out_specs=tuple(vmem(2)),
        compiler_params=PARAMS,
        name="pack_queries",
    )(place, query_rows, kv_own)
    kv_mirror = routed(kv_other, lambda h, r: (1 - h, 3 - r))
    q_swap = ring(q_other, "xl", 1)
    blocks = [kv_own] + [ring(kv_own, "z", k) for k in (1, 2, 3)]
    blocks += [kv_mirror] + [ring(kv_mirror, "z", k) for k in (1, 2, 3)]
    blocks = jnp.stack(blocks)
    queries = [jnp.stack([q_own, q_swap])]
    queries += [jnp.stack([ring(q_own, "y", k), ring(q_swap, "y", k)]) for k in (1, 2, 3)]
    parts = [ring(attend(k, place, queries[k], blocks), "y", 4 - k) for k in (1, 3, 2)]
    parts.append(attend(0, place, queries[0], blocks))
    merged = pl.pallas_call(
        merge_kernel,
        out_shape=jax.ShapeDtypeStruct((4, 2, 128, 256), jnp.bfloat16),
        in_specs=[smem()] + vmem(4),
        out_specs=vmem(1)[0],
        compiler_params=PARAMS,
        name="merge",
    )(place, *parts)
    merged = merged.reshape(8, 128, 256)
    spread = lax.all_to_all(merged, ("xh", "core", "xl"), split_axis=0, concat_axis=0, tiled=True)
    return spread.transpose(1, 0, 2).reshape(128, 2048)


def solution(mesh):
    fine = Mesh(mesh.devices.reshape(2, 4, 4, 2, 2), ("xl", "y", "z", "xh", "core"))
    tokens, heads = ("xl", "y", "z"), ("xh", "core")
    return jax.shard_map(
        on_device,
        mesh=fine,
        in_specs=(P(tokens, heads),) * 3,
        out_specs=P(tokens + heads, None),
        check_vma=False,
    )
```

profile of v0, /device:TPU:1, one launch (start us, length us, event | category | flops | bytes accessed | tf_op | source)
XLA Modules:
  0.0 99.7 jit_solution(6059982982278194528)
XLA Ops:
  0.0 0.1 pad_add_fusion.place
  0.1 0.9 copy-done.1
  1.0 0.9 copy-done.2
  2.0 0.7 pack_keys.1
  2.7 2.5 %collective-permute-start.3 = (bf16[1024,128]{1,0:T(8,128)(2,1)S(1)}, bf16[1024,128]{1,0:T(8,128)(2,1)S(1)}, u32[]{:S(2)}, u32[]{:S(2)}) collective-permute-start(bf16[1024,128]{1,0:T(8,128)(2,1)S(1)} %get-tuple-element.9.after), channel_id=1, source_target_pairs={{0,4},{4,8},{8,12},{12,0},{1,5},{5,9},{9,13},{13,1},{2,6},{6,10},{... | collective-permute-start | bytes 786440 | tf_op jit(solution)/shard_map/ppermute | solution.py:236
  5.2 3.3 %collective-permute-start.4 = (bf16[1024,128]{1,0:T(8,128)(2,1)S(1)}, bf16[1024,128]{1,0:T(8,128)(2,1)S(1)}, u32[]{:S(2)}, u32[]{:S(2)}) collective-permute-start(bf16[1024,128]{1,0:T(8,128)(2,1)S(1)} %get-tuple-element.9.after), channel_id=1, source_target_pairs={{0,8},{4,12},{8,0},{12,4},{1,9},{5,13},{9,1},{13,5},{2,10},{6,14},... | collective-permute-start | bytes 786440 | tf_op jit(solution)/shard_map/ppermute | solution.py:236
  8.5 0.7 collective-permute-start.5
  9.3 3.7 %collective-permute-start.6 = (bf16[1024,128]{1,0:T(8,128)(2,1)S(1)}, bf16[1024,128]{1,0:T(8,128)(2,1)S(1)}, u32[]{:S(2)}, u32[]{:S(2)}) collective-permute-start(bf16[1024,128]{1,0:T(8,128)(2,1)S(1)} %get-tuple-element.12), channel_id=1, source_target_pairs={{0,112},{16,96},{32,80},{48,64},{64,48},{80,32},{96,16},{112,0},{1... | collective-permute-start | bytes 786440 | tf_op jit(solution)/shard_map/ppermute | solution.py:245
  12.9 1.0 %copy-done = bf16[512,512]{1,0:T(8,128)(2,1)S(1)} copy-done((bf16[512,512]{1,0:T(8,128)(2,1)S(1)}, bf16[512,512]{1,0:T(8,128)(2,1)}, u32[]{:S(2)}) %copy-start) | copy-done | bytes 524312
  14.0 0.6 pack_queries.1
  14.6 0.4 collective-permute-start.14
  15.1 2.0 %collective-permute-start.11 = (bf16[1024,128]{1,0:T(8,128)(2,1)S(1)}, bf16[1024,128]{1,0:T(8,128)(2,1)S(1)}, u32[]{:S(2)}, u32[]{:S(2)}) collective-permute-start(bf16[1024,128]{1,0:T(8,128)(2,1)S(1)} %get-tuple-element.10), channel_id=1, source_target_pairs={{0,48},{16,0},{32,16},{48,32},{1,49},{17,1},{33,17},{49,33},{2,50}... | collective-permute-start | bytes 786440 | tf_op jit(solution)/shard_map/ppermute | solution.py:236
  17.1 2.8 %collective-permute-done.4 = bf16[1024,128]{1,0:T(8,128)(2,1)S(1)} collective-permute-done((bf16[1024,128]{1,0:T(8,128)(2,1)S(1)}, bf16[1024,128]{1,0:T(8,128)(2,1)S(1)}, u32[]{:S(2)}, u32[]{:S(2)}) %collective-permute-start.4) | collective-permute-done | bytes 262176 | tf_op jit(solution)/shard_map/ppermute | solution.py:236
  19.9 1.2 %collective-permute-start.1 = (bf16[1024,128]{1,0:T(8,128)(2,1)S(1)}, bf16[1024,128]{1,0:T(8,128)(2,1)S(1)}, u32[]{:S(2)}, u32[]{:S(2)}) collective-permute-start(bf16[1024,128]{1,0:T(8,128)(2,1)S(1)} %get-tuple-element.11), channel_id=1, source_target_pairs={{0,64},{64,0},{1,65},{65,1},{2,66},{66,2},{3,67},{67,3},{4,68},{68... | collective-permute-start | bytes 786440 | tf_op jit(solution)/shard_map/ppermute | solution.py:236
  21.1 0.4 collective-permute-start.8
  21.6 14.0 %collective-permute-done.7 = bf16[1024,128]{1,0:T(8,128)(2,1)S(1)} collective-permute-done((bf16[1024,128]{1,0:T(8,128)(2,1)S(1)}, bf16[1024,128]{1,0:T(8,128)(2,1)S(1)}, u32[]{:S(2)}, u32[]{:S(2)}) %collective-permute-start.7) | collective-permute-done | bytes 262176 | tf_op jit(solution)/shard_map/ppermute | solution.py:236
  35.7 0.6 collective-permute-start
  36.3 2.7 %collective-permute-start.15 = (bf16[1024,128]{1,0:T(8,128)(2,1)S(1)}, bf16[1024,128]{1,0:T(8,128)(2,1)S(1)}, u32[]{:S(2)}, u32[]{:S(2)}) collective-permute-start(bf16[1024,128]{1,0:T(8,128)(2,1)S(1)} %collective-permute-done.1), channel_id=1, source_target_pairs={{0,32},{16,48},{32,0},{48,16},{1,33},{17,49},{33,1},{49,17},{2,34}... | collective-permute-start | bytes 786440 | tf_op jit(solution)/shard_map/ppermute | solution.py:236
  39.1 1.0 %collective-permute-start.12 = (bf16[1024,128]{1,0:T(8,128)(2,1)S(1)}, bf16[1024,128]{1,0:T(8,128)(2,1)S(1)}, u32[]{:S(2)}, u32[]{:S(2)}) collective-permute-start(bf16[1024,128]{1,0:T(8,128)(2,1)S(1)} %collective-permute-done.1), channel_id=1, source_target_pairs={{0,48},{16,0},{32,16},{48,32},{1,49},{17,1},{33,17},{49,33},{2,50}... | collective-permute-start | bytes 786440 | tf_op jit(solution)/shard_map/ppermute | solution.py:236
  40.1 2.4 %collective-permute-done.9 = bf16[1024,128]{1,0:T(8,128)(2,1)S(1)} collective-permute-done((bf16[1024,128]{1,0:T(8,128)(2,1)S(1)}, bf16[1024,128]{1,0:T(8,128)(2,1)S(1)}, u32[]{:S(2)}, u32[]{:S(2)}) %collective-permute-start.9) | collective-permute-done | bytes 262176 | tf_op jit(solution)/shard_map/ppermute | solution.py:236
  42.5 6.8 %collective-permute-done.15 = bf16[1024,128]{1,0:T(8,128)(2,1)S(1)} collective-permute-done((bf16[1024,128]{1,0:T(8,128)(2,1)S(1)}, bf16[1024,128]{1,0:T(8,128)(2,1)S(1)}, u32[]{:S(2)}, u32[]{:S(2)}) %collective-permute-start.15) | collective-permute-done | bytes 262176 | tf_op jit(solution)/shard_map/ppermute | solution.py:236
  49.4 5.4 %attend2.1 = bf16[2,144,1024]{2,1,0:T(8,128)(2,1)S(1)} custom-call(s32[3]{0:T(128)S(1)} %pad_add_fusion.place, bf16[2,1024,128]{2,1,0:T(8,128)(2,1)S(1)} %pad_maximum_fusion.2.q_ref, bf16[8,1024,128]{2,1,0:T(8,128)(2,1)S(1)} %bitcast_dynamic-update-slice_fusion.kv_ref), custom_call_target="tpu_custom_call" | custom-call | tf_op jit(solution)/shard_map/attend2/pallas_call | solution.py:193
  54.8 0.1 collective-permute-start.16
  54.9 5.8 %attend3.1 = bf16[2,144,1024]{2,1,0:T(8,128)(2,1)S(1)} custom-call(s32[3]{0:T(128)S(1)} %pad_add_fusion.place, bf16[2,1024,128]{2,1,0:T(8,128)(2,1)S(1)} %pad_maximum_fusion.1.q_ref, bf16[8,1024,128]{2,1,0:T(8,128)(2,1)S(1)} %bitcast_dynamic-update-slice_fusion.kv_ref), custom_call_target="tpu_custom_call" | custom-call | tf_op jit(solution)/shard_map/attend3/pallas_call | solution.py:193
  60.7 0.1 collective-permute-start.13
  60.8 6.8 %attend1.1 = bf16[2,144,1024]{2,1,0:T(8,128)(2,1)S(1)} custom-call(s32[3]{0:T(128)S(1)} %pad_add_fusion.place, bf16[2,1024,128]{2,1,0:T(8,128)(2,1)S(1)} %pad_maximum_fusion.q_ref, bf16[8,1024,128]{2,1,0:T(8,128)(2,1)S(1)} %bitcast_dynamic-update-slice_fusion.kv_ref), custom_call_target="tpu_custom_call" | custom-call | tf_op jit(solution)/shard_map/attend1/pallas_call | solution.py:193
  67.7 1.2 %collective-permute-start.10 = (bf16[2,144,1024]{2,1,0:T(8,128)(2,1)S(1)}, bf16[2,144,1024]{2,1,0:T(8,128)(2,1)S(1)}, u32[]{:S(2)}, u32[]{:S(2)}) collective-permute-start(bf16[2,144,1024]{2,1,0:T(8,128)(2,1)S(1)} %attend1.1), channel_id=1, source_target_pairs={{0,48},{16,0},{32,16},{48,32},{1,49},{17,1},{33,17},{49,33},{2,50}... | collective-permute-start | bytes 1769480 | tf_op jit(solution)/shard_map/ppermute | solution.py:236
  69.0 5.1 %attend0.1.refs_3_ = bf16[2,144,1024]{2,1,0:T(8,128)(2,1)S(1)} custom-call(s32[3]{0:T(128)S(1)} %pad_add_fusion.place, bf16[2,1024,128]{2,1,0:T(8,128)(2,1)S(1)} %pad_maximum_fusion.3.q_ref, bf16[8,1024,128]{2,1,0:T(8,128)(2,1)S(1)} %bitcast_dynamic-update-slice_fusion.kv_ref), custom_call_target="tpu_custom_call" | custom-call | tf_op jit(solution)/shard_map/attend0/pallas_call | solution.py:193
  74.1 8.8 %collective-permute-done.13.refs_1_ = bf16[2,144,1024]{2,1,0:T(8,128)(2,1)S(1)} collective-permute-done((bf16[2,144,1024]{2,1,0:T(8,128)(2,1)S(1)}, bf16[2,144,1024]{2,1,0:T(8,128)(2,1)S(1)}, u32[]{:S(2)}, u32[]{:S(2)}) %collective-permute-start.13) | collective-permute-done | bytes 589856 | tf_op jit(solution)/shard_map/ppermute | solution.py:236
  82.9 1.1 %merge.1 = bf16[4,2,128,256]{3,2,1,0:T(8,128)(2,1)S(1)} custom-call(s32[3]{0:T(128)S(1)} %pad_add_fusion.place, bf16[2,144,1024]{2,1,0:T(8,128)(2,1)S(1)} %collective-permute-done.10.refs_0_, bf16[2,144,1024]{2,1,0:T(8,128)(2,1)S(1)} %collective-permute-done.13.refs_1_, bf16[2,144,1024]{2,1,0:T(8,128)(2,1)S(1)} %collective-permute-done.16.refs_2_, ...), custom_call_target="tpu_custom_call" | custom-call | tf_op jit(solution)/shard_map/merge/pallas_call | solution.py:279
  84.0 14.9 %all_to_all.5 = bf16[8,128,256]{2,1,0:T(8,128)(2,1)S(1)} all-to-all(bf16[8,128,256]{2,1,0:T(8,128)(2,1)S(1)} %bitcast.31), channel_id=1, replica_groups=mesh['xl'=2,'y'=4,'z'=4,'xh'=2,'core'=2] {'xh','core','xl'}, dimensions={0} | all-to-all | bytes 1048576 | tf_op jit(solution)/shard_map/all_to_all | solution.py:288
  98.9 0.8 copy.5
  (30 shorter events, 0.5 us)
Async XLA Ops:
  0.1 1.0 copy-start.1
  1.0 0.9 copy-start.2
  2.7 12.4 %collective-permute-start.3 = (bf16[1024,128]{1,0:T(8,128)(2,1)S(1)}, bf16[1024,128]{1,0:T(8,128)(2,1)S(1)}, u32[]{:S(2)}, u32[]{:S(2)}) collective-permute-start(bf16[1024,128]{1,0:T(8,128)(2,1)S(1)} %get-tuple-element.9.after), channel_id=1, source_target_pairs={{0,4},{4,8},{8,12},{12,0},{1,5},{5,9},{9,13},{13,1},{2,6},{6,10},{... | collective-permute-start | bytes 786440 | tf_op jit(solution)/shard_map/ppermute | solution.py:236
  5.2 14.6 %collective-permute-start.4 = (bf16[1024,128]{1,0:T(8,128)(2,1)S(1)}, bf16[1024,128]{1,0:T(8,128)(2,1)S(1)}, u32[]{:S(2)}, u32[]{:S(2)}) collective-permute-start(bf16[1024,128]{1,0:T(8,128)(2,1)S(1)} %get-tuple-element.9.after), channel_id=1, source_target_pairs={{0,8},{4,12},{8,0},{12,4},{1,9},{5,13},{9,1},{13,5},{2,10},{6,14},... | collective-permute-start | bytes 786440 | tf_op jit(solution)/shard_map/ppermute | solution.py:236
  8.5 12.6 %collective-permute-start.5 = (bf16[1024,128]{1,0:T(8,128)(2,1)S(1)}, bf16[1024,128]{1,0:T(8,128)(2,1)S(1)}, u32[]{:S(2)}, u32[]{:S(2)}) collective-permute-start(bf16[1024,128]{1,0:T(8,128)(2,1)S(1)} %get-tuple-element.9.after), channel_id=1, source_target_pairs={{0,12},{4,0},{8,4},{12,8},{1,13},{5,1},{9,5},{13,9},{2,14},{6,2},{... | collective-permute-start | bytes 786440 | tf_op jit(solution)/shard_map/ppermute | solution.py:236
  9.3 11.8 %collective-permute-start.6 = (bf16[1024,128]{1,0:T(8,128)(2,1)S(1)}, bf16[1024,128]{1,0:T(8,128)(2,1)S(1)}, u32[]{:S(2)}, u32[]{:S(2)}) collective-permute-start(bf16[1024,128]{1,0:T(8,128)(2,1)S(1)} %get-tuple-element.12), channel_id=1, source_target_pairs={{0,112},{16,96},{32,80},{48,64},{64,48},{80,32},{96,16},{112,0},{1... | collective-permute-start | bytes 786440 | tf_op jit(solution)/shard_map/ppermute | solution.py:245
  12.9 1.0 %copy-start = (bf16[512,512]{1,0:T(8,128)(2,1)S(1)}, bf16[512,512]{1,0:T(8,128)(2,1)}, u32[]{:S(2)}) copy-start(bf16[512,512]{1,0:T(8,128)(2,1)} %query_ref.1) | copy-start | bytes 1572868
  14.6 24.4 %collective-permute-start.14 = (bf16[1024,128]{1,0:T(8,128)(2,1)S(1)}, bf16[1024,128]{1,0:T(8,128)(2,1)S(1)}, u32[]{:S(2)}, u32[]{:S(2)}) collective-permute-start(bf16[1024,128]{1,0:T(8,128)(2,1)S(1)} %get-tuple-element.10), channel_id=1, source_target_pairs={{0,32},{16,48},{32,0},{48,16},{1,33},{17,49},{33,1},{49,17},{2,34}... | collective-permute-start | bytes 786440 | tf_op jit(solution)/shard_map/ppermute | solution.py:236
  15.1 39.8 %collective-permute-start.11 = (bf16[1024,128]{1,0:T(8,128)(2,1)S(1)}, bf16[1024,128]{1,0:T(8,128)(2,1)S(1)}, u32[]{:S(2)}, u32[]{:S(2)}) collective-permute-start(bf16[1024,128]{1,0:T(8,128)(2,1)S(1)} %get-tuple-element.10), channel_id=1, source_target_pairs={{0,48},{16,0},{32,16},{48,32},{1,49},{17,1},{33,17},{49,33},{2,50}... | collective-permute-start | bytes 786440 | tf_op jit(solution)/shard_map/ppermute | solution.py:236
  19.9 15.8 %collective-permute-start.1 = (bf16[1024,128]{1,0:T(8,128)(2,1)S(1)}, bf16[1024,128]{1,0:T(8,128)(2,1)S(1)}, u32[]{:S(2)}, u32[]{:S(2)}) collective-permute-start(bf16[1024,128]{1,0:T(8,128)(2,1)S(1)} %get-tuple-element.11), channel_id=1, source_target_pairs={{0,64},{64,0},{1,65},{65,1},{2,66},{66,2},{3,67},{67,3},{4,68},{68... | collective-permute-start | bytes 786440 | tf_op jit(solution)/shard_map/ppermute | solution.py:236
  21.1 14.6 %collective-permute-start.7 = (bf16[1024,128]{1,0:T(8,128)(2,1)S(1)}, bf16[1024,128]{1,0:T(8,128)(2,1)S(1)}, u32[]{:S(2)}, u32[]{:S(2)}) collective-permute-start(bf16[1024,128]{1,0:T(8,128)(2,1)S(1)} %collective-permute-done.6), channel_id=1, source_target_pairs={{0,4},{4,8},{8,12},{12,0},{1,5},{5,9},{9,13},{13,1},{2,6},{6,10},{... | collective-permute-start | bytes 786440 | tf_op jit(solution)/shard_map/ppermute | solution.py:236
  21.1 15.1 %collective-permute-start.8 = (bf16[1024,128]{1,0:T(8,128)(2,1)S(1)}, bf16[1024,128]{1,0:T(8,128)(2,1)S(1)}, u32[]{:S(2)}, u32[]{:S(2)}) collective-permute-start(bf16[1024,128]{1,0:T(8,128)(2,1)S(1)} %collective-permute-done.6), channel_id=1, source_target_pairs={{0,8},{4,12},{8,0},{12,4},{1,9},{5,13},{9,1},{13,5},{2,10},{6,14},... | collective-permute-start | bytes 786440 | tf_op jit(solution)/shard_map/ppermute | solution.py:236
  35.6 6.8 %collective-permute-start.9 = (bf16[1024,128]{1,0:T(8,128)(2,1)S(1)}, bf16[1024,128]{1,0:T(8,128)(2,1)S(1)}, u32[]{:S(2)}, u32[]{:S(2)}) collective-permute-start(bf16[1024,128]{1,0:T(8,128)(2,1)S(1)} %collective-permute-done.6), channel_id=1, source_target_pairs={{0,12},{4,0},{8,4},{12,8},{1,13},{5,1},{9,5},{13,9},{2,14},{6,2},{... | collective-permute-start | bytes 786440 | tf_op jit(solution)/shard_map/ppermute | solution.py:236
  35.7 25.1 %collective-permute-start = (bf16[1024,128]{1,0:T(8,128)(2,1)S(1)}, bf16[1024,128]{1,0:T(8,128)(2,1)S(1)}, u32[]{:S(2)}, u32[]{:S(2)}) collective-permute-start(bf16[1024,128]{1,0:T(8,128)(2,1)S(1)} %get-tuple-element.10), channel_id=1, source_target_pairs={{0,16},{16,32},{32,48},{48,0},{1,17},{17,33},{33,49},{49,1},{2,18}... | collective-permute-start | bytes 786440 | tf_op jit(solution)/shard_map/ppermute | solution.py:236
  36.3 13.1 %collective-permute-start.15 = (bf16[1024,128]{1,0:T(8,128)(2,1)S(1)}, bf16[1024,128]{1,0:T(8,128)(2,1)S(1)}, u32[]{:S(2)}, u32[]{:S(2)}) collective-permute-start(bf16[1024,128]{1,0:T(8,128)(2,1)S(1)} %collective-permute-done.1), channel_id=1, source_target_pairs={{0,32},{16,48},{32,0},{48,16},{1,33},{17,49},{33,1},{49,17},{2,34}... | collective-permute-start | bytes 786440 | tf_op jit(solution)/shard_map/ppermute | solution.py:236
  39.1 15.8 %collective-permute-start.12 = (bf16[1024,128]{1,0:T(8,128)(2,1)S(1)}, bf16[1024,128]{1,0:T(8,128)(2,1)S(1)}, u32[]{:S(2)}, u32[]{:S(2)}) collective-permute-start(bf16[1024,128]{1,0:T(8,128)(2,1)S(1)} %collective-permute-done.1), channel_id=1, source_target_pairs={{0,48},{16,0},{32,16},{48,32},{1,49},{17,1},{33,17},{49,33},{2,50}... | collective-permute-start | bytes 786440 | tf_op jit(solution)/shard_map/ppermute | solution.py:236
  42.5 18.3 %collective-permute-start.2 = (bf16[1024,128]{1,0:T(8,128)(2,1)S(1)}, bf16[1024,128]{1,0:T(8,128)(2,1)S(1)}, u32[]{:S(2)}, u32[]{:S(2)}) collective-permute-start(bf16[1024,128]{1,0:T(8,128)(2,1)S(1)} %collective-permute-done.1), channel_id=1, source_target_pairs={{0,16},{16,32},{32,48},{48,0},{1,17},{17,33},{33,49},{49,1},{2,18}... | collective-permute-start | bytes 786440 | tf_op jit(solution)/shard_map/ppermute | solution.py:236
  54.8 19.3 %collective-permute-start.16 = (bf16[2,144,1024]{2,1,0:T(8,128)(2,1)S(1)}, bf16[2,144,1024]{2,1,0:T(8,128)(2,1)S(1)}, u32[]{:S(2)}, u32[]{:S(2)}) collective-permute-start(bf16[2,144,1024]{2,1,0:T(8,128)(2,1)S(1)} %attend2.1), channel_id=1, source_target_pairs={{0,32},{16,48},{32,0},{48,16},{1,33},{17,49},{33,1},{49,17},{2,34}... | collective-permute-start | bytes 1769480 | tf_op jit(solution)/shard_map/ppermute | solution.py:236
  60.7 22.2 %collective-permute-start.13 = (bf16[2,144,1024]{2,1,0:T(8,128)(2,1)S(1)}, bf16[2,144,1024]{2,1,0:T(8,128)(2,1)S(1)}, u32[]{:S(2)}, u32[]{:S(2)}) collective-permute-start(bf16[2,144,1024]{2,1,0:T(8,128)(2,1)S(1)} %attend3.1), channel_id=1, source_target_pairs={{0,16},{16,32},{32,48},{48,0},{1,17},{17,33},{33,49},{49,1},{2,18}... | collective-permute-start | bytes 1769480 | tf_op jit(solution)/shard_map/ppermute | solution.py:236
  67.7 15.2 %collective-permute-start.10 = (bf16[2,144,1024]{2,1,0:T(8,128)(2,1)S(1)}, bf16[2,144,1024]{2,1,0:T(8,128)(2,1)S(1)}, u32[]{:S(2)}, u32[]{:S(2)}) collective-permute-start(bf16[2,144,1024]{2,1,0:T(8,128)(2,1)S(1)} %attend1.1), channel_id=1, source_target_pairs={{0,48},{16,0},{32,16},{48,32},{1,49},{17,1},{33,17},{49,33},{2,50}... | collective-permute-start | bytes 1769480 | tf_op jit(solution)/shard_map/ppermute | solution.py:236
where the time goes:
time: 100 us; the launch traced here: 99.7 us
  waiting for transfers between devices  34.8 us (35%)
  Pallas kernels  25.5 us (26%)
  starting transfers between devices  20 us (20%)
  blocking collectives  14.9 us (15%)
  local copies, waits for them, and re-layouts  4.05 us (4%)
    ppermute x16, waiting for transfers between devices, ring(): lax.ppermute(value, axis, [(at, (at + steps) % size) for at in range(size)])  34.8 us
    pallas_call x4, Pallas kernels, attend(): pl.pallas_call(functools.partial(attend_kernel, step), out_shape=jax.Shap...  23.1 us
    ppermute x16, starting transfers between devices, ring(): lax.ppermute(value, axis, [(at, (at + steps) % size) for at in range(size)])  16.3 us
    all_to_all x1, blocking collectives, on_device(): lax.all_to_all(merged, ('xh', 'core', 'xl'), split_axis=0, concat_axis=0,...  14.9 us
    ppermute x1, starting transfers between devices, routed(): return lax.ppermute(value, ('xl', 'y'), pairs)  3.66 us
    unnamed x13, local copies, waits for them, and re-layouts  3.17 us
  transfers between devices with their start and end apart: 17, of which 5 were waited for; matrix products, arithmetic and copies ran while one was open for 0% of the time, Pallas kernels for 24%

commit v1 on v0

--- a/solution.py
+++ b/solution.py
@@ -29,8 +29,14 @@
     return pl.BlockSpec(memory_space=pltpu.SMEM)
 
 
-def pack_keys_kernel(place, key_ref, value_ref, kv_own, kv_other):
+def pack_keys_kernel(place, key_in, value_in, kv_own, kv_other, key_ref, value_ref, done):
     half = place[0]
+    keys = pltpu.make_async_copy(key_in, key_ref, done.at[0])
+    values = pltpu.make_async_copy(value_in, value_ref, done.at[1])
+    keys.start()
+    values.start()
+    keys.wait()
+    values.wait()
     for head, kv_out in ((1 - half, kv_other), (half, kv_own)):
         at = pl.multiple_of(head * 128, 128)
         kv_out[:BLOCK] = key_ref[:, pl.ds(at, 128)]
@@ -41,16 +47,15 @@
             )
 
 
-def pack_queries_kernel(place, query_ref, after, q_own, q_other):
+def pack_queries_kernel(place, query_in, after, q_own, q_other, query_ref, done):
     half = place[0]
+    queries = pltpu.make_async_copy(query_in, query_ref, done)
+    queries.start()
+    queries.wait()
     for head, q_out in ((1 - half, q_other), (half, q_own)):
         for part in range(2):
             at = pl.multiple_of(head * 256 + part * 128, 128)
             q_out[part * BLOCK : (part + 1) * BLOCK] = query_ref[:, pl.ds(at, 128)]
-
-
-def whole(shape):
-    return pl.BlockSpec(shape, lambda _: (0,) * len(shape))
 
 
 def attend_kernel(step, place, q_ref, kv_ref, out_ref, best, acc, held, peak, todo):
@@ -251,29 +256,41 @@
     message = jax.ShapeDtypeStruct((ROWS, 128), jnp.bfloat16)
     kv_own, kv_other = pl.pallas_call(
         pack_keys_kernel,
-        grid=(1,),
         out_shape=(message,) * 2,
-        in_specs=[smem(), whole((BLOCK, 256)), whole((BLOCK, 256))],
+        in_specs=[smem()] + [pl.BlockSpec(memory_space=pltpu.HBM), pl.BlockSpec(memory_space=pltpu.HBM)],
         out_specs=tuple(vmem(2)),
+        scratch_shapes=[
+            pltpu.VMEM((BLOCK, 256), jnp.bfloat16),
+            pltpu.VMEM((BLOCK, 256), jnp.bfloat16),
+            pltpu.SemaphoreType.DMA((2,)),
+        ],
         compiler_params=PARAMS,
         name="pack_keys",
     )(place, key_rows, value_rows)
     q_own, q_other = pl.pallas_call(
         pack_queries_kernel,
-        grid=(1,),
         out_shape=(message,) * 2,
-        in_specs=[smem(), whole((BLOCK, 512)), pl.BlockSpec(memory_space=pl.ANY)],
+        in_specs=[smem()] + [pl.BlockSpec(memory_space=pltpu.HBM), pl.BlockSpec(memory_space=pl.ANY)],
         out_specs=tuple(vmem(2)),
+        scratch_shapes=[pltpu.VMEM((BLOCK, 512), jnp.bfloat16), pltpu.SemaphoreType.DMA],
         compiler_params=PARAMS,
         name="pack_queries",
     )(place, query_rows, kv_own)
     kv_mirror = routed(kv_other, lambda h, r: (1 - h, 3 - r))
     q_swap = ring(q_other, "xl", 1)
-    blocks = [kv_own] + [ring(kv_own, "z", k) for k in (1, 2, 3)]
-    blocks += [kv_mirror] + [ring(kv_mirror, "z", k) for k in (1, 2, 3)]
-    blocks = jnp.stack(blocks)
-    queries = [jnp.stack([q_own, q_swap])]
-    queries += [jnp.stack([ring(q_own, "y", k), ring(q_swap, "y", k)]) for k in (1, 2, 3)]
+    kv_own, _ = lax.optimization_barrier((kv_own, q_other))
+    own_near = [ring(kv_own, "z", k) for k in (1, 3)]
+    mirror_near = [ring(kv_mirror, "z", k) for k in (1, 3)]
+    kv_far = ring(jnp.stack([kv_own, kv_mirror]), "z", 2)
+    blocks = jnp.stack(
+        [kv_own, own_near[0], kv_far[0], own_near[1]]
+        + [kv_mirror, mirror_near[0], kv_far[1], mirror_near[1]]
+    )
+    q_pair = jnp.stack([q_own, q_swap])
+    queries = {k: ring(q_pair, "y", k) for k in (1, 3)}
+    q_late, _ = lax.optimization_barrier((q_pair, mirror_near[1]))
+    queries[2] = ring(q_late, "y", 2)
+    queries[0] = q_pair
     parts = [ring(attend(k, place, queries[k], blocks), "y", 4 - k) for k in (1, 3, 2)]
     parts.append(attend(0, place, queries[0], blocks))
     merged = pl.pallas_call(

time: 100 us -> 102 us (1.020)
  the two profiles are of different devices: /device:TPU:1 before, /device:TPU:120 now
where the time goes in v1:
time: 102 us; the launch traced here: 101 us
  waiting for transfers between devices  35 us (34%)
  Pallas kernels  28.3 us (28%)
  starting transfers between devices  18.9 us (19%)
  blocking collectives  14.8 us (15%)
  local copies, waits for them, and re-layouts  4.06 us (4%)
    ppermute x12, waiting for transfers between devices, ring(): lax.ppermute(value, axis, [(at, (at + steps) % size) for at in range(size)])  29.3 us
    pallas_call x4, Pallas kernels, attend(): pl.pallas_call(functools.partial(attend_kernel, step), out_shape=jax.Shap...  25.7 us
    ppermute x12, starting transfers between devices, ring(): lax.ppermute(value, axis, [(at, (at + steps) % size) for at in range(size)])  17.6 us
    all_to_all x1, blocking collectives, on_device(): lax.all_to_all(merged, ('xh', 'core', 'xl'), split_axis=0, concat_axis=0,...  14.8 us
    ppermute x1, waiting for transfers between devices, routed(): return lax.ppermute(value, ('xl', 'y'), pairs)  5.72 us
    unnamed x13, local copies, waits for them, and re-layouts  3.18 us
  transfers between devices with their start and end apart: 13, of which 5 were waited for; matrix products, arithmetic and copies ran while one was open for 0% of the time, Pallas kernels for 26%

profile of v1, /device:TPU:120, one launch (start us, length us, event | category | flops | bytes accessed | tf_op | source)
XLA Modules:
  0.0 101.3 jit_solution(4624998182758618233)
XLA Ops:
  0.0 0.1 pad_add_fusion.place
  0.1 0.9 copy-done.1
  1.0 0.9 copy-done.2
  2.0 0.8 pack_keys.1
  2.8 1.2 %collective-permute-start.3 = (bf16[1024,128]{1,0:T(8,128)(2,1)S(1)}, bf16[1024,128]{1,0:T(8,128)(2,1)S(1)}, u32[]{:S(2)}, u32[]{:S(2)}) collective-permute-start(bf16[1024,128]{1,0:T(8,128)(2,1)S(1)} %get-tuple-element.15), channel_id=1, source_target_pairs={{0,112},{16,96},{32,80},{48,64},{64,48},{80,32},{96,16},{112,0},{1... | collective-permute-start | bytes 786440 | tf_op jit(solution)/shard_map/ppermute | solution.py:250
  4.0 1.0 %copy-done = bf16[512,512]{1,0:T(8,128)(2,1)S(1)} copy-done((bf16[512,512]{1,0:T(8,128)(2,1)S(1)}, bf16[512,512]{1,0:T(8,128)(2,1)}, u32[]{:S(2)}) %copy-start) | copy-done | bytes 524312
  5.0 0.7 pack_queries.1
  5.7 0.1 collective-permute-start.2
  5.8 2.0 %collective-permute-start.5 = (bf16[1024,128]{1,0:T(8,128)(2,1)S(1)}, bf16[1024,128]{1,0:T(8,128)(2,1)S(1)}, u32[]{:S(2)}, u32[]{:S(2)}) collective-permute-start(bf16[1024,128]{1,0:T(8,128)(2,1)S(1)} %get-tuple-element.14.after), channel_id=1, source_target_pairs={{0,12},{4,0},{8,4},{12,8},{1,13},{5,1},{9,5},{13,9},{2,14},{6,2},{... | collective-permute-start | bytes 786440 | tf_op jit(solution)/shard_map/ppermute | solution.py:241
  7.8 0.5 collective-permute-start
  8.3 5.7 %collective-permute-done.3 = bf16[1024,128]{1,0:T(8,128)(2,1)S(1)} collective-permute-done((bf16[1024,128]{1,0:T(8,128)(2,1)S(1)}, bf16[1024,128]{1,0:T(8,128)(2,1)S(1)}, u32[]{:S(2)}, u32[]{:S(2)}) %collective-permute-start.3) | collective-permute-done | bytes 262176 | tf_op jit(solution)/shard_map/ppermute | solution.py:250
  14.1 0.1 pad_maximum_fusion.1
  14.1 0.5 collective-permute-start.4
  14.6 0.1 collective-permute-start.7
  14.7 1.5 %collective-permute-done = bf16[1024,128]{1,0:T(8,128)(2,1)S(1)} collective-permute-done((bf16[1024,128]{1,0:T(8,128)(2,1)S(1)}, bf16[1024,128]{1,0:T(8,128)(2,1)S(1)}, u32[]{:S(2)}, u32[]{:S(2)}) %collective-permute-start) | collective-permute-done | bytes 262176 | tf_op jit(solution)/shard_map/ppermute | solution.py:241
  16.3 0.9 collective-permute-start.9
  17.3 2.4 %collective-permute-start.1 = (bf16[2,1024,128]{2,1,0:T(8,128)(2,1)S(1)}, bf16[2,1024,128]{2,1,0:T(8,128)(2,1)S(1)}, u32[]{:S(2)}, u32[]{:S(2)}) collective-permute-start(bf16[2,1024,128]{2,1,0:T(8,128)(2,1)S(1)} %pad_maximum_fusion.q_ref), channel_id=1, source_target_pairs={{0,16},{16,32},{32,48},{48,0},{1,17},{17,33},{33,49},{49,1},{2,18}... | collective-permute-start | bytes 1572872 | tf_op jit(solution)/shard_map/ppermute | solution.py:241
  19.6 13.4 %collective-permute-done.7 = bf16[1024,128]{1,0:T(8,128)(2,1)S(1)} collective-permute-done((bf16[1024,128]{1,0:T(8,128)(2,1)S(1)}, bf16[1024,128]{1,0:T(8,128)(2,1)S(1)}, u32[]{:S(2)}, u32[]{:S(2)}) %collective-permute-start.7) | collective-permute-done | bytes 262176 | tf_op jit(solution)/shard_map/ppermute | solution.py:241
  33.0 0.6 collective-permute-start.6
  33.6 0.6 collective-permute-start.11
  34.4 6.8 %collective-permute-done.6 = bf16[1024,128]{1,0:T(8,128)(2,1)S(1)} collective-permute-done((bf16[1024,128]{1,0:T(8,128)(2,1)S(1)}, bf16[1024,128]{1,0:T(8,128)(2,1)S(1)}, u32[]{:S(2)}, u32[]{:S(2)}) %collective-permute-start.6) | collective-permute-done | bytes 262176 | tf_op jit(solution)/shard_map/ppermute | solution.py:241
  41.4 6.1 %attend3.1 = bf16[2,144,1024]{2,1,0:T(8,128)(2,1)S(1)} custom-call(s32[3]{0:T(128)S(1)} %pad_add_fusion.place, bf16[2,1024,128]{2,1,0:T(8,128)(2,1)S(1)} %collective-permute-done.9.q_ref, bf16[8,1024,128]{2,1,0:T(8,128)(2,1)S(1)} %bitcast_dynamic-update-slice_fusion.kv_ref), custom_call_target="tpu_custom_call" | custom-call | tf_op jit(solution)/shard_map/attend3/pallas_call | solution.py:198
  47.5 0.1 collective-permute-start.10
  47.6 5.8 %attend1.1 = bf16[2,144,1024]{2,1,0:T(8,128)(2,1)S(1)} custom-call(s32[3]{0:T(128)S(1)} %pad_add_fusion.place, bf16[2,1024,128]{2,1,0:T(8,128)(2,1)S(1)} %collective-permute-done.1.q_ref, bf16[8,1024,128]{2,1,0:T(8,128)(2,1)S(1)} %bitcast_dynamic-update-slice_fusion.kv_ref), custom_call_target="tpu_custom_call" | custom-call | tf_op jit(solution)/shard_map/attend1/pallas_call | solution.py:198
  53.3 2.8 %collective-permute-start.8 = (bf16[2,144,1024]{2,1,0:T(8,128)(2,1)S(1)}, bf16[2,144,1024]{2,1,0:T(8,128)(2,1)S(1)}, u32[]{:S(2)}, u32[]{:S(2)}) collective-permute-start(bf16[2,144,1024]{2,1,0:T(8,128)(2,1)S(1)} %attend1.1), channel_id=1, source_target_pairs={{0,48},{16,0},{32,16},{48,32},{1,49},{17,1},{33,17},{49,33},{2,50}... | collective-permute-start | bytes 1769480 | tf_op jit(solution)/shard_map/ppermute | solution.py:241
  56.1 5.4 %attend2.1 = bf16[2,144,1024]{2,1,0:T(8,128)(2,1)S(1)} custom-call(s32[3]{0:T(128)S(1)} %pad_add_fusion.place, bf16[2,1024,128]{2,1,0:T(8,128)(2,1)S(1)} %collective-permute-done.11.q_ref, bf16[8,1024,128]{2,1,0:T(8,128)(2,1)S(1)} %bitcast_dynamic-update-slice_fusion.kv_ref), custom_call_target="tpu_custom_call" | custom-call | tf_op jit(solution)/shard_map/attend2/pallas_call | solution.py:198
  61.5 7.0 %collective-permute-start.12 = (bf16[2,144,1024]{2,1,0:T(8,128)(2,1)S(1)}, bf16[2,144,1024]{2,1,0:T(8,128)(2,1)S(1)}, u32[]{:S(2)}, u32[]{:S(2)}) collective-permute-start(bf16[2,144,1024]{2,1,0:T(8,128)(2,1)S(1)} %attend2.1), channel_id=1, source_target_pairs={{0,32},{16,48},{32,0},{48,16},{1,33},{17,49},{33,1},{49,17},{2,34}... | collective-permute-start | bytes 1769480 | tf_op jit(solution)/shard_map/ppermute | solution.py:241
  68.5 8.5 %attend0.1.refs_3_ = bf16[2,144,1024]{2,1,0:T(8,128)(2,1)S(1)} custom-call(s32[3]{0:T(128)S(1)} %pad_add_fusion.place, bf16[2,1024,128]{2,1,0:T(8,128)(2,1)S(1)} %pad_maximum_fusion.q_ref, bf16[8,1024,128]{2,1,0:T(8,128)(2,1)S(1)} %bitcast_dynamic-update-slice_fusion.kv_ref), custom_call_target="tpu_custom_call" | custom-call | tf_op jit(solution)/shard_map/attend0/pallas_call | solution.py:198
  77.0 7.5 %collective-permute-done.12.refs_2_ = bf16[2,144,1024]{2,1,0:T(8,128)(2,1)S(1)} collective-permute-done((bf16[2,144,1024]{2,1,0:T(8,128)(2,1)S(1)}, bf16[2,144,1024]{2,1,0:T(8,128)(2,1)S(1)}, u32[]{:S(2)}, u32[]{:S(2)}) %collective-permute-start.12) | collective-permute-done | bytes 589856 | tf_op jit(solution)/shard_map/ppermute | solution.py:241
  84.5 1.1 %merge.1 = bf16[4,2,128,256]{3,2,1,0:T(8,128)(2,1)S(1)} custom-call(s32[3]{0:T(128)S(1)} %pad_add_fusion.place, bf16[2,144,1024]{2,1,0:T(8,128)(2,1)S(1)} %collective-permute-done.8.refs_0_, bf16[2,144,1024]{2,1,0:T(8,128)(2,1)S(1)} %collective-permute-done.10.refs_1_, bf16[2,144,1024]{2,1,0:T(8,128)(2,1)S(1)} %collective-permute-done.12.refs_2_, ...), custom_call_target="tpu_custom_call" | custom-call | tf_op jit(solution)/shard_map/merge/pallas_call | solution.py:296
  85.7 14.8 %all_to_all.5 = bf16[8,128,256]{2,1,0:T(8,128)(2,1)S(1)} all-to-all(bf16[8,128,256]{2,1,0:T(8,128)(2,1)S(1)} %bitcast.22), channel_id=1, replica_groups=mesh['xl'=2,'y'=4,'z'=4,'xh'=2,'core'=2] {'xh','core','xl'}, dimensions={0} | all-to-all | bytes 1048576 | tf_op jit(solution)/shard_map/all_to_all | solution.py:305
  100.5 0.8 copy.5
  (20 shorter events, 0.3 us)
Async XLA Ops:
  0.1 1.0 copy-start.1
  1.0 0.9 copy-start.2
  2.8 11.3 %collective-permute-start.3 = (bf16[1024,128]{1,0:T(8,128)(2,1)S(1)}, bf16[1024,128]{1,0:T(8,128)(2,1)S(1)}, u32[]{:S(2)}, u32[]{:S(2)}) collective-permute-start(bf16[1024,128]{1,0:T(8,128)(2,1)S(1)} %get-tuple-element.15), channel_id=1, source_target_pairs={{0,112},{16,96},{32,80},{48,64},{64,48},{80,32},{96,16},{112,0},{1... | collective-permute-start | bytes 786440 | tf_op jit(solution)/shard_map/ppermute | solution.py:250
  4.0 1.0 %copy-start = (bf16[512,512]{1,0:T(8,128)(2,1)S(1)}, bf16[512,512]{1,0:T(8,128)(2,1)}, u32[]{:S(2)}) copy-start(bf16[512,512]{1,0:T(8,128)(2,1)} %query_in.1) | copy-start | bytes 1572868
  5.7 11.5 %collective-permute-start.2 = (bf16[1024,128]{1,0:T(8,128)(2,1)S(1)}, bf16[1024,128]{1,0:T(8,128)(2,1)S(1)}, u32[]{:S(2)}, u32[]{:S(2)}) collective-permute-start(bf16[1024,128]{1,0:T(8,128)(2,1)S(1)} %get-tuple-element.14.after), channel_id=1, source_target_pairs={{0,4},{4,8},{8,12},{12,0},{1,5},{5,9},{9,13},{13,1},{2,6},{6,10},{... | collective-permute-start | bytes 786440 | tf_op jit(solution)/shard_map/ppermute | solution.py:241
  5.8 28.5 %collective-permute-start.5 = (bf16[1024,128]{1,0:T(8,128)(2,1)S(1)}, bf16[1024,128]{1,0:T(8,128)(2,1)S(1)}, u32[]{:S(2)}, u32[]{:S(2)}) collective-permute-start(bf16[1024,128]{1,0:T(8,128)(2,1)S(1)} %get-tuple-element.14.after), channel_id=1, source_target_pairs={{0,12},{4,0},{8,4},{12,8},{1,13},{5,1},{9,5},{13,9},{2,14},{6,2},{... | collective-permute-start | bytes 786440 | tf_op jit(solution)/shard_map/ppermute | solution.py:241
  7.8 8.4 %collective-permute-start = (bf16[1024,128]{1,0:T(8,128)(2,1)S(1)}, bf16[1024,128]{1,0:T(8,128)(2,1)S(1)}, u32[]{:S(2)}, u32[]{:S(2)}) collective-permute-start(bf16[1024,128]{1,0:T(8,128)(2,1)S(1)} %get-tuple-element.13), channel_id=1, source_target_pairs={{0,64},{64,0},{1,65},{65,1},{2,66},{66,2},{3,67},{67,3},{4,68},{68... | collective-permute-start | bytes 786440 | tf_op jit(solution)/shard_map/ppermute | solution.py:241
  14.1 19.5 %collective-permute-start.4 = (bf16[2,1024,128]{2,1,0:T(8,128)(2,1)S(1)}, bf16[2,1024,128]{2,1,0:T(8,128)(2,1)S(1)}, u32[]{:S(2)}, u32[]{:S(2)}) collective-permute-start(bf16[2,1024,128]{2,1,0:T(8,128)(2,1)S(1)} %pad_maximum_fusion.1), channel_id=1, source_target_pairs={{0,8},{4,12},{8,0},{12,4},{1,9},{5,13},{9,1},{13,5},{2,10},{6,14},... | collective-permute-start | bytes 1572872 | tf_op jit(solution)/shard_map/ppermute | solution.py:241
  14.6 18.4 %collective-permute-start.7 = (bf16[1024,128]{1,0:T(8,128)(2,1)S(1)}, bf16[1024,128]{1,0:T(8,128)(2,1)S(1)}, u32[]{:S(2)}, u32[]{:S(2)}) collective-permute-start(bf16[1024,128]{1,0:T(8,128)(2,1)S(1)} %collective-permute-done.3), channel_id=1, source_target_pairs={{0,12},{4,0},{8,4},{12,8},{1,13},{5,1},{9,5},{13,9},{2,14},{6,2},{... | collective-permute-start | bytes 786440 | tf_op jit(solution)/shard_map/ppermute | solution.py:241
  16.3 25.1 %collective-permute-start.9 = (bf16[2,1024,128]{2,1,0:T(8,128)(2,1)S(1)}, bf16[2,1024,128]{2,1,0:T(8,128)(2,1)S(1)}, u32[]{:S(2)}, u32[]{:S(2)}) collective-permute-start(bf16[2,1024,128]{2,1,0:T(8,128)(2,1)S(1)} %pad_maximum_fusion.q_ref), channel_id=1, source_target_pairs={{0,48},{16,0},{32,16},{48,32},{1,49},{17,1},{33,17},{49,33},{2,50}... | collective-permute-start | bytes 1572872 | tf_op jit(solution)/shard_map/ppermute | solution.py:241
  17.3 30.3 %collective-permute-start.1 = (bf16[2,1024,128]{2,1,0:T(8,128)(2,1)S(1)}, bf16[2,1024,128]{2,1,0:T(8,128)(2,1)S(1)}, u32[]{:S(2)}, u32[]{:S(2)}) collective-permute-start(bf16[2,1024,128]{2,1,0:T(8,128)(2,1)S(1)} %pad_maximum_fusion.q_ref), channel_id=1, source_target_pairs={{0,16},{16,32},{32,48},{48,0},{1,17},{17,33},{33,49},{49,1},{2,18}... | collective-permute-start | bytes 1572872 | tf_op jit(solution)/shard_map/ppermute | solution.py:241
  33.0 8.2 %collective-permute-start.6 = (bf16[1024,128]{1,0:T(8,128)(2,1)S(1)}, bf16[1024,128]{1,0:T(8,128)(2,1)S(1)}, u32[]{:S(2)}, u32[]{:S(2)}) collective-permute-start(bf16[1024,128]{1,0:T(8,128)(2,1)S(1)} %collective-permute-done.3), channel_id=1, source_target_pairs={{0,4},{4,8},{8,12},{12,0},{1,5},{5,9},{9,13},{13,1},{2,6},{6,10},{... | collective-permute-start | bytes 786440 | tf_op jit(solution)/shard_map/ppermute | solution.py:241
  33.6 22.5 %collective-permute-start.11 = (bf16[2,1024,128]{2,1,0:T(8,128)(2,1)S(1)}, bf16[2,1024,128]{2,1,0:T(8,128)(2,1)S(1)}, u32[]{:S(2)}, u32[]{:S(2)}) collective-permute-start(bf16[2,1024,128]{2,1,0:T(8,128)(2,1)S(1)} %pad_maximum_fusion.q_ref), channel_id=1, source_target_pairs={{0,32},{16,48},{32,0},{48,16},{1,33},{17,49},{33,1},{49,17},{2,34}... | collective-permute-start | bytes 1572872 | tf_op jit(solution)/shard_map/ppermute | solution.py:241
  47.5 29.5 %collective-permute-start.10 = (bf16[2,144,1024]{2,1,0:T(8,128)(2,1)S(1)}, bf16[2,144,1024]{2,1,0:T(8,128)(2,1)S(1)}, u32[]{:S(2)}, u32[]{:S(2)}) collective-permute-start(bf16[2,144,1024]{2,1,0:T(8,128)(2,1)S(1)} %attend3.1), channel_id=1, source_target_pairs={{0,16},{16,32},{32,48},{48,0},{1,17},{17,33},{33,49},{49,1},{2,18}... | collective-permute-start | bytes 1769480 | tf_op jit(solution)/shard_map/ppermute | solution.py:241
  53.3 23.7 %collective-permute-start.8 = (bf16[2,144,1024]{2,1,0:T(8,128)(2,1)S(1)}, bf16[2,144,1024]{2,1,0:T(8,128)(2,1)S(1)}, u32[]{:S(2)}, u32[]{:S(2)}) collective-permute-start(bf16[2,144,1024]{2,1,0:T(8,128)(2,1)S(1)} %attend1.1), channel_id=1, source_target_pairs={{0,48},{16,0},{32,16},{48,32},{1,49},{17,1},{33,17},{49,33},{2,50}... | collective-permute-start | bytes 1769480 | tf_op jit(solution)/shard_map/ppermute | solution.py:241
  61.5 23.0 %collective-permute-start.12 = (bf16[2,144,1024]{2,1,0:T(8,128)(2,1)S(1)}, bf16[2,144,1024]{2,1,0:T(8,128)(2,1)S(1)}, u32[]{:S(2)}, u32[]{:S(2)}) collective-permute-start(bf16[2,144,1024]{2,1,0:T(8,128)(2,1)S(1)} %attend2.1), channel_id=1, source_target_pairs={{0,32},{16,48},{32,0},{48,16},{1,33},{17,49},{33,1},{49,17},{2,34}... | collective-permute-start | bytes 1769480 | tf_op jit(solution)/shard_map/ppermute | solution.py:241

commit v2 on v1

--- a/solution.py
+++ b/solution.py
@@ -236,6 +236,10 @@
                 )
 
 
+def pinned(value):
+    return pltpu.with_memory_space_constraint(value, pltpu.HBM)
+
+
 def ring(value, axis, steps):
     size = lax.axis_size(axis)
     return lax.ppermute(value, axis, [(at, (at + steps) % size) for at in range(size)])
@@ -266,7 +270,7 @@
         ],
         compiler_params=PARAMS,
         name="pack_keys",
-    )(place, key_rows, value_rows)
+    )(place, pinned(key_rows), pinned(value_rows))
     q_own, q_other = pl.pallas_call(
         pack_queries_kernel,
         out_shape=(message,) * 2,
@@ -275,22 +279,23 @@
         scratch_shapes=[pltpu.VMEM((BLOCK, 512), jnp.bfloat16), pltpu.SemaphoreType.DMA],
         compiler_params=PARAMS,
         name="pack_queries",
-    )(place, query_rows, kv_own)
+    )(place, pinned(query_rows), kv_own)
     kv_mirror = routed(kv_other, lambda h, r: (1 - h, 3 - r))
     q_swap = ring(q_other, "xl", 1)
     kv_own, _ = lax.optimization_barrier((kv_own, q_other))
     own_near = [ring(kv_own, "z", k) for k in (1, 3)]
     mirror_near = [ring(kv_mirror, "z", k) for k in (1, 3)]
-    kv_far = ring(jnp.stack([kv_own, kv_mirror]), "z", 2)
+    kv_pair = jnp.stack([kv_own, kv_mirror])
+    kv_pair, *near = lax.optimization_barrier((kv_pair, *own_near, *mirror_near))
+    own_near, mirror_near = near[:2], near[2:]
+    kv_far = ring(kv_pair, "z", 2)
     blocks = jnp.stack(
         [kv_own, own_near[0], kv_far[0], own_near[1]]
         + [kv_mirror, mirror_near[0], kv_far[1], mirror_near[1]]
     )
     q_pair = jnp.stack([q_own, q_swap])
-    queries = {k: ring(q_pair, "y", k) for k in (1, 3)}
-    q_late, _ = lax.optimization_barrier((q_pair, mirror_near[1]))
-    queries[2] = ring(q_late, "y", 2)
-    queries[0] = q_pair
+    queries = {0: q_pair, 2: ring(q_pair, "y", 2)}
+    queries |= {k: ring(q_pair, "y", k) for k in (3, 1)}
     parts = [ring(attend(k, place, queries[k], blocks), "y", 4 - k) for k in (1, 3, 2)]
     parts.append(attend(0, place, queries[0], blocks))
     merged = pl.pallas_call(

time: 102 us -> 98.2 us (0.963)
  the two profiles are of different devices: /device:TPU:120 before, /device:TPU:1 now
where the time goes in v2:
time: 98.2 us; the launch traced here: 98 us
  waiting for transfers between devices  32.3 us (33%)
  Pallas kernels  27.3 us (28%)
  starting transfers between devices  21.5 us (22%)
  blocking collectives  15.5 us (16%)
  local copies, waits for them, and re-layouts  1.12 us (1%)
    ppermute x12, waiting for transfers between devices, ring(): lax.ppermute(value, axis, [(at, (at + steps) % size) for at in range(size)])  31.9 us
    pallas_call x4, Pallas kernels, attend(): pl.pallas_call(functools.partial(attend_kernel, step), out_shape=jax.Shap...  22.8 us
    ppermute x12, starting transfers between devices, ring(): lax.ppermute(value, axis, [(at, (at + steps) % size) for at in range(size)])  16.9 us
    all_to_all x1, blocking collectives, on_device(): lax.all_to_all(merged, ('xh', 'core', 'xl'), split_axis=0, concat_axis=0,...  15.5 us
    ppermute x1, starting transfers between devices, routed(): return lax.ppermute(value, ('xl', 'y'), pairs)  4.57 us
  transfers between devices with their start and end apart: 13, of which 8 were waited for; matrix products, arithmetic and copies ran while one was open for 0% of the time, Pallas kernels for 25%

profile of v2, /device:TPU:1, one launch (start us, length us, event | category | flops | bytes accessed | tf_op | source)
XLA Modules:
  0.0 98.0 jit_solution(8353326939105644604)
XLA Ops:
  0.0 0.1 pad_add_fusion.place
  0.1 1.8 %pack_keys.1 = (bf16[1024,128]{1,0:T(8,128)(2,1)S(1)}, bf16[1024,128]{1,0:T(8,128)(2,1)S(1)}) custom-call(s32[3]{0:T(128)S(1)} %pad_add_fusion.place, bf16[512,256]{1,0:T(8,128)(2,1)} %key_in.1, bf16[512,256]{1,0:T(8,128)(2,1)} %value_in.1), custom_call_target="tpu_custom_call" | custom-call | tf_op jit(solution)/shard_map/pack_keys/pallas_call | solution.py:261
  1.8 4.6 %collective-permute-start.2 = (bf16[1024,128]{1,0:T(8,128)(2,1)S(1)}, bf16[1024,128]{1,0:T(8,128)(2,1)S(1)}, u32[]{:S(2)}, u32[]{:S(2)}) collective-permute-start(bf16[1024,128]{1,0:T(8,128)(2,1)S(1)} %get-tuple-element.19), channel_id=1, source_target_pairs={{0,112},{16,96},{32,80},{48,64},{64,48},{80,32},{96,16},{112,0},{1... | collective-permute-start | bytes 786440 | tf_op jit(solution)/shard_map/ppermute | solution.py:254
  6.4 1.7 %pack_queries.1 = (bf16[1024,128]{1,0:T(8,128)(2,1)S(1)}, bf16[1024,128]{1,0:T(8,128)(2,1)S(1)}) custom-call(s32[3]{0:T(128)S(1)} %pad_add_fusion.place, bf16[512,512]{1,0:T(8,128)(2,1)} %query_in.1, bf16[1024,128]{1,0:T(8,128)(2,1)S(1)} %get-tuple-element.18.after), custom_call_target="tpu_custom_call" | custom-call | tf_op jit(solution)/shard_map/pack_queries/pallas_call | solution.py:274
  8.1 1.7 %collective-permute-start.3 = (bf16[1024,128]{1,0:T(8,128)(2,1)S(1)}, bf16[1024,128]{1,0:T(8,128)(2,1)S(1)}, u32[]{:S(2)}, u32[]{:S(2)}) collective-permute-start(bf16[1024,128]{1,0:T(8,128)(2,1)S(1)} %get-tuple-element.18.after), channel_id=1, source_target_pairs={{0,4},{4,8},{8,12},{12,0},{1,5},{5,9},{9,13},{13,1},{2,6},{6,10},{... | collective-permute-start | bytes 786440 | tf_op jit(solution)/shard_map/ppermute | solution.py:245
  9.8 2.2 %collective-permute-start.4 = (bf16[1024,128]{1,0:T(8,128)(2,1)S(1)}, bf16[1024,128]{1,0:T(8,128)(2,1)S(1)}, u32[]{:S(2)}, u32[]{:S(2)}) collective-permute-start(bf16[1024,128]{1,0:T(8,128)(2,1)S(1)} %get-tuple-element.18.after), channel_id=1, source_target_pairs={{0,12},{4,0},{8,4},{12,8},{1,13},{5,1},{9,5},{13,9},{2,14},{6,2},{... | collective-permute-start | bytes 786440 | tf_op jit(solution)/shard_map/ppermute | solution.py:245
  12.0 0.3 collective-permute-done.2
  12.3 1.5 %collective-permute-start.5 = (bf16[1024,128]{1,0:T(8,128)(2,1)S(1)}, bf16[1024,128]{1,0:T(8,128)(2,1)S(1)}, u32[]{:S(2)}, u32[]{:S(2)}) collective-permute-start(bf16[1024,128]{1,0:T(8,128)(2,1)S(1)} %collective-permute-done.2), channel_id=1, source_target_pairs={{0,4},{4,8},{8,12},{12,0},{1,5},{5,9},{9,13},{13,1},{2,6},{6,10},{... | collective-permute-start | bytes 786440 | tf_op jit(solution)/shard_map/ppermute | solution.py:245
  13.9 2.1 %collective-permute-start.6 = (bf16[1024,128]{1,0:T(8,128)(2,1)S(1)}, bf16[1024,128]{1,0:T(8,128)(2,1)S(1)}, u32[]{:S(2)}, u32[]{:S(2)}) collective-permute-start(bf16[1024,128]{1,0:T(8,128)(2,1)S(1)} %collective-permute-done.2), channel_id=1, source_target_pairs={{0,12},{4,0},{8,4},{12,8},{1,13},{5,1},{9,5},{13,9},{2,14},{6,2},{... | collective-permute-start | bytes 786440 | tf_op jit(solution)/shard_map/ppermute | solution.py:245
  16.0 1.0 %collective-permute-start = (bf16[1024,128]{1,0:T(8,128)(2,1)S(1)}, bf16[1024,128]{1,0:T(8,128)(2,1)S(1)}, u32[]{:S(2)}, u32[]{:S(2)}) collective-permute-start(bf16[1024,128]{1,0:T(8,128)(2,1)S(1)} %get-tuple-element.17), channel_id=1, source_target_pairs={{0,64},{64,0},{1,65},{65,1},{2,66},{66,2},{3,67},{67,3},{4,68},{68... | collective-permute-start | bytes 786440 | tf_op jit(solution)/shard_map/ppermute | solution.py:245
  17.0 0.1 pad_maximum_fusion.1
  17.1 0.6 collective-permute-done.3
  17.6 5.6 %collective-permute-done.5 = bf16[1024,128]{1,0:T(8,128)(2,1)S(1)} collective-permute-done((bf16[1024,128]{1,0:T(8,128)(2,1)S(1)}, bf16[1024,128]{1,0:T(8,128)(2,1)S(1)}, u32[]{:S(2)}, u32[]{:S(2)}) %collective-permute-start.5) | collective-permute-done | bytes 262176 | tf_op jit(solution)/shard_map/ppermute | solution.py:245
  23.3 2.3 %collective-permute-start.7 = (bf16[2,1024,128]{2,1,0:T(8,128)(2,1)S(1)}, bf16[2,1024,128]{2,1,0:T(8,128)(2,1)S(1)}, u32[]{:S(2)}, u32[]{:S(2)}) collective-permute-start(bf16[2,1024,128]{2,1,0:T(8,128)(2,1)S(1)} %pad_maximum_fusion.1), channel_id=1, source_target_pairs={{0,8},{4,12},{8,0},{12,4},{1,9},{5,13},{9,1},{13,5},{2,10},{6,14},... | collective-permute-start | bytes 1572872 | tf_op jit(solution)/shard_map/ppermute | solution.py:245
  25.6 0.1 pad_maximum_fusion.q_ref
  25.6 0.1 collective-permute-start.11
  25.7 2.3 %collective-permute-start.9 = (bf16[2,1024,128]{2,1,0:T(8,128)(2,1)S(1)}, bf16[2,1024,128]{2,1,0:T(8,128)(2,1)S(1)}, u32[]{:S(2)}, u32[]{:S(2)}) collective-permute-start(bf16[2,1024,128]{2,1,0:T(8,128)(2,1)S(1)} %pad_maximum_fusion.q_ref), channel_id=1, source_target_pairs={{0,48},{16,0},{32,16},{48,32},{1,49},{17,1},{33,17},{49,33},{2,50}... | collective-permute-start | bytes 1572872 | tf_op jit(solution)/shard_map/ppermute | solution.py:245
  28.1 8.6 %collective-permute-done.7 = bf16[2,1024,128]{2,1,0:T(8,128)(2,1)S(1)} collective-permute-done((bf16[2,1024,128]{2,1,0:T(8,128)(2,1)S(1)}, bf16[2,1024,128]{2,1,0:T(8,128)(2,1)S(1)}, u32[]{:S(2)}, u32[]{:S(2)}) %collective-permute-start.7) | collective-permute-done | bytes 524320 | tf_op jit(solution)/shard_map/ppermute | solution.py:245
  36.9 1.6 %collective-permute-done.11.q_ref = bf16[2,1024,128]{2,1,0:T(8,128)(2,1)S(1)} collective-permute-done((bf16[2,1024,128]{2,1,0:T(8,128)(2,1)S(1)}, bf16[2,1024,128]{2,1,0:T(8,128)(2,1)S(1)}, u32[]{:S(2)}, u32[]{:S(2)}) %collective-permute-start.11) | collective-permute-done | bytes 524320 | tf_op jit(solution)/shard_map/ppermute | solution.py:245
  38.5 5.4 %attend2.1 = bf16[2,144,1024]{2,1,0:T(8,128)(2,1)S(1)} custom-call(s32[3]{0:T(128)S(1)} %pad_add_fusion.place, bf16[2,1024,128]{2,1,0:T(8,128)(2,1)S(1)} %collective-permute-done.11.q_ref, bf16[8,1024,128]{2,1,0:T(8,128)(2,1)S(1)} %bitcast_dynamic-update-slice_fusion.kv_ref), custom_call_target="tpu_custom_call" | custom-call | tf_op jit(solution)/shard_map/attend2/pallas_call | solution.py:198
  43.9 0.1 collective-permute-start.12
  44.0 7.1 %collective-permute-done.9.q_ref = bf16[2,1024,128]{2,1,0:T(8,128)(2,1)S(1)} collective-permute-done((bf16[2,1024,128]{2,1,0:T(8,128)(2,1)S(1)}, bf16[2,1024,128]{2,1,0:T(8,128)(2,1)S(1)}, u32[]{:S(2)}, u32[]{:S(2)}) %collective-permute-start.9) | collective-permute-done | bytes 524320 | tf_op jit(solution)/shard_map/ppermute | solution.py:245
  51.1 5.5 %attend3.1 = bf16[2,144,1024]{2,1,0:T(8,128)(2,1)S(1)} custom-call(s32[3]{0:T(128)S(1)} %pad_add_fusion.place, bf16[2,1024,128]{2,1,0:T(8,128)(2,1)S(1)} %collective-permute-done.9.q_ref, bf16[8,1024,128]{2,1,0:T(8,128)(2,1)S(1)} %bitcast_dynamic-update-slice_fusion.kv_ref), custom_call_target="tpu_custom_call" | custom-call | tf_op jit(solution)/shard_map/attend3/pallas_call | solution.py:198
  56.6 3.5 %collective-permute-start.10 = (bf16[2,144,1024]{2,1,0:T(8,128)(2,1)S(1)}, bf16[2,144,1024]{2,1,0:T(8,128)(2,1)S(1)}, u32[]{:S(2)}, u32[]{:S(2)}) collective-permute-start(bf16[2,144,1024]{2,1,0:T(8,128)(2,1)S(1)} %attend3.1), channel_id=1, source_target_pairs={{0,16},{16,32},{32,48},{48,0},{1,17},{17,33},{33,49},{49,1},{2,18}... | collective-permute-start | bytes 1769480 | tf_op jit(solution)/shard_map/ppermute | solution.py:245
  60.2 6.8 %attend1.1 = bf16[2,144,1024]{2,1,0:T(8,128)(2,1)S(1)} custom-call(s32[3]{0:T(128)S(1)} %pad_add_fusion.place, bf16[2,1024,128]{2,1,0:T(8,128)(2,1)S(1)} %collective-permute-done.1.q_ref, bf16[8,1024,128]{2,1,0:T(8,128)(2,1)S(1)} %bitcast_dynamic-update-slice_fusion.kv_ref), custom_call_target="tpu_custom_call" | custom-call | tf_op jit(solution)/shard_map/attend1/pallas_call | solution.py:198
  67.0 0.1 collective-permute-start.8
  67.1 5.0 %attend0.1.refs_3_ = bf16[2,144,1024]{2,1,0:T(8,128)(2,1)S(1)} custom-call(s32[3]{0:T(128)S(1)} %pad_add_fusion.place, bf16[2,1024,128]{2,1,0:T(8,128)(2,1)S(1)} %pad_maximum_fusion.q_ref, bf16[8,1024,128]{2,1,0:T(8,128)(2,1)S(1)} %bitcast_dynamic-update-slice_fusion.kv_ref), custom_call_target="tpu_custom_call" | custom-call | tf_op jit(solution)/shard_map/attend0/pallas_call | solution.py:198
  72.1 5.1 %collective-permute-done.10.refs_1_ = bf16[2,144,1024]{2,1,0:T(8,128)(2,1)S(1)} collective-permute-done((bf16[2,144,1024]{2,1,0:T(8,128)(2,1)S(1)}, bf16[2,144,1024]{2,1,0:T(8,128)(2,1)S(1)}, u32[]{:S(2)}, u32[]{:S(2)}) %collective-permute-start.10) | collective-permute-done | bytes 589856 | tf_op jit(solution)/shard_map/ppermute | solution.py:245
  77.2 3.3 %collective-permute-done.8.refs_0_ = bf16[2,144,1024]{2,1,0:T(8,128)(2,1)S(1)} collective-permute-done((bf16[2,144,1024]{2,1,0:T(8,128)(2,1)S(1)}, bf16[2,144,1024]{2,1,0:T(8,128)(2,1)S(1)}, u32[]{:S(2)}, u32[]{:S(2)}) %collective-permute-start.8) | collective-permute-done | bytes 589856 | tf_op jit(solution)/shard_map/ppermute | solution.py:245
  80.5 1.1 %merge.1 = bf16[4,2,128,256]{3,2,1,0:T(8,128)(2,1)S(1)} custom-call(s32[3]{0:T(128)S(1)} %pad_add_fusion.place, bf16[2,144,1024]{2,1,0:T(8,128)(2,1)S(1)} %collective-permute-done.8.refs_0_, bf16[2,144,1024]{2,1,0:T(8,128)(2,1)S(1)} %collective-permute-done.10.refs_1_, bf16[2,144,1024]{2,1,0:T(8,128)(2,1)S(1)} %collective-permute-done.12.refs_2_, ...), custom_call_target="tpu_custom_call" | custom-call | tf_op jit(solution)/shard_map/merge/pallas_call | solution.py:301
  81.7 15.5 %all_to_all.5 = bf16[8,128,256]{2,1,0:T(8,128)(2,1)S(1)} all-to-all(bf16[8,128,256]{2,1,0:T(8,128)(2,1)S(1)} %bitcast.22), channel_id=1, replica_groups=mesh['xl'=2,'y'=4,'z'=4,'xh'=2,'core'=2] {'xh','core','xl'}, dimensions={0} | all-to-all | bytes 1048576 | tf_op jit(solution)/shard_map/all_to_all | solution.py:310
  97.2 0.8 copy.5
  (14 shorter events, 0.3 us)
Async XLA Ops:
  1.8 10.5 %collective-permute-start.2 = (bf16[1024,128]{1,0:T(8,128)(2,1)S(1)}, bf16[1024,128]{1,0:T(8,128)(2,1)S(1)}, u32[]{:S(2)}, u32[]{:S(2)}) collective-permute-start(bf16[1024,128]{1,0:T(8,128)(2,1)S(1)} %get-tuple-element.19), channel_id=1, source_target_pairs={{0,112},{16,96},{32,80},{48,64},{64,48},{80,32},{96,16},{112,0},{1... | collective-permute-start | bytes 786440 | tf_op jit(solution)/shard_map/ppermute | solution.py:254
  8.1 9.5 %collective-permute-start.3 = (bf16[1024,128]{1,0:T(8,128)(2,1)S(1)}, bf16[1024,128]{1,0:T(8,128)(2,1)S(1)}, u32[]{:S(2)}, u32[]{:S(2)}) collective-permute-start(bf16[1024,128]{1,0:T(8,128)(2,1)S(1)} %get-tuple-element.18.after), channel_id=1, source_target_pairs={{0,4},{4,8},{8,12},{12,0},{1,5},{5,9},{9,13},{13,1},{2,6},{6,10},{... | collective-permute-start | bytes 786440 | tf_op jit(solution)/shard_map/ppermute | solution.py:245
  9.8 7.8 %collective-permute-start.4 = (bf16[1024,128]{1,0:T(8,128)(2,1)S(1)}, bf16[1024,128]{1,0:T(8,128)(2,1)S(1)}, u32[]{:S(2)}, u32[]{:S(2)}) collective-permute-start(bf16[1024,128]{1,0:T(8,128)(2,1)S(1)} %get-tuple-element.18.after), channel_id=1, source_target_pairs={{0,12},{4,0},{8,4},{12,8},{1,13},{5,1},{9,5},{13,9},{2,14},{6,2},{... | collective-permute-start | bytes 786440 | tf_op jit(solution)/shard_map/ppermute | solution.py:245
  12.3 10.9 %collective-permute-start.5 = (bf16[1024,128]{1,0:T(8,128)(2,1)S(1)}, bf16[1024,128]{1,0:T(8,128)(2,1)S(1)}, u32[]{:S(2)}, u32[]{:S(2)}) collective-permute-start(bf16[1024,128]{1,0:T(8,128)(2,1)S(1)} %collective-permute-done.2), channel_id=1, source_target_pairs={{0,4},{4,8},{8,12},{12,0},{1,5},{5,9},{9,13},{13,1},{2,6},{6,10},{... | collective-permute-start | bytes 786440 | tf_op jit(solution)/shard_map/ppermute | solution.py:245
  13.9 9.4 %collective-permute-start.6 = (bf16[1024,128]{1,0:T(8,128)(2,1)S(1)}, bf16[1024,128]{1,0:T(8,128)(2,1)S(1)}, u32[]{:S(2)}, u32[]{:S(2)}) collective-permute-start(bf16[1024,128]{1,0:T(8,128)(2,1)S(1)} %collective-permute-done.2), channel_id=1, source_target_pairs={{0,12},{4,0},{8,4},{12,8},{1,13},{5,1},{9,5},{13,9},{2,14},{6,2},{... | collective-permute-start | bytes 786440 | tf_op jit(solution)/shard_map/ppermute | solution.py:245
  16.0 9.6 %collective-permute-start = (bf16[1024,128]{1,0:T(8,128)(2,1)S(1)}, bf16[1024,128]{1,0:T(8,128)(2,1)S(1)}, u32[]{:S(2)}, u32[]{:S(2)}) collective-permute-start(bf16[1024,128]{1,0:T(8,128)(2,1)S(1)} %get-tuple-element.17), channel_id=1, source_target_pairs={{0,64},{64,0},{1,65},{65,1},{2,66},{66,2},{3,67},{67,3},{4,68},{68... | collective-permute-start | bytes 786440 | tf_op jit(solution)/shard_map/ppermute | solution.py:245
  23.3 13.4 %collective-permute-start.7 = (bf16[2,1024,128]{2,1,0:T(8,128)(2,1)S(1)}, bf16[2,1024,128]{2,1,0:T(8,128)(2,1)S(1)}, u32[]{:S(2)}, u32[]{:S(2)}) collective-permute-start(bf16[2,1024,128]{2,1,0:T(8,128)(2,1)S(1)} %pad_maximum_fusion.1), channel_id=1, source_target_pairs={{0,8},{4,12},{8,0},{12,4},{1,9},{5,13},{9,1},{13,5},{2,10},{6,14},... | collective-permute-start | bytes 1572872 | tf_op jit(solution)/shard_map/ppermute | solution.py:245
  25.6 12.9 %collective-permute-start.11 = (bf16[2,1024,128]{2,1,0:T(8,128)(2,1)S(1)}, bf16[2,1024,128]{2,1,0:T(8,128)(2,1)S(1)}, u32[]{:S(2)}, u32[]{:S(2)}) collective-permute-start(bf16[2,1024,128]{2,1,0:T(8,128)(2,1)S(1)} %pad_maximum_fusion.q_ref), channel_id=1, source_target_pairs={{0,32},{16,48},{32,0},{48,16},{1,33},{17,49},{33,1},{49,17},{2,34}... | collective-permute-start | bytes 1572872 | tf_op jit(solution)/shard_map/ppermute | solution.py:245
  25.7 25.4 %collective-permute-start.9 = (bf16[2,1024,128]{2,1,0:T(8,128)(2,1)S(1)}, bf16[2,1024,128]{2,1,0:T(8,128)(2,1)S(1)}, u32[]{:S(2)}, u32[]{:S(2)}) collective-permute-start(bf16[2,1024,128]{2,1,0:T(8,128)(2,1)S(1)} %pad_maximum_fusion.q_ref), channel_id=1, source_target_pairs={{0,48},{16,0},{32,16},{48,32},{1,49},{17,1},{33,17},{49,33},{2,50}... | collective-permute-start | bytes 1572872 | tf_op jit(solution)/shard_map/ppermute | solution.py:245
  28.0 32.2 %collective-permute-start.1 = (bf16[2,1024,128]{2,1,0:T(8,128)(2,1)S(1)}, bf16[2,1024,128]{2,1,0:T(8,128)(2,1)S(1)}, u32[]{:S(2)}, u32[]{:S(2)}) collective-permute-start(bf16[2,1024,128]{2,1,0:T(8,128)(2,1)S(1)} %pad_maximum_fusion.q_ref), channel_id=1, source_target_pairs={{0,16},{16,32},{32,48},{48,0},{1,17},{17,33},{33,49},{49,1},{2,18}... | collective-permute-start | bytes 1572872 | tf_op jit(solution)/shard_map/ppermute | solution.py:245
  43.9 28.2 %collective-permute-start.12 = (bf16[2,144,1024]{2,1,0:T(8,128)(2,1)S(1)}, bf16[2,144,1024]{2,1,0:T(8,128)(2,1)S(1)}, u32[]{:S(2)}, u32[]{:S(2)}) collective-permute-start(bf16[2,144,1024]{2,1,0:T(8,128)(2,1)S(1)} %attend2.1), channel_id=1, source_target_pairs={{0,32},{16,48},{32,0},{48,16},{1,33},{17,49},{33,1},{49,17},{2,34}... | collective-permute-start | bytes 1769480 | tf_op jit(solution)/shard_map/ppermute | solution.py:245
  56.6 20.6 %collective-permute-start.10 = (bf16[2,144,1024]{2,1,0:T(8,128)(2,1)S(1)}, bf16[2,144,1024]{2,1,0:T(8,128)(2,1)S(1)}, u32[]{:S(2)}, u32[]{:S(2)}) collective-permute-start(bf16[2,144,1024]{2,1,0:T(8,128)(2,1)S(1)} %attend3.1), channel_id=1, source_target_pairs={{0,16},{16,32},{32,48},{48,0},{1,17},{17,33},{33,49},{49,1},{2,18}... | collective-permute-start | bytes 1769480 | tf_op jit(solution)/shard_map/ppermute | solution.py:245
  67.0 13.6 %collective-permute-start.8 = (bf16[2,144,1024]{2,1,0:T(8,128)(2,1)S(1)}, bf16[2,144,1024]{2,1,0:T(8,128)(2,1)S(1)}, u32[]{:S(2)}, u32[]{:S(2)}) collective-permute-start(bf16[2,144,1024]{2,1,0:T(8,128)(2,1)S(1)} %attend1.1), channel_id=1, source_target_pairs={{0,48},{16,0},{32,16},{48,32},{1,49},{17,1},{33,17},{49,33},{2,50}... | collective-permute-start | bytes 1769480 | tf_op jit(solution)/shard_map/ppermute | solution.py:245

commit v3 on v0

--- a/solution.py
+++ b/solution.py
@@ -29,28 +29,34 @@
     return pl.BlockSpec(memory_space=pltpu.SMEM)
 
 
-def pack_keys_kernel(place, key_ref, value_ref, kv_own, kv_other):
+def pack_kernel(
+    place, query_in, key_in, value_in, kv_other, q_other, kv_own, q_own, query_ref, key_ref, value_ref, done
+):
     half = place[0]
+    copies = [
+        pltpu.make_async_copy(key_in, key_ref, done.at[0]),
+        pltpu.make_async_copy(value_in, value_ref, done.at[1]),
+        pltpu.make_async_copy(query_in, query_ref, done.at[2]),
+    ]
+    for copy in copies:
+        copy.start()
+    copies[0].wait()
     for head, kv_out in ((1 - half, kv_other), (half, kv_own)):
         at = pl.multiple_of(head * 128, 128)
         kv_out[:BLOCK] = key_ref[:, pl.ds(at, 128)]
+    copies[1].wait()
+    for head, kv_out in ((1 - half, kv_other), (half, kv_own)):
+        at = pl.multiple_of(head * 128, 128)
         for part in range(4):
             rows = value_ref[part * 128 : (part + 1) * 128, pl.ds(at, 128)]
             kv_out[BLOCK + part * 128 : BLOCK + (part + 1) * 128] = (
                 rows.astype(jnp.float32).T.astype(jnp.bfloat16)
             )
-
-
-def pack_queries_kernel(place, query_ref, after, q_own, q_other):
-    half = place[0]
+    copies[2].wait()
     for head, q_out in ((1 - half, q_other), (half, q_own)):
         for part in range(2):
             at = pl.multiple_of(head * 256 + part * 128, 128)
             q_out[part * BLOCK : (part + 1) * BLOCK] = query_ref[:, pl.ds(at, 128)]
-
-
-def whole(shape):
-    return pl.BlockSpec(shape, lambda _: (0,) * len(shape))
 
 
 def attend_kernel(step, place, q_ref, kv_ref, out_ref, best, acc, held, peak, todo):
@@ -152,7 +158,7 @@
 
         def far(part, strip):
             return jnp.concatenate(
-                [part[:BLOCK], jnp.where(z >= 3, part[BLOCK:], LOWEST)], axis=0
+                [jnp.where(z >= 3, part[:BLOCK], LOWEST), part[BLOCK:]], axis=0
             )
 
         def alone(pair, mask):
@@ -231,6 +237,10 @@
                 )
 
 
+def pinned(value):
+    return pltpu.with_memory_space_constraint(value, pltpu.HBM)
+
+
 def ring(value, axis, steps):
     size = lax.axis_size(axis)
     return lax.ppermute(value, axis, [(at, (at + steps) % size) for at in range(size)])
@@ -249,31 +259,31 @@
     half, y, z = lax.axis_index("xl"), lax.axis_index("y"), lax.axis_index("z")
     place = jnp.stack([half, y, z]).astype(jnp.int32)
     message = jax.ShapeDtypeStruct((ROWS, 128), jnp.bfloat16)
-    kv_own, kv_other = pl.pallas_call(
-        pack_keys_kernel,
-        grid=(1,),
-        out_shape=(message,) * 2,
-        in_specs=[smem(), whole((BLOCK, 256)), whole((BLOCK, 256))],
-        out_specs=tuple(vmem(2)),
+    kv_other, q_other, kv_own, q_own = pl.pallas_call(
+        pack_kernel,
+        out_shape=(message,) * 4,
+        in_specs=[smem()] + [pl.BlockSpec(memory_space=pltpu.HBM)] * 3,
+        out_specs=tuple(vmem(4)),
+        scratch_shapes=[
+            pltpu.VMEM((BLOCK, 512), jnp.bfloat16),
+            pltpu.VMEM((BLOCK, 256), jnp.bfloat16),
+            pltpu.VMEM((BLOCK, 256), jnp.bfloat16),
+            pltpu.SemaphoreType.DMA((3,)),
+        ],
         compiler_params=PARAMS,
-        name="pack_keys",
-    )(place, key_rows, value_rows)
-    q_own, q_other = pl.pallas_call(
-        pack_queries_kernel,
-        grid=(1,),
-        out_shape=(message,) * 2,
-        in_specs=[smem(), whole((BLOCK, 512)), pl.BlockSpec(memory_space=pl.ANY)],
-        out_specs=tuple(vmem(2)),
-        compiler_params=PARAMS,
-        name="pack_queries",
-    )(place, query_rows, kv_own)
+        name="pack",
+    )(place, pinned(query_rows), pinned(key_rows), pinned(value_rows))
     kv_mirror = routed(kv_other, lambda h, r: (1 - h, 3 - r))
     q_swap = ring(q_other, "xl", 1)
-    blocks = [kv_own] + [ring(kv_own, "z", k) for k in (1, 2, 3)]
-    blocks += [kv_mirror] + [ring(kv_mirror, "z", k) for k in (1, 2, 3)]
-    blocks = jnp.stack(blocks)
-    queries = [jnp.stack([q_own, q_swap])]
-    queries += [jnp.stack([ring(q_own, "y", k), ring(q_swap, "y", k)]) for k in (1, 2, 3)]
+    kv_pair = jnp.stack([kv_own, kv_mirror])
+    pairs = {0: kv_pair}
+    pairs |= {k: ring(kv_pair, "z", k) for k in (2, 3, 1)}
+    blocks = jnp.concatenate(
+        [pairs[k][row : row + 1] for row in range(2) for k in (0, 1, 3, 2)], axis=0
+    )
+    q_pair = jnp.stack([q_own, q_swap])
+    queries = {0: q_pair}
+    queries |= {k: ring(q_pair, "y", k) for k in (1, 3, 2)}
     parts = [ring(attend(k, place, queries[k], blocks), "y", 4 - k) for k in (1, 3, 2)]
     parts.append(attend(0, place, queries[0], blocks))
     merged = pl.pallas_call(

time: 100 us -> 94.3 us (0.943); the launches traced: 99.7 us -> 92.8 us
  waiting for transfers between devices: 34.8 us -> 31.7 us
  local copies, waits for them, and re-layouts: 4.05 us -> 1.12 us
  starting transfers between devices: 20 us -> 17.3 us
  blocking collectives: 14.9 us -> 16.6 us
    ppermute x16 -> x10, waiting for transfers between devices: 34.8 us -> 25.8 us  [ring(): lax.ppermute(value, axis, [(at, (at + steps) % size) for at in range(size)])]
    ppermute x1, waiting for transfers between devices: 0.01 us -> 5.91 us  [routed(): return lax.ppermute(value, ('xl', 'y'), pairs)]
    ppermute x16 -> x10, starting transfers between devices: 16.3 us -> 12.8 us  [ring(): lax.ppermute(value, axis, [(at, (at + steps) % size) for at in range(size)])]
    unnamed x13 -> x7, local copies, waits for them, and re-layouts: 3.17 us -> 0.23 us
    all_to_all x1, blocking collectives: 14.9 us -> 16.6 us  [on_device(): lax.all_to_all(merged, ('xh', 'core', 'xl'), split_axis=0, concat_axis=0,...]
  transfers between devices with their start and end apart: 17 -> 11, of which waited for: 5 -> 7; matrix products, arithmetic and copies ran while one was open for 0% -> 0% of each run, Pallas kernels for 24% -> 25%
where the time goes in v3:
time: 94.3 us; the launch traced here: 92.8 us
  waiting for transfers between devices  31.7 us (34%)
  Pallas kernels  25.8 us (27%)
  starting transfers between devices  17.3 us (18%)
  blocking collectives  16.6 us (18%)
  local copies, waits for them, and re-layouts  1.12 us (1%)
    ppermute x10, waiting for transfers between devices, ring(): lax.ppermute(value, axis, [(at, (at + steps) % size) for at in range(size)])  25.8 us
    pallas_call x4, Pallas kernels, attend(): pl.pallas_call(functools.partial(attend_kernel, step), out_shape=jax.Shap...  22.8 us
    all_to_all x1, blocking collectives, on_device(): lax.all_to_all(merged, ('xh', 'core', 'xl'), split_axis=0, concat_axis=0,...  16.6 us
    ppermute x10, starting transfers between devices, ring(): lax.ppermute(value, axis, [(at, (at + steps) % size) for at in range(size)])  12.8 us
    ppermute x1, waiting for transfers between devices, routed(): return lax.ppermute(value, ('xl', 'y'), pairs)  5.91 us
    ppermute x1, starting transfers between devices, routed(): return lax.ppermute(value, ('xl', 'y'), pairs)  4.57 us
  transfers between devices with their start and end apart: 11, of which 7 were waited for; matrix products, arithmetic and copies ran while one was open for 0% of the time, Pallas kernels for 25%

profile of v3, /device:TPU:1, one launch (start us, length us, event | category | flops | bytes accessed | tf_op | source)
XLA Modules:
  0.0 92.8 jit_solution(10540428806632033266)
XLA Ops:
  0.0 0.1 pad_add_fusion.place
  0.1 1.9 %pack.1 = (bf16[1024,128]{1,0:T(8,128)(2,1)S(1)}, bf16[1024,128]{1,0:T(8,128)(2,1)S(1)}, bf16[1024,128]{1,0:T(8,128)(2,1)S(1)}, bf16[1024,128]{1,0:T(8,128)(2,1)S(1)}) custom-call(s32[3]{0:T(128)S(1)} %pad_add_fusion.place, bf16[512,512]{1,0:T(8,128)(2,1)} %query_in.1, bf16[512,256]{1,0:T(8,128)(2,1)} %key_in.1, bf16[512,256]{1,0:T(8,128)(2,1)} %value_in.1), custom_call_target="tpu_custom_call" | custom-call | tf_op jit(solution)/shard_map/pack/pallas_call | solution.py:262
  1.9 4.6 %collective-permute-start.2 = (bf16[1024,128]{1,0:T(8,128)(2,1)S(1)}, bf16[1024,128]{1,0:T(8,128)(2,1)S(1)}, u32[]{:S(2)}, u32[]{:S(2)}) collective-permute-start(bf16[1024,128]{1,0:T(8,128)(2,1)S(1)} %get-tuple-element.12), channel_id=1, source_target_pairs={{0,112},{16,96},{32,80},{48,64},{64,48},{80,32},{96,16},{112,0},{1... | collective-permute-start | bytes 786440 | tf_op jit(solution)/shard_map/ppermute | solution.py:255
  6.5 5.9 %collective-permute-done.2 = bf16[1024,128]{1,0:T(8,128)(2,1)S(1)} collective-permute-done((bf16[1024,128]{1,0:T(8,128)(2,1)S(1)}, bf16[1024,128]{1,0:T(8,128)(2,1)S(1)}, u32[]{:S(2)}, u32[]{:S(2)}) %collective-permute-start.2) | collective-permute-done | bytes 262176 | tf_op jit(solution)/shard_map/ppermute | solution.py:255
  12.4 0.1 pad_maximum_fusion.1
  12.5 1.6 %collective-permute-start.3 = (bf16[2,1024,128]{2,1,0:T(8,128)(2,1)S(1)}, bf16[2,1024,128]{2,1,0:T(8,128)(2,1)S(1)}, u32[]{:S(2)}, u32[]{:S(2)}) collective-permute-start(bf16[2,1024,128]{2,1,0:T(8,128)(2,1)S(1)} %pad_maximum_fusion.1), channel_id=1, source_target_pairs={{0,4},{4,8},{8,12},{12,0},{1,5},{5,9},{9,13},{13,1},{2,6},{6,10},{... | collective-permute-start | bytes 1572872 | tf_op jit(solution)/shard_map/ppermute | solution.py:246
  14.1 1.0 %collective-permute-start = (bf16[1024,128]{1,0:T(8,128)(2,1)S(1)}, bf16[1024,128]{1,0:T(8,128)(2,1)S(1)}, u32[]{:S(2)}, u32[]{:S(2)}) collective-permute-start(bf16[1024,128]{1,0:T(8,128)(2,1)S(1)} %get-tuple-element.10), channel_id=1, source_target_pairs={{0,64},{64,0},{1,65},{65,1},{2,66},{66,2},{3,67},{67,3},{4,68},{68... | collective-permute-start | bytes 786440 | tf_op jit(solution)/shard_map/ppermute | solution.py:246
  15.1 2.2 %collective-permute-start.4 = (bf16[2,1024,128]{2,1,0:T(8,128)(2,1)S(1)}, bf16[2,1024,128]{2,1,0:T(8,128)(2,1)S(1)}, u32[]{:S(2)}, u32[]{:S(2)}) collective-permute-start(bf16[2,1024,128]{2,1,0:T(8,128)(2,1)S(1)} %pad_maximum_fusion.1), channel_id=1, source_target_pairs={{0,12},{4,0},{8,4},{12,8},{1,13},{5,1},{9,5},{13,9},{2,14},{6,2},{... | collective-permute-start | bytes 1572872 | tf_op jit(solution)/shard_map/ppermute | solution.py:246
  17.3 1.3 %collective-permute-start.5 = (bf16[2,1024,128]{2,1,0:T(8,128)(2,1)S(1)}, bf16[2,1024,128]{2,1,0:T(8,128)(2,1)S(1)}, u32[]{:S(2)}, u32[]{:S(2)}) collective-permute-start(bf16[2,1024,128]{2,1,0:T(8,128)(2,1)S(1)} %pad_maximum_fusion.1), channel_id=1, source_target_pairs={{0,8},{4,12},{8,0},{12,4},{1,9},{5,13},{9,1},{13,5},{2,10},{6,14},... | collective-permute-start | bytes 1572872 | tf_op jit(solution)/shard_map/ppermute | solution.py:246
  18.6 1.5 %collective-permute-done = bf16[1024,128]{1,0:T(8,128)(2,1)S(1)} collective-permute-done((bf16[1024,128]{1,0:T(8,128)(2,1)S(1)}, bf16[1024,128]{1,0:T(8,128)(2,1)S(1)}, u32[]{:S(2)}, u32[]{:S(2)}) %collective-permute-start) | collective-permute-done | bytes 262176 | tf_op jit(solution)/shard_map/ppermute | solution.py:246
  20.2 0.1 pad_maximum_fusion.q_ref
  20.2 1.5 %collective-permute-start.9 = (bf16[2,1024,128]{2,1,0:T(8,128)(2,1)S(1)}, bf16[2,1024,128]{2,1,0:T(8,128)(2,1)S(1)}, u32[]{:S(2)}, u32[]{:S(2)}) collective-permute-start(bf16[2,1024,128]{2,1,0:T(8,128)(2,1)S(1)} %pad_maximum_fusion.q_ref), channel_id=1, source_target_pairs={{0,32},{16,48},{32,0},{48,16},{1,33},{17,49},{33,1},{49,17},{2,34}... | collective-permute-start | bytes 1572872 | tf_op jit(solution)/shard_map/ppermute | solution.py:246
  21.7 1.1 %collective-permute-start.7 = (bf16[2,1024,128]{2,1,0:T(8,128)(2,1)S(1)}, bf16[2,1024,128]{2,1,0:T(8,128)(2,1)S(1)}, u32[]{:S(2)}, u32[]{:S(2)}) collective-permute-start(bf16[2,1024,128]{2,1,0:T(8,128)(2,1)S(1)} %pad_maximum_fusion.q_ref), channel_id=1, source_target_pairs={{0,48},{16,0},{32,16},{48,32},{1,49},{17,1},{33,17},{49,33},{2,50}... | collective-permute-start | bytes 1572872 | tf_op jit(solution)/shard_map/ppermute | solution.py:246
  22.8 4.2 %collective-permute-done.3 = bf16[2,1024,128]{2,1,0:T(8,128)(2,1)S(1)} collective-permute-done((bf16[2,1024,128]{2,1,0:T(8,128)(2,1)S(1)}, bf16[2,1024,128]{2,1,0:T(8,128)(2,1)S(1)}, u32[]{:S(2)}, u32[]{:S(2)}) %collective-permute-start.3) | collective-permute-done | bytes 524320 | tf_op jit(solution)/shard_map/ppermute | solution.py:246
  27.0 0.0 collective-permute-start.1
  27.0 0.1 collective-permute-done.4
  27.2 11.9 %collective-permute-done.5 = bf16[2,1024,128]{2,1,0:T(8,128)(2,1)S(1)} collective-permute-done((bf16[2,1024,128]{2,1,0:T(8,128)(2,1)S(1)}, bf16[2,1024,128]{2,1,0:T(8,128)(2,1)S(1)}, u32[]{:S(2)}, u32[]{:S(2)}) %collective-permute-start.5) | collective-permute-done | bytes 524320 | tf_op jit(solution)/shard_map/ppermute | solution.py:246
  39.4 5.4 %attend2.1 = bf16[2,144,1024]{2,1,0:T(8,128)(2,1)S(1)} custom-call(s32[3]{0:T(128)S(1)} %pad_add_fusion.place, bf16[2,1024,128]{2,1,0:T(8,128)(2,1)S(1)} %collective-permute-done.9.q_ref, bf16[8,1024,128]{2,1,0:T(8,128)(2,1)S(1)} %slice_dynamic-update-slice_fusion.kv_ref), custom_call_target="tpu_custom_call" | custom-call | tf_op jit(solution)/shard_map/attend2/pallas_call | solution.py:199
  44.7 0.1 collective-permute-start.10
  44.8 0.7 collective-permute-done.7.q_ref
  45.5 5.5 %attend3.1 = bf16[2,144,1024]{2,1,0:T(8,128)(2,1)S(1)} custom-call(s32[3]{0:T(128)S(1)} %pad_add_fusion.place, bf16[2,1024,128]{2,1,0:T(8,128)(2,1)S(1)} %collective-permute-done.7.q_ref, bf16[8,1024,128]{2,1,0:T(8,128)(2,1)S(1)} %slice_dynamic-update-slice_fusion.kv_ref), custom_call_target="tpu_custom_call" | custom-call | tf_op jit(solution)/shard_map/attend3/pallas_call | solution.py:199
  51.0 3.9 %collective-permute-start.8 = (bf16[2,144,1024]{2,1,0:T(8,128)(2,1)S(1)}, bf16[2,144,1024]{2,1,0:T(8,128)(2,1)S(1)}, u32[]{:S(2)}, u32[]{:S(2)}) collective-permute-start(bf16[2,144,1024]{2,1,0:T(8,128)(2,1)S(1)} %attend3.1), channel_id=1, source_target_pairs={{0,16},{16,32},{32,48},{48,0},{1,17},{17,33},{33,49},{49,1},{2,18}... | collective-permute-start | bytes 1769480 | tf_op jit(solution)/shard_map/ppermute | solution.py:246
  54.9 0.0 collective-permute-done.1.q_ref
  54.9 6.8 %attend1.1 = bf16[2,144,1024]{2,1,0:T(8,128)(2,1)S(1)} custom-call(s32[3]{0:T(128)S(1)} %pad_add_fusion.place, bf16[2,1024,128]{2,1,0:T(8,128)(2,1)S(1)} %collective-permute-done.1.q_ref, bf16[8,1024,128]{2,1,0:T(8,128)(2,1)S(1)} %slice_dynamic-update-slice_fusion.kv_ref), custom_call_target="tpu_custom_call" | custom-call | tf_op jit(solution)/shard_map/attend1/pallas_call | solution.py:199
  61.7 0.1 collective-permute-start.6
  61.8 5.0 %attend0.1.refs_3_ = bf16[2,144,1024]{2,1,0:T(8,128)(2,1)S(1)} custom-call(s32[3]{0:T(128)S(1)} %pad_add_fusion.place, bf16[2,1024,128]{2,1,0:T(8,128)(2,1)S(1)} %pad_maximum_fusion.q_ref, bf16[8,1024,128]{2,1,0:T(8,128)(2,1)S(1)} %slice_dynamic-update-slice_fusion.kv_ref), custom_call_target="tpu_custom_call" | custom-call | tf_op jit(solution)/shard_map/attend0/pallas_call | solution.py:199
  66.8 0.0 collective-permute-done.10.refs_2_
  66.9 7.3 %collective-permute-done.8.refs_1_ = bf16[2,144,1024]{2,1,0:T(8,128)(2,1)S(1)} collective-permute-done((bf16[2,144,1024]{2,1,0:T(8,128)(2,1)S(1)}, bf16[2,144,1024]{2,1,0:T(8,128)(2,1)S(1)}, u32[]{:S(2)}, u32[]{:S(2)}) %collective-permute-start.8) | collective-permute-done | bytes 589856 | tf_op jit(solution)/shard_map/ppermute | solution.py:246
  74.2 0.0 collective-permute-done.6.refs_0_
  74.2 1.1 %merge.1 = bf16[4,2,128,256]{3,2,1,0:T(8,128)(2,1)S(1)} custom-call(s32[3]{0:T(128)S(1)} %pad_add_fusion.place, bf16[2,144,1024]{2,1,0:T(8,128)(2,1)S(1)} %collective-permute-done.6.refs_0_, bf16[2,144,1024]{2,1,0:T(8,128)(2,1)S(1)} %collective-permute-done.8.refs_1_, bf16[2,144,1024]{2,1,0:T(8,128)(2,1)S(1)} %collective-permute-done.10.refs_2_, ...), custom_call_target="tpu_custom_call" | custom-call | tf_op jit(solution)/shard_map/merge/pallas_call | solution.py:289
  75.3 16.6 %all_to_all.5 = bf16[8,128,256]{2,1,0:T(8,128)(2,1)S(1)} all-to-all(bf16[8,128,256]{2,1,0:T(8,128)(2,1)S(1)} %bitcast.13), channel_id=1, replica_groups=mesh['xl'=2,'y'=4,'z'=4,'xh'=2,'core'=2] {'xh','core','xl'}, dimensions={0} | all-to-all | bytes 1048576 | tf_op jit(solution)/shard_map/all_to_all | solution.py:298
  92.0 0.8 copy.5
  (9 shorter events, 0.3 us)
Async XLA Ops:
  1.9 10.5 %collective-permute-start.2 = (bf16[1024,128]{1,0:T(8,128)(2,1)S(1)}, bf16[1024,128]{1,0:T(8,128)(2,1)S(1)}, u32[]{:S(2)}, u32[]{:S(2)}) collective-permute-start(bf16[1024,128]{1,0:T(8,128)(2,1)S(1)} %get-tuple-element.12), channel_id=1, source_target_pairs={{0,112},{16,96},{32,80},{48,64},{64,48},{80,32},{96,16},{112,0},{1... | collective-permute-start | bytes 786440 | tf_op jit(solution)/shard_map/ppermute | solution.py:255
  12.5 14.5 %collective-permute-start.3 = (bf16[2,1024,128]{2,1,0:T(8,128)(2,1)S(1)}, bf16[2,1024,128]{2,1,0:T(8,128)(2,1)S(1)}, u32[]{:S(2)}, u32[]{:S(2)}) collective-permute-start(bf16[2,1024,128]{2,1,0:T(8,128)(2,1)S(1)} %pad_maximum_fusion.1), channel_id=1, source_target_pairs={{0,4},{4,8},{8,12},{12,0},{1,5},{5,9},{9,13},{13,1},{2,6},{6,10},{... | collective-permute-start | bytes 1572872 | tf_op jit(solution)/shard_map/ppermute | solution.py:246
  14.1 6.1 %collective-permute-start = (bf16[1024,128]{1,0:T(8,128)(2,1)S(1)}, bf16[1024,128]{1,0:T(8,128)(2,1)S(1)}, u32[]{:S(2)}, u32[]{:S(2)}) collective-permute-start(bf16[1024,128]{1,0:T(8,128)(2,1)S(1)} %get-tuple-element.10), channel_id=1, source_target_pairs={{0,64},{64,0},{1,65},{65,1},{2,66},{66,2},{3,67},{67,3},{4,68},{68... | collective-permute-start | bytes 786440 | tf_op jit(solution)/shard_map/ppermute | solution.py:246
  15.1 12.1 %collective-permute-start.4 = (bf16[2,1024,128]{2,1,0:T(8,128)(2,1)S(1)}, bf16[2,1024,128]{2,1,0:T(8,128)(2,1)S(1)}, u32[]{:S(2)}, u32[]{:S(2)}) collective-permute-start(bf16[2,1024,128]{2,1,0:T(8,128)(2,1)S(1)} %pad_maximum_fusion.1), channel_id=1, source_target_pairs={{0,12},{4,0},{8,4},{12,8},{1,13},{5,1},{9,5},{13,9},{2,14},{6,2},{... | collective-permute-start | bytes 1572872 | tf_op jit(solution)/shard_map/ppermute | solution.py:246
  17.3 21.8 %collective-permute-start.5 = (bf16[2,1024,128]{2,1,0:T(8,128)(2,1)S(1)}, bf16[2,1024,128]{2,1,0:T(8,128)(2,1)S(1)}, u32[]{:S(2)}, u32[]{:S(2)}) collective-permute-start(bf16[2,1024,128]{2,1,0:T(8,128)(2,1)S(1)} %pad_maximum_fusion.1), channel_id=1, source_target_pairs={{0,8},{4,12},{8,0},{12,4},{1,9},{5,13},{9,1},{13,5},{2,10},{6,14},... | collective-permute-start | bytes 1572872 | tf_op jit(solution)/shard_map/ppermute | solution.py:246
  20.2 19.1 %collective-permute-start.9 = (bf16[2,1024,128]{2,1,0:T(8,128)(2,1)S(1)}, bf16[2,1024,128]{2,1,0:T(8,128)(2,1)S(1)}, u32[]{:S(2)}, u32[]{:S(2)}) collective-permute-start(bf16[2,1024,128]{2,1,0:T(8,128)(2,1)S(1)} %pad_maximum_fusion.q_ref), channel_id=1, source_target_pairs={{0,32},{16,48},{32,0},{48,16},{1,33},{17,49},{33,1},{49,17},{2,34}... | collective-permute-start | bytes 1572872 | tf_op jit(solution)/shard_map/ppermute | solution.py:246
  21.7 23.8 %collective-permute-start.7 = (bf16[2,1024,128]{2,1,0:T(8,128)(2,1)S(1)}, bf16[2,1024,128]{2,1,0:T(8,128)(2,1)S(1)}, u32[]{:S(2)}, u32[]{:S(2)}) collective-permute-start(bf16[2,1024,128]{2,1,0:T(8,128)(2,1)S(1)} %pad_maximum_fusion.q_ref), channel_id=1, source_target_pairs={{0,48},{16,0},{32,16},{48,32},{1,49},{17,1},{33,17},{49,33},{2,50}... | collective-permute-start | bytes 1572872 | tf_op jit(solution)/shard_map/ppermute | solution.py:246
  27.0 27.9 %collective-permute-start.1 = (bf16[2,1024,128]{2,1,0:T(8,128)(2,1)S(1)}, bf16[2,1024,128]{2,1,0:T(8,128)(2,1)S(1)}, u32[]{:S(2)}, u32[]{:S(2)}) collective-permute-start(bf16[2,1024,128]{2,1,0:T(8,128)(2,1)S(1)} %pad_maximum_fusion.q_ref), channel_id=1, source_target_pairs={{0,16},{16,32},{32,48},{48,0},{1,17},{17,33},{33,49},{49,1},{2,18}... | collective-permute-start | bytes 1572872 | tf_op jit(solution)/shard_map/ppermute | solution.py:246
  44.7 22.1 %collective-permute-start.10 = (bf16[2,144,1024]{2,1,0:T(8,128)(2,1)S(1)}, bf16[2,144,1024]{2,1,0:T(8,128)(2,1)S(1)}, u32[]{:S(2)}, u32[]{:S(2)}) collective-permute-start(bf16[2,144,1024]{2,1,0:T(8,128)(2,1)S(1)} %attend2.1), channel_id=1, source_target_pairs={{0,32},{16,48},{32,0},{48,16},{1,33},{17,49},{33,1},{49,17},{2,34}... | collective-permute-start | bytes 1769480 | tf_op jit(solution)/shard_map/ppermute | solution.py:246
  51.0 23.2 %collective-permute-start.8 = (bf16[2,144,1024]{2,1,0:T(8,128)(2,1)S(1)}, bf16[2,144,1024]{2,1,0:T(8,128)(2,1)S(1)}, u32[]{:S(2)}, u32[]{:S(2)}) collective-permute-start(bf16[2,144,1024]{2,1,0:T(8,128)(2,1)S(1)} %attend3.1), channel_id=1, source_target_pairs={{0,16},{16,32},{32,48},{48,0},{1,17},{17,33},{33,49},{49,1},{2,18}... | collective-permute-start | bytes 1769480 | tf_op jit(solution)/shard_map/ppermute | solution.py:246
  61.7 12.5 %collective-permute-start.6 = (bf16[2,144,1024]{2,1,0:T(8,128)(2,1)S(1)}, bf16[2,144,1024]{2,1,0:T(8,128)(2,1)S(1)}, u32[]{:S(2)}, u32[]{:S(2)}) collective-permute-start(bf16[2,144,1024]{2,1,0:T(8,128)(2,1)S(1)} %attend1.1), channel_id=1, source_target_pairs={{0,48},{16,0},{32,16},{48,32},{1,49},{17,1},{33,17},{49,33},{2,50}... | collective-permute-start | bytes 1769480 | tf_op jit(solution)/shard_map/ppermute | solution.py:246

commit v4 on v3

--- a/solution.py
+++ b/solution.py
@@ -283,8 +283,8 @@
     )
     q_pair = jnp.stack([q_own, q_swap])
     queries = {0: q_pair}
-    queries |= {k: ring(q_pair, "y", k) for k in (1, 3, 2)}
-    parts = [ring(attend(k, place, queries[k], blocks), "y", 4 - k) for k in (1, 3, 2)]
+    queries |= {k: ring(q_pair, "y", k) for k in (3, 1, 2)}
+    parts = [ring(attend(k, place, queries[k], blocks), "y", 4 - k) for k in (3, 1, 2)]
     parts.append(attend(0, place, queries[0], blocks))
     merged = pl.pallas_call(
         merge_kernel,

time: 94.3 us -> 95.6 us (1.014)
  the two profiles are of different devices: /device:TPU:1 before, /device:TPU:72 now
where the time goes in v4:
time: 95.6 us; the launch traced here: 95.4 us
  waiting for transfers between devices  31.9 us (33%)
  Pallas kernels  28.7 us (30%)
  starting transfers between devices  19.3 us (20%)
  blocking collectives  14.2 us (15%)
  local copies, waits for them, and re-layouts  1.12 us (1%)
    pallas_call x4, Pallas kernels, attend(): pl.pallas_call(functools.partial(attend_kernel, step), out_shape=jax.Shap...  25.6 us
    ppermute x10, waiting for transfers between devices, ring(): lax.ppermute(value, axis, [(at, (at + steps) % size) for at in range(size)])  25.5 us
    ppermute x10, starting transfers between devices, ring(): lax.ppermute(value, axis, [(at, (at + steps) % size) for at in range(size)])  16.7 us
    all_to_all x1, blocking collectives, on_device(): lax.all_to_all(merged, ('xh', 'core', 'xl'), split_axis=0, concat_axis=0,...  14.2 us
    ppermute x1, waiting for transfers between devices, routed(): return lax.ppermute(value, ('xl', 'y'), pairs)  6.44 us
    ppermute x1, starting transfers between devices, routed(): return lax.ppermute(value, ('xl', 'y'), pairs)  2.58 us
  transfers between devices with their start and end apart: 11, of which 6 were waited for; matrix products, arithmetic and copies ran while one was open for 0% of the time, Pallas kernels for 27%

profile of v4, /device:TPU:72, one launch (start us, length us, event | category | flops | bytes accessed | tf_op | source)
XLA Modules:
  0.0 95.4 jit_solution(7299260299992356308)
XLA Ops:
  0.0 0.1 pad_add_fusion.place
  0.1 1.9 %pack.1 = (bf16[1024,128]{1,0:T(8,128)(2,1)S(1)}, bf16[1024,128]{1,0:T(8,128)(2,1)S(1)}, bf16[1024,128]{1,0:T(8,128)(2,1)S(1)}, bf16[1024,128]{1,0:T(8,128)(2,1)S(1)}) custom-call(s32[3]{0:T(128)S(1)} %pad_add_fusion.place, bf16[512,512]{1,0:T(8,128)(2,1)} %query_in.1, bf16[512,256]{1,0:T(8,128)(2,1)} %key_in.1, bf16[512,256]{1,0:T(8,128)(2,1)} %value_in.1), custom_call_target="tpu_custom_call" | custom-call | tf_op jit(solution)/shard_map/pack/pallas_call | solution.py:262
  1.9 2.6 %collective-permute-start.2 = (bf16[1024,128]{1,0:T(8,128)(2,1)S(1)}, bf16[1024,128]{1,0:T(8,128)(2,1)S(1)}, u32[]{:S(2)}, u32[]{:S(2)}) collective-permute-start(bf16[1024,128]{1,0:T(8,128)(2,1)S(1)} %get-tuple-element.12), channel_id=1, source_target_pairs={{0,112},{16,96},{32,80},{48,64},{64,48},{80,32},{96,16},{112,0},{1... | collective-permute-start | bytes 786440 | tf_op jit(solution)/shard_map/ppermute | solution.py:255
  4.5 6.4 %collective-permute-done.2 = bf16[1024,128]{1,0:T(8,128)(2,1)S(1)} collective-permute-done((bf16[1024,128]{1,0:T(8,128)(2,1)S(1)}, bf16[1024,128]{1,0:T(8,128)(2,1)S(1)}, u32[]{:S(2)}, u32[]{:S(2)}) %collective-permute-start.2) | collective-permute-done | bytes 262176 | tf_op jit(solution)/shard_map/ppermute | solution.py:255
  11.0 0.1 pad_maximum_fusion.1
  11.0 1.7 %collective-permute-start.3 = (bf16[2,1024,128]{2,1,0:T(8,128)(2,1)S(1)}, bf16[2,1024,128]{2,1,0:T(8,128)(2,1)S(1)}, u32[]{:S(2)}, u32[]{:S(2)}) collective-permute-start(bf16[2,1024,128]{2,1,0:T(8,128)(2,1)S(1)} %pad_maximum_fusion.1), channel_id=1, source_target_pairs={{0,4},{4,8},{8,12},{12,0},{1,5},{5,9},{9,13},{13,1},{2,6},{6,10},{... | collective-permute-start | bytes 1572872 | tf_op jit(solution)/shard_map/ppermute | solution.py:246
  12.7 1.5 %collective-permute-start = (bf16[1024,128]{1,0:T(8,128)(2,1)S(1)}, bf16[1024,128]{1,0:T(8,128)(2,1)S(1)}, u32[]{:S(2)}, u32[]{:S(2)}) collective-permute-start(bf16[1024,128]{1,0:T(8,128)(2,1)S(1)} %get-tuple-element.10), channel_id=1, source_target_pairs={{0,64},{64,0},{1,65},{65,1},{2,66},{66,2},{3,67},{67,3},{4,68},{68... | collective-permute-start | bytes 786440 | tf_op jit(solution)/shard_map/ppermute | solution.py:246
  14.2 0.4 collective-permute-start.4
  14.6 1.8 %collective-permute-start.5 = (bf16[2,1024,128]{2,1,0:T(8,128)(2,1)S(1)}, bf16[2,1024,128]{2,1,0:T(8,128)(2,1)S(1)}, u32[]{:S(2)}, u32[]{:S(2)}) collective-permute-start(bf16[2,1024,128]{2,1,0:T(8,128)(2,1)S(1)} %pad_maximum_fusion.1), channel_id=1, source_target_pairs={{0,8},{4,12},{8,0},{12,4},{1,9},{5,13},{9,1},{13,5},{2,10},{6,14},... | collective-permute-start | bytes 1572872 | tf_op jit(solution)/shard_map/ppermute | solution.py:246
  16.5 3.1 %collective-permute-done = bf16[1024,128]{1,0:T(8,128)(2,1)S(1)} collective-permute-done((bf16[1024,128]{1,0:T(8,128)(2,1)S(1)}, bf16[1024,128]{1,0:T(8,128)(2,1)S(1)}, u32[]{:S(2)}, u32[]{:S(2)}) %collective-permute-start) | collective-permute-done | bytes 262176 | tf_op jit(solution)/shard_map/ppermute | solution.py:246
  19.6 0.1 pad_maximum_fusion.q_ref
  19.7 3.6 %collective-permute-start.9 = (bf16[2,1024,128]{2,1,0:T(8,128)(2,1)S(1)}, bf16[2,1024,128]{2,1,0:T(8,128)(2,1)S(1)}, u32[]{:S(2)}, u32[]{:S(2)}) collective-permute-start(bf16[2,1024,128]{2,1,0:T(8,128)(2,1)S(1)} %pad_maximum_fusion.q_ref), channel_id=1, source_target_pairs={{0,32},{16,48},{32,0},{48,16},{1,33},{17,49},{33,1},{49,17},{2,34}... | collective-permute-start | bytes 1572872 | tf_op jit(solution)/shard_map/ppermute | solution.py:246
  23.2 0.0 collective-permute-start.7
  23.3 11.9 %collective-permute-done.3 = bf16[2,1024,128]{2,1,0:T(8,128)(2,1)S(1)} collective-permute-done((bf16[2,1024,128]{2,1,0:T(8,128)(2,1)S(1)}, bf16[2,1024,128]{2,1,0:T(8,128)(2,1)S(1)}, u32[]{:S(2)}, u32[]{:S(2)}) %collective-permute-start.3) | collective-permute-done | bytes 524320 | tf_op jit(solution)/shard_map/ppermute | solution.py:246
  35.1 1.9 %collective-permute-start.1 = (bf16[2,1024,128]{2,1,0:T(8,128)(2,1)S(1)}, bf16[2,1024,128]{2,1,0:T(8,128)(2,1)S(1)}, u32[]{:S(2)}, u32[]{:S(2)}) collective-permute-start(bf16[2,1024,128]{2,1,0:T(8,128)(2,1)S(1)} %pad_maximum_fusion.q_ref), channel_id=1, source_target_pairs={{0,48},{16,0},{32,16},{48,32},{1,49},{17,1},{33,17},{49,33},{2,50}... | collective-permute-start | bytes 1572872 | tf_op jit(solution)/shard_map/ppermute | solution.py:246
  37.0 0.0 collective-permute-done.4
  37.1 0.0 collective-permute-done.5
  37.3 0.0 collective-permute-done.9.q_ref
  37.3 7.6 %attend2.1 = bf16[2,144,1024]{2,1,0:T(8,128)(2,1)S(1)} custom-call(s32[3]{0:T(128)S(1)} %pad_add_fusion.place, bf16[2,1024,128]{2,1,0:T(8,128)(2,1)S(1)} %collective-permute-done.9.q_ref, bf16[8,1024,128]{2,1,0:T(8,128)(2,1)S(1)} %slice_dynamic-update-slice_fusion.kv_ref), custom_call_target="tpu_custom_call" | custom-call | tf_op jit(solution)/shard_map/attend2/pallas_call | solution.py:199
  44.9 0.2 collective-permute-start.10
  45.1 2.1 %collective-permute-done.7.q_ref = bf16[2,1024,128]{2,1,0:T(8,128)(2,1)S(1)} collective-permute-done((bf16[2,1024,128]{2,1,0:T(8,128)(2,1)S(1)}, bf16[2,1024,128]{2,1,0:T(8,128)(2,1)S(1)}, u32[]{:S(2)}, u32[]{:S(2)}) %collective-permute-start.7) | collective-permute-done | bytes 524320 | tf_op jit(solution)/shard_map/ppermute | solution.py:246
  47.2 3.3 %attend1.1 = bf16[2,144,1024]{2,1,0:T(8,128)(2,1)S(1)} custom-call(s32[3]{0:T(128)S(1)} %pad_add_fusion.place, bf16[2,1024,128]{2,1,0:T(8,128)(2,1)S(1)} %collective-permute-done.7.q_ref, bf16[8,1024,128]{2,1,0:T(8,128)(2,1)S(1)} %slice_dynamic-update-slice_fusion.kv_ref), custom_call_target="tpu_custom_call" | custom-call | tf_op jit(solution)/shard_map/attend1/pallas_call | solution.py:199
  50.5 5.5 %collective-permute-start.8 = (bf16[2,144,1024]{2,1,0:T(8,128)(2,1)S(1)}, bf16[2,144,1024]{2,1,0:T(8,128)(2,1)S(1)}, u32[]{:S(2)}, u32[]{:S(2)}) collective-permute-start(bf16[2,144,1024]{2,1,0:T(8,128)(2,1)S(1)} %attend1.1), channel_id=1, source_target_pairs={{0,48},{16,0},{32,16},{48,32},{1,49},{17,1},{33,17},{49,33},{2,50}... | collective-permute-start | bytes 1769480 | tf_op jit(solution)/shard_map/ppermute | solution.py:246
  56.0 0.0 collective-permute-done.1.q_ref
  56.0 8.3 %attend3.1 = bf16[2,144,1024]{2,1,0:T(8,128)(2,1)S(1)} custom-call(s32[3]{0:T(128)S(1)} %pad_add_fusion.place, bf16[2,1024,128]{2,1,0:T(8,128)(2,1)S(1)} %collective-permute-done.1.q_ref, bf16[8,1024,128]{2,1,0:T(8,128)(2,1)S(1)} %slice_dynamic-update-slice_fusion.kv_ref), custom_call_target="tpu_custom_call" | custom-call | tf_op jit(solution)/shard_map/attend3/pallas_call | solution.py:199
  64.3 0.1 collective-permute-start.6
  64.4 6.5 %attend0.1.refs_3_ = bf16[2,144,1024]{2,1,0:T(8,128)(2,1)S(1)} custom-call(s32[3]{0:T(128)S(1)} %pad_add_fusion.place, bf16[2,1024,128]{2,1,0:T(8,128)(2,1)S(1)} %pad_maximum_fusion.q_ref, bf16[8,1024,128]{2,1,0:T(8,128)(2,1)S(1)} %slice_dynamic-update-slice_fusion.kv_ref), custom_call_target="tpu_custom_call" | custom-call | tf_op jit(solution)/shard_map/attend0/pallas_call | solution.py:199
  70.9 0.2 collective-permute-done.8.refs_1_
  71.1 8.2 %collective-permute-done.6.refs_0_ = bf16[2,144,1024]{2,1,0:T(8,128)(2,1)S(1)} collective-permute-done((bf16[2,144,1024]{2,1,0:T(8,128)(2,1)S(1)}, bf16[2,144,1024]{2,1,0:T(8,128)(2,1)S(1)}, u32[]{:S(2)}, u32[]{:S(2)}) %collective-permute-start.6) | collective-permute-done | bytes 589856 | tf_op jit(solution)/shard_map/ppermute | solution.py:246
  79.3 1.1 %merge.1 = bf16[4,2,128,256]{3,2,1,0:T(8,128)(2,1)S(1)} custom-call(s32[3]{0:T(128)S(1)} %pad_add_fusion.place, bf16[2,144,1024]{2,1,0:T(8,128)(2,1)S(1)} %collective-permute-done.6.refs_0_, bf16[2,144,1024]{2,1,0:T(8,128)(2,1)S(1)} %collective-permute-done.8.refs_1_, bf16[2,144,1024]{2,1,0:T(8,128)(2,1)S(1)} %collective-permute-done.10.refs_2_, ...), custom_call_target="tpu_custom_call" | custom-call | tf_op jit(solution)/shard_map/merge/pallas_call | solution.py:289
  80.4 14.2 %all_to_all.5 = bf16[8,128,256]{2,1,0:T(8,128)(2,1)S(1)} all-to-all(bf16[8,128,256]{2,1,0:T(8,128)(2,1)S(1)} %bitcast.13), channel_id=1, replica_groups=mesh['xl'=2,'y'=4,'z'=4,'xh'=2,'core'=2] {'xh','core','xl'}, dimensions={0} | all-to-all | bytes 1048576 | tf_op jit(solution)/shard_map/all_to_all | solution.py:298
  94.6 0.8 copy.5
  (9 shorter events, 0.3 us)
Async XLA Ops:
  1.9 9.0 %collective-permute-start.2 = (bf16[1024,128]{1,0:T(8,128)(2,1)S(1)}, bf16[1024,128]{1,0:T(8,128)(2,1)S(1)}, u32[]{:S(2)}, u32[]{:S(2)}) collective-permute-start(bf16[1024,128]{1,0:T(8,128)(2,1)S(1)} %get-tuple-element.12), channel_id=1, source_target_pairs={{0,112},{16,96},{32,80},{48,64},{64,48},{80,32},{96,16},{112,0},{1... | collective-permute-start | bytes 786440 | tf_op jit(solution)/shard_map/ppermute | solution.py:255
  11.0 24.1 %collective-permute-start.3 = (bf16[2,1024,128]{2,1,0:T(8,128)(2,1)S(1)}, bf16[2,1024,128]{2,1,0:T(8,128)(2,1)S(1)}, u32[]{:S(2)}, u32[]{:S(2)}) collective-permute-start(bf16[2,1024,128]{2,1,0:T(8,128)(2,1)S(1)} %pad_maximum_fusion.1), channel_id=1, source_target_pairs={{0,4},{4,8},{8,12},{12,0},{1,5},{5,9},{9,13},{13,1},{2,6},{6,10},{... | collective-permute-start | bytes 1572872 | tf_op jit(solution)/shard_map/ppermute | solution.py:246
  12.7 6.9 %collective-permute-start = (bf16[1024,128]{1,0:T(8,128)(2,1)S(1)}, bf16[1024,128]{1,0:T(8,128)(2,1)S(1)}, u32[]{:S(2)}, u32[]{:S(2)}) collective-permute-start(bf16[1024,128]{1,0:T(8,128)(2,1)S(1)} %get-tuple-element.10), channel_id=1, source_target_pairs={{0,64},{64,0},{1,65},{65,1},{2,66},{66,2},{3,67},{67,3},{4,68},{68... | collective-permute-start | bytes 786440 | tf_op jit(solution)/shard_map/ppermute | solution.py:246
  14.2 22.8 %collective-permute-start.4 = (bf16[2,1024,128]{2,1,0:T(8,128)(2,1)S(1)}, bf16[2,1024,128]{2,1,0:T(8,128)(2,1)S(1)}, u32[]{:S(2)}, u32[]{:S(2)}) collective-permute-start(bf16[2,1024,128]{2,1,0:T(8,128)(2,1)S(1)} %pad_maximum_fusion.1), channel_id=1, source_target_pairs={{0,12},{4,0},{8,4},{12,8},{1,13},{5,1},{9,5},{13,9},{2,14},{6,2},{... | collective-permute-start | bytes 1572872 | tf_op jit(solution)/shard_map/ppermute | solution.py:246
  14.6 22.4 %collective-permute-start.5 = (bf16[2,1024,128]{2,1,0:T(8,128)(2,1)S(1)}, bf16[2,1024,128]{2,1,0:T(8,128)(2,1)S(1)}, u32[]{:S(2)}, u32[]{:S(2)}) collective-permute-start(bf16[2,1024,128]{2,1,0:T(8,128)(2,1)S(1)} %pad_maximum_fusion.1), channel_id=1, source_target_pairs={{0,8},{4,12},{8,0},{12,4},{1,9},{5,13},{9,1},{13,5},{2,10},{6,14},... | collective-permute-start | bytes 1572872 | tf_op jit(solution)/shard_map/ppermute | solution.py:246
  19.7 17.6 %collective-permute-start.9 = (bf16[2,1024,128]{2,1,0:T(8,128)(2,1)S(1)}, bf16[2,1024,128]{2,1,0:T(8,128)(2,1)S(1)}, u32[]{:S(2)}, u32[]{:S(2)}) collective-permute-start(bf16[2,1024,128]{2,1,0:T(8,128)(2,1)S(1)} %pad_maximum_fusion.q_ref), channel_id=1, source_target_pairs={{0,32},{16,48},{32,0},{48,16},{1,33},{17,49},{33,1},{49,17},{2,34}... | collective-permute-start | bytes 1572872 | tf_op jit(solution)/shard_map/ppermute | solution.py:246
  23.2 23.9 %collective-permute-start.7 = (bf16[2,1024,128]{2,1,0:T(8,128)(2,1)S(1)}, bf16[2,1024,128]{2,1,0:T(8,128)(2,1)S(1)}, u32[]{:S(2)}, u32[]{:S(2)}) collective-permute-start(bf16[2,1024,128]{2,1,0:T(8,128)(2,1)S(1)} %pad_maximum_fusion.q_ref), channel_id=1, source_target_pairs={{0,16},{16,32},{32,48},{48,0},{1,17},{17,33},{33,49},{49,1},{2,18}... | collective-permute-start | bytes 1572872 | tf_op jit(solution)/shard_map/ppermute | solution.py:246
  35.1 20.9 %collective-permute-start.1 = (bf16[2,1024,128]{2,1,0:T(8,128)(2,1)S(1)}, bf16[2,1024,128]{2,1,0:T(8,128)(2,1)S(1)}, u32[]{:S(2)}, u32[]{:S(2)}) collective-permute-start(bf16[2,1024,128]{2,1,0:T(8,128)(2,1)S(1)} %pad_maximum_fusion.q_ref), channel_id=1, source_target_pairs={{0,48},{16,0},{32,16},{48,32},{1,49},{17,1},{33,17},{49,33},{2,50}... | collective-permute-start | bytes 1572872 | tf_op jit(solution)/shard_map/ppermute | solution.py:246
  44.9 26.0 %collective-permute-start.10 = (bf16[2,144,1024]{2,1,0:T(8,128)(2,1)S(1)}, bf16[2,144,1024]{2,1,0:T(8,128)(2,1)S(1)}, u32[]{:S(2)}, u32[]{:S(2)}) collective-permute-start(bf16[2,144,1024]{2,1,0:T(8,128)(2,1)S(1)} %attend2.1), channel_id=1, source_target_pairs={{0,32},{16,48},{32,0},{48,16},{1,33},{17,49},{33,1},{49,17},{2,34}... | collective-permute-start | bytes 1769480 | tf_op jit(solution)/shard_map/ppermute | solution.py:246
  50.5 20.6 %collective-permute-start.8 = (bf16[2,144,1024]{2,1,0:T(8,128)(2,1)S(1)}, bf16[2,144,1024]{2,1,0:T(8,128)(2,1)S(1)}, u32[]{:S(2)}, u32[]{:S(2)}) collective-permute-start(bf16[2,144,1024]{2,1,0:T(8,128)(2,1)S(1)} %attend1.1), channel_id=1, source_target_pairs={{0,48},{16,0},{32,16},{48,32},{1,49},{17,1},{33,17},{49,33},{2,50}... | collective-permute-start | bytes 1769480 | tf_op jit(solution)/shard_map/ppermute | solution.py:246
  64.3 15.0 %collective-permute-start.6 = (bf16[2,144,1024]{2,1,0:T(8,128)(2,1)S(1)}, bf16[2,144,1024]{2,1,0:T(8,128)(2,1)S(1)}, u32[]{:S(2)}, u32[]{:S(2)}) collective-permute-start(bf16[2,144,1024]{2,1,0:T(8,128)(2,1)S(1)} %attend3.1), channel_id=1, source_target_pairs={{0,16},{16,32},{32,48},{48,0},{1,17},{17,33},{33,49},{49,1},{2,18}... | collective-permute-start | bytes 1769480 | tf_op jit(solution)/shard_map/ppermute | solution.py:246

commit v5 on v3

--- a/solution.py
+++ b/solution.py
@@ -275,6 +275,8 @@
     )(place, pinned(query_rows), pinned(key_rows), pinned(value_rows))
     kv_mirror = routed(kv_other, lambda h, r: (1 - h, 3 - r))
     q_swap = ring(q_other, "xl", 1)
+    q_early = ring(q_own, "y", 3)
+    kv_mirror, q_early = lax.optimization_barrier((kv_mirror, q_early))
     kv_pair = jnp.stack([kv_own, kv_mirror])
     pairs = {0: kv_pair}
     pairs |= {k: ring(kv_pair, "z", k) for k in (2, 3, 1)}
@@ -283,7 +285,9 @@
     )
     q_pair = jnp.stack([q_own, q_swap])
     queries = {0: q_pair}
-    queries |= {k: ring(q_pair, "y", k) for k in (1, 3, 2)}
+    queries[1] = ring(q_pair, "y", 1)
+    queries[3] = jnp.stack([q_early, ring(q_swap, "y", 3)])
+    queries[2] = ring(q_pair, "y", 2)
     parts = [ring(attend(k, place, queries[k], blocks), "y", 4 - k) for k in (1, 3, 2)]
     parts.append(attend(0, place, queries[0], blocks))
     merged = pl.pallas_call(

time: 94.3 us -> 97.7 us (1.036); the launches traced: 92.8 us -> 97.5 us
  waiting for transfers between devices: 31.7 us -> 36 us
  starting transfers between devices: 17.3 us -> 19.8 us
  blocking collectives: 16.6 us -> 14.5 us
    ppermute x10 -> x11, waiting for transfers between devices: 25.8 us -> 36 us  [ring(): lax.ppermute(value, axis, [(at, (at + steps) % size) for at in range(size)])]
    ppermute x1, waiting for transfers between devices: 5.91 us -> 0.01 us  [routed(): return lax.ppermute(value, ('xl', 'y'), pairs)]
    ppermute x10 -> x11, starting transfers between devices: 12.8 us -> 18.4 us  [ring(): lax.ppermute(value, axis, [(at, (at + steps) % size) for at in range(size)])]
    ppermute x1, starting transfers between devices: 4.57 us -> 1.39 us  [routed(): return lax.ppermute(value, ('xl', 'y'), pairs)]
    all_to_all x1, blocking collectives: 16.6 us -> 14.5 us  [on_device(): lax.all_to_all(merged, ('xh', 'core', 'xl'), split_axis=0, concat_axis=0,...]
  transfers between devices with their start and end apart: 11 -> 12, of which waited for: 7 -> 5; matrix products, arithmetic and copies ran while one was open for 0% -> 0% of each run, Pallas kernels for 25% -> 23%
where the time goes in v5:
time: 97.7 us; the launch traced here: 97.5 us
  waiting for transfers between devices  36 us (37%)
  Pallas kernels  25.8 us (26%)
  starting transfers between devices  19.8 us (20%)
  blocking collectives  14.5 us (15%)
  local copies, waits for them, and re-layouts  1.12 us (1%)
    ppermute x11, waiting for transfers between devices, ring(): lax.ppermute(value, axis, [(at, (at + steps) % size) for at in range(size)])  36 us
    pallas_call x4, Pallas kernels, attend(): pl.pallas_call(functools.partial(attend_kernel, step), out_shape=jax.Shap...  22.8 us
    ppermute x11, starting transfers between devices, ring(): lax.ppermute(value, axis, [(at, (at + steps) % size) for at in range(size)])  18.4 us
    all_to_all x1, blocking collectives, on_device(): lax.all_to_all(merged, ('xh', 'core', 'xl'), split_axis=0, concat_axis=0,...  14.5 us
  transfers between devices with their start and end apart: 12, of which 5 were waited for; matrix products, arithmetic and copies ran while one was open for 0% of the time, Pallas kernels for 23%

profile of v5, /device:TPU:1, one launch (start us, length us, event | category | flops | bytes accessed | tf_op | source)
XLA Modules:
  0.0 97.5 jit_solution(8644118013746002620)
XLA Ops:
  0.0 0.1 pad_add_fusion.place
  0.1 1.9 %pack.1 = (bf16[1024,128]{1,0:T(8,128)(2,1)S(1)}, bf16[1024,128]{1,0:T(8,128)(2,1)S(1)}, bf16[1024,128]{1,0:T(8,128)(2,1)S(1)}, bf16[1024,128]{1,0:T(8,128)(2,1)S(1)}) custom-call(s32[3]{0:T(128)S(1)} %pad_add_fusion.place, bf16[512,512]{1,0:T(8,128)(2,1)} %query_in.1, bf16[512,256]{1,0:T(8,128)(2,1)} %key_in.1, bf16[512,256]{1,0:T(8,128)(2,1)} %value_in.1), custom_call_target="tpu_custom_call" | custom-call | tf_op jit(solution)/shard_map/pack/pallas_call | solution.py:262
  1.9 3.6 %collective-permute-start.3 = (bf16[1024,128]{1,0:T(8,128)(2,1)S(1)}, bf16[1024,128]{1,0:T(8,128)(2,1)S(1)}, u32[]{:S(2)}, u32[]{:S(2)}) collective-permute-start(bf16[1024,128]{1,0:T(8,128)(2,1)S(1)} %get-tuple-element.11), channel_id=1, source_target_pairs={{0,48},{16,0},{32,16},{48,32},{1,49},{17,1},{33,17},{49,33},{2,50}... | collective-permute-start | bytes 786440 | tf_op jit(solution)/shard_map/ppermute | solution.py:246
  5.6 1.4 %collective-permute-start.2 = (bf16[1024,128]{1,0:T(8,128)(2,1)S(1)}, bf16[1024,128]{1,0:T(8,128)(2,1)S(1)}, u32[]{:S(2)}, u32[]{:S(2)}) collective-permute-start(bf16[1024,128]{1,0:T(8,128)(2,1)S(1)} %get-tuple-element.14), channel_id=1, source_target_pairs={{0,112},{16,96},{32,80},{48,64},{64,48},{80,32},{96,16},{112,0},{1... | collective-permute-start | bytes 786440 | tf_op jit(solution)/shard_map/ppermute | solution.py:255
  7.0 0.3 collective-permute-start
  7.2 8.9 %collective-permute-done.3 = bf16[1024,128]{1,0:T(8,128)(2,1)S(1)} collective-permute-done((bf16[1024,128]{1,0:T(8,128)(2,1)S(1)}, bf16[1024,128]{1,0:T(8,128)(2,1)S(1)}, u32[]{:S(2)}, u32[]{:S(2)}) %collective-permute-start.3) | collective-permute-done | bytes 262176 | tf_op jit(solution)/shard_map/ppermute | solution.py:246
  16.2 0.1 pad_maximum_fusion.1
  16.2 1.7 %collective-permute-start.4 = (bf16[2,1024,128]{2,1,0:T(8,128)(2,1)S(1)}, bf16[2,1024,128]{2,1,0:T(8,128)(2,1)S(1)}, u32[]{:S(2)}, u32[]{:S(2)}) collective-permute-start(bf16[2,1024,128]{2,1,0:T(8,128)(2,1)S(1)} %pad_maximum_fusion.1), channel_id=1, source_target_pairs={{0,4},{4,8},{8,12},{12,0},{1,5},{5,9},{9,13},{13,1},{2,6},{6,10},{... | collective-permute-start | bytes 1572872 | tf_op jit(solution)/shard_map/ppermute | solution.py:246
  17.9 2.2 %collective-permute-start.5 = (bf16[2,1024,128]{2,1,0:T(8,128)(2,1)S(1)}, bf16[2,1024,128]{2,1,0:T(8,128)(2,1)S(1)}, u32[]{:S(2)}, u32[]{:S(2)}) collective-permute-start(bf16[2,1024,128]{2,1,0:T(8,128)(2,1)S(1)} %pad_maximum_fusion.1), channel_id=1, source_target_pairs={{0,12},{4,0},{8,4},{12,8},{1,13},{5,1},{9,5},{13,9},{2,14},{6,2},{... | collective-permute-start | bytes 1572872 | tf_op jit(solution)/shard_map/ppermute | solution.py:246
  20.1 0.0 collective-permute-done
  20.1 3.4 %collective-permute-start.8 = (bf16[1024,128]{1,0:T(8,128)(2,1)S(1)}, bf16[1024,128]{1,0:T(8,128)(2,1)S(1)}, u32[]{:S(2)}, u32[]{:S(2)}) collective-permute-start(bf16[1024,128]{1,0:T(8,128)(2,1)S(1)} %collective-permute-done), channel_id=1, source_target_pairs={{0,48},{16,0},{32,16},{48,32},{1,49},{17,1},{33,17},{49,33},{2,50}... | collective-permute-start | bytes 786440 | tf_op jit(solution)/shard_map/ppermute | solution.py:246
  23.6 1.3 %collective-permute-start.6 = (bf16[2,1024,128]{2,1,0:T(8,128)(2,1)S(1)}, bf16[2,1024,128]{2,1,0:T(8,128)(2,1)S(1)}, u32[]{:S(2)}, u32[]{:S(2)}) collective-permute-start(bf16[2,1024,128]{2,1,0:T(8,128)(2,1)S(1)} %pad_maximum_fusion.1), channel_id=1, source_target_pairs={{0,8},{4,12},{8,0},{12,4},{1,9},{5,13},{9,1},{13,5},{2,10},{6,14},... | collective-permute-start | bytes 1572872 | tf_op jit(solution)/shard_map/ppermute | solution.py:246
  24.9 0.1 pad_maximum_fusion.q_ref
  24.9 0.1 collective-permute-start.10
  25.0 3.7 %collective-permute-done.8 = bf16[1024,128]{1,0:T(8,128)(2,1)S(1)} collective-permute-done((bf16[1024,128]{1,0:T(8,128)(2,1)S(1)}, bf16[1024,128]{1,0:T(8,128)(2,1)S(1)}, u32[]{:S(2)}, u32[]{:S(2)}) %collective-permute-start.8) | collective-permute-done | bytes 262176 | tf_op jit(solution)/shard_map/ppermute | solution.py:246
  28.7 0.0 collective-permute-start.1
  28.7 0.1 pad_maximum_fusion.2.q_ref
  28.8 1.8 %collective-permute-done.4 = bf16[2,1024,128]{2,1,0:T(8,128)(2,1)S(1)} collective-permute-done((bf16[2,1024,128]{2,1,0:T(8,128)(2,1)S(1)}, bf16[2,1024,128]{2,1,0:T(8,128)(2,1)S(1)}, u32[]{:S(2)}, u32[]{:S(2)}) %collective-permute-start.4) | collective-permute-done | bytes 524320 | tf_op jit(solution)/shard_map/ppermute | solution.py:246
  30.6 0.0 collective-permute-done.5
  30.7 12.0 %collective-permute-done.6 = bf16[2,1024,128]{2,1,0:T(8,128)(2,1)S(1)} collective-permute-done((bf16[2,1024,128]{2,1,0:T(8,128)(2,1)S(1)}, bf16[2,1024,128]{2,1,0:T(8,128)(2,1)S(1)}, u32[]{:S(2)}, u32[]{:S(2)}) %collective-permute-start.6) | collective-permute-done | bytes 524320 | tf_op jit(solution)/shard_map/ppermute | solution.py:246
  42.9 0.0 collective-permute-done.10.q_ref
  42.9 5.4 %attend2.1 = bf16[2,144,1024]{2,1,0:T(8,128)(2,1)S(1)} custom-call(s32[3]{0:T(128)S(1)} %pad_add_fusion.place, bf16[2,1024,128]{2,1,0:T(8,128)(2,1)S(1)} %collective-permute-done.10.q_ref, bf16[8,1024,128]{2,1,0:T(8,128)(2,1)S(1)} %slice_dynamic-update-slice_fusion.kv_ref), custom_call_target="tpu_custom_call" | custom-call | tf_op jit(solution)/shard_map/attend2/pallas_call | solution.py:199
  48.3 0.1 collective-permute-start.11
  48.4 5.5 %attend3.1 = bf16[2,144,1024]{2,1,0:T(8,128)(2,1)S(1)} custom-call(s32[3]{0:T(128)S(1)} %pad_add_fusion.place, bf16[2,1024,128]{2,1,0:T(8,128)(2,1)S(1)} %pad_maximum_fusion.2.q_ref, bf16[8,1024,128]{2,1,0:T(8,128)(2,1)S(1)} %slice_dynamic-update-slice_fusion.kv_ref), custom_call_target="tpu_custom_call" | custom-call | tf_op jit(solution)/shard_map/attend3/pallas_call | solution.py:199
  53.9 5.7 %collective-permute-start.9 = (bf16[2,144,1024]{2,1,0:T(8,128)(2,1)S(1)}, bf16[2,144,1024]{2,1,0:T(8,128)(2,1)S(1)}, u32[]{:S(2)}, u32[]{:S(2)}) collective-permute-start(bf16[2,144,1024]{2,1,0:T(8,128)(2,1)S(1)} %attend3.1), channel_id=1, source_target_pairs={{0,16},{16,32},{32,48},{48,0},{1,17},{17,33},{33,49},{49,1},{2,18}... | collective-permute-start | bytes 1769480 | tf_op jit(solution)/shard_map/ppermute | solution.py:246
  59.6 6.8 %attend1.1 = bf16[2,144,1024]{2,1,0:T(8,128)(2,1)S(1)} custom-call(s32[3]{0:T(128)S(1)} %pad_add_fusion.place, bf16[2,1024,128]{2,1,0:T(8,128)(2,1)S(1)} %collective-permute-done.1.q_ref, bf16[8,1024,128]{2,1,0:T(8,128)(2,1)S(1)} %slice_dynamic-update-slice_fusion.kv_ref), custom_call_target="tpu_custom_call" | custom-call | tf_op jit(solution)/shard_map/attend1/pallas_call | solution.py:199
  66.4 0.1 collective-permute-start.7
  66.5 5.0 %attend0.1.refs_3_ = bf16[2,144,1024]{2,1,0:T(8,128)(2,1)S(1)} custom-call(s32[3]{0:T(128)S(1)} %pad_add_fusion.place, bf16[2,1024,128]{2,1,0:T(8,128)(2,1)S(1)} %pad_maximum_fusion.q_ref, bf16[8,1024,128]{2,1,0:T(8,128)(2,1)S(1)} %slice_dynamic-update-slice_fusion.kv_ref), custom_call_target="tpu_custom_call" | custom-call | tf_op jit(solution)/shard_map/attend0/pallas_call | solution.py:199
  71.6 9.5 %collective-permute-done.9.refs_1_ = bf16[2,144,1024]{2,1,0:T(8,128)(2,1)S(1)} collective-permute-done((bf16[2,144,1024]{2,1,0:T(8,128)(2,1)S(1)}, bf16[2,144,1024]{2,1,0:T(8,128)(2,1)S(1)}, u32[]{:S(2)}, u32[]{:S(2)}) %collective-permute-start.9) | collective-permute-done | bytes 589856 | tf_op jit(solution)/shard_map/ppermute | solution.py:246
  81.0 1.1 %merge.1 = bf16[4,2,128,256]{3,2,1,0:T(8,128)(2,1)S(1)} custom-call(s32[3]{0:T(128)S(1)} %pad_add_fusion.place, bf16[2,144,1024]{2,1,0:T(8,128)(2,1)S(1)} %collective-permute-done.7.refs_0_, bf16[2,144,1024]{2,1,0:T(8,128)(2,1)S(1)} %collective-permute-done.9.refs_1_, bf16[2,144,1024]{2,1,0:T(8,128)(2,1)S(1)} %collective-permute-done.11.refs_2_, ...), custom_call_target="tpu_custom_call" | custom-call | tf_op jit(solution)/shard_map/merge/pallas_call | solution.py:293
  82.2 14.5 %all_to_all.5 = bf16[8,128,256]{2,1,0:T(8,128)(2,1)S(1)} all-to-all(bf16[8,128,256]{2,1,0:T(8,128)(2,1)S(1)} %bitcast.15), channel_id=1, replica_groups=mesh['xl'=2,'y'=4,'z'=4,'xh'=2,'core'=2] {'xh','core','xl'}, dimensions={0} | all-to-all | bytes 1048576 | tf_op jit(solution)/shard_map/all_to_all | solution.py:302
  96.7 0.8 copy.5
  (12 shorter events, 0.3 us)
Async XLA Ops:
  1.9 14.2 %collective-permute-start.3 = (bf16[1024,128]{1,0:T(8,128)(2,1)S(1)}, bf16[1024,128]{1,0:T(8,128)(2,1)S(1)}, u32[]{:S(2)}, u32[]{:S(2)}) collective-permute-start(bf16[1024,128]{1,0:T(8,128)(2,1)S(1)} %get-tuple-element.11), channel_id=1, source_target_pairs={{0,48},{16,0},{32,16},{48,32},{1,49},{17,1},{33,17},{49,33},{2,50}... | collective-permute-start | bytes 786440 | tf_op jit(solution)/shard_map/ppermute | solution.py:246
  5.6 10.6 %collective-permute-start.2 = (bf16[1024,128]{1,0:T(8,128)(2,1)S(1)}, bf16[1024,128]{1,0:T(8,128)(2,1)S(1)}, u32[]{:S(2)}, u32[]{:S(2)}) collective-permute-start(bf16[1024,128]{1,0:T(8,128)(2,1)S(1)} %get-tuple-element.14), channel_id=1, source_target_pairs={{0,112},{16,96},{32,80},{48,64},{64,48},{80,32},{96,16},{112,0},{1... | collective-permute-start | bytes 786440 | tf_op jit(solution)/shard_map/ppermute | solution.py:255
  7.0 13.2 %collective-permute-start = (bf16[1024,128]{1,0:T(8,128)(2,1)S(1)}, bf16[1024,128]{1,0:T(8,128)(2,1)S(1)}, u32[]{:S(2)}, u32[]{:S(2)}) collective-permute-start(bf16[1024,128]{1,0:T(8,128)(2,1)S(1)} %get-tuple-element.12), channel_id=1, source_target_pairs={{0,64},{64,0},{1,65},{65,1},{2,66},{66,2},{3,67},{67,3},{4,68},{68... | collective-permute-start | bytes 786440 | tf_op jit(solution)/shard_map/ppermute | solution.py:246
  16.2 14.4 %collective-permute-start.4 = (bf16[2,1024,128]{2,1,0:T(8,128)(2,1)S(1)}, bf16[2,1024,128]{2,1,0:T(8,128)(2,1)S(1)}, u32[]{:S(2)}, u32[]{:S(2)}) collective-permute-start(bf16[2,1024,128]{2,1,0:T(8,128)(2,1)S(1)} %pad_maximum_fusion.1), channel_id=1, source_target_pairs={{0,4},{4,8},{8,12},{12,0},{1,5},{5,9},{9,13},{13,1},{2,6},{6,10},{... | collective-permute-start | bytes 1572872 | tf_op jit(solution)/shard_map/ppermute | solution.py:246
  17.9 12.7 %collective-permute-start.5 = (bf16[2,1024,128]{2,1,0:T(8,128)(2,1)S(1)}, bf16[2,1024,128]{2,1,0:T(8,128)(2,1)S(1)}, u32[]{:S(2)}, u32[]{:S(2)}) collective-permute-start(bf16[2,1024,128]{2,1,0:T(8,128)(2,1)S(1)} %pad_maximum_fusion.1), channel_id=1, source_target_pairs={{0,12},{4,0},{8,4},{12,8},{1,13},{5,1},{9,5},{13,9},{2,14},{6,2},{... | collective-permute-start | bytes 1572872 | tf_op jit(solution)/shard_map/ppermute | solution.py:246
  20.1 8.6 %collective-permute-start.8 = (bf16[1024,128]{1,0:T(8,128)(2,1)S(1)}, bf16[1024,128]{1,0:T(8,128)(2,1)S(1)}, u32[]{:S(2)}, u32[]{:S(2)}) collective-permute-start(bf16[1024,128]{1,0:T(8,128)(2,1)S(1)} %collective-permute-done), channel_id=1, source_target_pairs={{0,48},{16,0},{32,16},{48,32},{1,49},{17,1},{33,17},{49,33},{2,50}... | collective-permute-start | bytes 786440 | tf_op jit(solution)/shard_map/ppermute | solution.py:246
  23.6 19.1 %collective-permute-start.6 = (bf16[2,1024,128]{2,1,0:T(8,128)(2,1)S(1)}, bf16[2,1024,128]{2,1,0:T(8,128)(2,1)S(1)}, u32[]{:S(2)}, u32[]{:S(2)}) collective-permute-start(bf16[2,1024,128]{2,1,0:T(8,128)(2,1)S(1)} %pad_maximum_fusion.1), channel_id=1, source_target_pairs={{0,8},{4,12},{8,0},{12,4},{1,9},{5,13},{9,1},{13,5},{2,10},{6,14},... | collective-permute-start | bytes 1572872 | tf_op jit(solution)/shard_map/ppermute | solution.py:246
  24.9 18.0 %collective-permute-start.10 = (bf16[2,1024,128]{2,1,0:T(8,128)(2,1)S(1)}, bf16[2,1024,128]{2,1,0:T(8,128)(2,1)S(1)}, u32[]{:S(2)}, u32[]{:S(2)}) collective-permute-start(bf16[2,1024,128]{2,1,0:T(8,128)(2,1)S(1)} %pad_maximum_fusion.q_ref), channel_id=1, source_target_pairs={{0,32},{16,48},{32,0},{48,16},{1,33},{17,49},{33,1},{49,17},{2,34}... | collective-permute-start | bytes 1572872 | tf_op jit(solution)/shard_map/ppermute | solution.py:246
  28.7 30.9 %collective-permute-start.1 = (bf16[2,1024,128]{2,1,0:T(8,128)(2,1)S(1)}, bf16[2,1024,128]{2,1,0:T(8,128)(2,1)S(1)}, u32[]{:S(2)}, u32[]{:S(2)}) collective-permute-start(bf16[2,1024,128]{2,1,0:T(8,128)(2,1)S(1)} %pad_maximum_fusion.q_ref), channel_id=1, source_target_pairs={{0,16},{16,32},{32,48},{48,0},{1,17},{17,33},{33,49},{49,1},{2,18}... | collective-permute-start | bytes 1572872 | tf_op jit(solution)/shard_map/ppermute | solution.py:246
  48.3 23.2 %collective-permute-start.11 = (bf16[2,144,1024]{2,1,0:T(8,128)(2,1)S(1)}, bf16[2,144,1024]{2,1,0:T(8,128)(2,1)S(1)}, u32[]{:S(2)}, u32[]{:S(2)}) collective-permute-start(bf16[2,144,1024]{2,1,0:T(8,128)(2,1)S(1)} %attend2.1), channel_id=1, source_target_pairs={{0,32},{16,48},{32,0},{48,16},{1,33},{17,49},{33,1},{49,17},{2,34}... | collective-permute-start | bytes 1769480 | tf_op jit(solution)/shard_map/ppermute | solution.py:246
  53.9 27.1 %collective-permute-start.9 = (bf16[2,144,1024]{2,1,0:T(8,128)(2,1)S(1)}, bf16[2,144,1024]{2,1,0:T(8,128)(2,1)S(1)}, u32[]{:S(2)}, u32[]{:S(2)}) collective-permute-start(bf16[2,144,1024]{2,1,0:T(8,128)(2,1)S(1)} %attend3.1), channel_id=1, source_target_pairs={{0,16},{16,32},{32,48},{48,0},{1,17},{17,33},{33,49},{49,1},{2,18}... | collective-permute-start | bytes 1769480 | tf_op jit(solution)/shard_map/ppermute | solution.py:246
  66.4 14.6 %collective-permute-start.7 = (bf16[2,144,1024]{2,1,0:T(8,128)(2,1)S(1)}, bf16[2,144,1024]{2,1,0:T(8,128)(2,1)S(1)}, u32[]{:S(2)}, u32[]{:S(2)}) collective-permute-start(bf16[2,144,1024]{2,1,0:T(8,128)(2,1)S(1)} %attend1.1), channel_id=1, source_target_pairs={{0,48},{16,0},{32,16},{48,32},{1,49},{17,1},{33,17},{49,33},{2,50}... | collective-permute-start | bytes 1769480 | tf_op jit(solution)/shard_map/ppermute | solution.py:246

commit v6 on v5

--- a/solution.py
+++ b/solution.py
@@ -276,7 +276,7 @@
     kv_mirror = routed(kv_other, lambda h, r: (1 - h, 3 - r))
     q_swap = ring(q_other, "xl", 1)
     q_early = ring(q_own, "y", 3)
-    kv_mirror, q_early = lax.optimization_barrier((kv_mirror, q_early))
+    q_swap, q_early = lax.optimization_barrier((q_swap, q_early))
     kv_pair = jnp.stack([kv_own, kv_mirror])
     pairs = {0: kv_pair}
     pairs |= {k: ring(kv_pair, "z", k) for k in (2, 3, 1)}

time: 97.7 us -> 94.9 us (0.971)
  waiting for transfers between devices: 36 us -> 33 us
  blocking collectives: 14.5 us -> 13.3 us
    ppermute x11, waiting for transfers between devices: 36 us -> 27.5 us  [ring(): lax.ppermute(value, axis, [(at, (at + steps) % size) for at in range(size)])]
    ppermute x1, waiting for transfers between devices: 0.01 us -> 5.54 us  [routed(): return lax.ppermute(value, ('xl', 'y'), pairs)]
    ppermute x1, starting transfers between devices: 1.39 us -> 4.57 us  [routed(): return lax.ppermute(value, ('xl', 'y'), pairs)]
    ppermute x11, starting transfers between devices: 18.4 us -> 16.1 us  [ring(): lax.ppermute(value, axis, [(at, (at + steps) % size) for at in range(size)])]
    all_to_all x1, blocking collectives: 14.5 us -> 13.3 us  [on_device(): lax.all_to_all(merged, ('xh', 'core', 'xl'), split_axis=0, concat_axis=0,...]
  transfers between devices with their start and end apart: 12 -> 12, of which waited for: 5 -> 6; matrix products, arithmetic and copies ran while one was open for 0% -> 0% of each run, Pallas kernels for 23% -> 24%
where the time goes in v6:
time: 94.9 us; the launch traced here: 94.2 us
  waiting for transfers between devices  33 us (35%)
  Pallas kernels  25.8 us (27%)
  starting transfers between devices  20.7 us (22%)
  blocking collectives  13.3 us (14%)
  local copies, waits for them, and re-layouts  1.12 us (1%)
    ppermute x11, waiting for transfers between devices, ring(): lax.ppermute(value, axis, [(at, (at + steps) % size) for at in range(size)])  27.5 us
    pallas_call x4, Pallas kernels, attend(): pl.pallas_call(functools.partial(attend_kernel, step), out_shape=jax.Shap...  22.8 us
    ppermute x11, starting transfers between devices, ring(): lax.ppermute(value, axis, [(at, (at + steps) % size) for at in range(size)])  16.1 us
    all_to_all x1, blocking collectives, on_device(): lax.all_to_all(merged, ('xh', 'core', 'xl'), split_axis=0, concat_axis=0,...  13.3 us
    ppermute x1, waiting for transfers between devices, routed(): return lax.ppermute(value, ('xl', 'y'), pairs)  5.54 us
    ppermute x1, starting transfers between devices, routed(): return lax.ppermute(value, ('xl', 'y'), pairs)  4.57 us
  transfers between devices with their start and end apart: 12, of which 6 were waited for; matrix products, arithmetic and copies ran while one was open for 0% of the time, Pallas kernels for 24%

profile of v6, /device:TPU:1, one launch (start us, length us, event | category | flops | bytes accessed | tf_op | source)
XLA Modules:
  0.0 94.2 jit_solution(9235923062629640505)
XLA Ops:
  0.0 0.1 pad_add_fusion.place
  0.1 1.9 %pack.1 = (bf16[1024,128]{1,0:T(8,128)(2,1)S(1)}, bf16[1024,128]{1,0:T(8,128)(2,1)S(1)}, bf16[1024,128]{1,0:T(8,128)(2,1)S(1)}, bf16[1024,128]{1,0:T(8,128)(2,1)S(1)}) custom-call(s32[3]{0:T(128)S(1)} %pad_add_fusion.place, bf16[512,512]{1,0:T(8,128)(2,1)} %query_in.1, bf16[512,256]{1,0:T(8,128)(2,1)} %key_in.1, bf16[512,256]{1,0:T(8,128)(2,1)} %value_in.1), custom_call_target="tpu_custom_call" | custom-call | tf_op jit(solution)/shard_map/pack/pallas_call | solution.py:262
  1.9 4.6 %collective-permute-start.3 = (bf16[1024,128]{1,0:T(8,128)(2,1)S(1)}, bf16[1024,128]{1,0:T(8,128)(2,1)S(1)}, u32[]{:S(2)}, u32[]{:S(2)}) collective-permute-start(bf16[1024,128]{1,0:T(8,128)(2,1)S(1)} %get-tuple-element.15), channel_id=1, source_target_pairs={{0,112},{16,96},{32,80},{48,64},{64,48},{80,32},{96,16},{112,0},{1... | collective-permute-start | bytes 786440 | tf_op jit(solution)/shard_map/ppermute | solution.py:255
  6.5 0.0 collective-permute-start.1
  6.5 0.4 collective-permute-start
  6.9 5.5 %collective-permute-done.3 = bf16[1024,128]{1,0:T(8,128)(2,1)S(1)} collective-permute-done((bf16[1024,128]{1,0:T(8,128)(2,1)S(1)}, bf16[1024,128]{1,0:T(8,128)(2,1)S(1)}, u32[]{:S(2)}, u32[]{:S(2)}) %collective-permute-start.3) | collective-permute-done | bytes 262176 | tf_op jit(solution)/shard_map/ppermute | solution.py:255
  12.4 0.1 pad_maximum_fusion.1
  12.5 1.6 %collective-permute-start.4 = (bf16[2,1024,128]{2,1,0:T(8,128)(2,1)S(1)}, bf16[2,1024,128]{2,1,0:T(8,128)(2,1)S(1)}, u32[]{:S(2)}, u32[]{:S(2)}) collective-permute-start(bf16[2,1024,128]{2,1,0:T(8,128)(2,1)S(1)} %pad_maximum_fusion.1), channel_id=1, source_target_pairs={{0,4},{4,8},{8,12},{12,0},{1,5},{5,9},{9,13},{13,1},{2,6},{6,10},{... | collective-permute-start | bytes 1572872 | tf_op jit(solution)/shard_map/ppermute | solution.py:246
  14.1 2.2 %collective-permute-start.5 = (bf16[2,1024,128]{2,1,0:T(8,128)(2,1)S(1)}, bf16[2,1024,128]{2,1,0:T(8,128)(2,1)S(1)}, u32[]{:S(2)}, u32[]{:S(2)}) collective-permute-start(bf16[2,1024,128]{2,1,0:T(8,128)(2,1)S(1)} %pad_maximum_fusion.1), channel_id=1, source_target_pairs={{0,12},{4,0},{8,4},{12,8},{1,13},{5,1},{9,5},{13,9},{2,14},{6,2},{... | collective-permute-start | bytes 1572872 | tf_op jit(solution)/shard_map/ppermute | solution.py:246
  16.3 1.8 %collective-permute-done.1 = bf16[1024,128]{1,0:T(8,128)(2,1)S(1)} collective-permute-done((bf16[1024,128]{1,0:T(8,128)(2,1)S(1)}, bf16[1024,128]{1,0:T(8,128)(2,1)S(1)}, u32[]{:S(2)}, u32[]{:S(2)}) %collective-permute-start.1) | collective-permute-done | bytes 262176 | tf_op jit(solution)/shard_map/ppermute | solution.py:246
  18.1 0.0 collective-permute-done
  18.1 3.4 %collective-permute-start.8 = (bf16[1024,128]{1,0:T(8,128)(2,1)S(1)}, bf16[1024,128]{1,0:T(8,128)(2,1)S(1)}, u32[]{:S(2)}, u32[]{:S(2)}) collective-permute-start(bf16[1024,128]{1,0:T(8,128)(2,1)S(1)} %collective-permute-done), channel_id=1, source_target_pairs={{0,48},{16,0},{32,16},{48,32},{1,49},{17,1},{33,17},{49,33},{2,50}... | collective-permute-start | bytes 786440 | tf_op jit(solution)/shard_map/ppermute | solution.py:246
  21.6 3.7 %collective-permute-start.6 = (bf16[2,1024,128]{2,1,0:T(8,128)(2,1)S(1)}, bf16[2,1024,128]{2,1,0:T(8,128)(2,1)S(1)}, u32[]{:S(2)}, u32[]{:S(2)}) collective-permute-start(bf16[2,1024,128]{2,1,0:T(8,128)(2,1)S(1)} %pad_maximum_fusion.1), channel_id=1, source_target_pairs={{0,8},{4,12},{8,0},{12,4},{1,9},{5,13},{9,1},{13,5},{2,10},{6,14},... | collective-permute-start | bytes 1572872 | tf_op jit(solution)/shard_map/ppermute | solution.py:246
  25.2 0.1 pad_maximum_fusion.q_ref
  25.3 0.1 collective-permute-start.10
  25.4 12.4 %collective-permute-done.8 = bf16[1024,128]{1,0:T(8,128)(2,1)S(1)} collective-permute-done((bf16[1024,128]{1,0:T(8,128)(2,1)S(1)}, bf16[1024,128]{1,0:T(8,128)(2,1)S(1)}, u32[]{:S(2)}, u32[]{:S(2)}) %collective-permute-start.8) | collective-permute-done | bytes 262176 | tf_op jit(solution)/shard_map/ppermute | solution.py:246
  37.8 0.1 pad_maximum_fusion.2.q_ref
  38.0 0.1 collective-permute-done.6
  38.3 0.9 %collective-permute-done.10.q_ref = bf16[2,1024,128]{2,1,0:T(8,128)(2,1)S(1)} collective-permute-done((bf16[2,1024,128]{2,1,0:T(8,128)(2,1)S(1)}, bf16[2,1024,128]{2,1,0:T(8,128)(2,1)S(1)}, u32[]{:S(2)}, u32[]{:S(2)}) %collective-permute-start.10) | collective-permute-done | bytes 524320 | tf_op jit(solution)/shard_map/ppermute | solution.py:246
  39.2 5.4 %attend2.1 = bf16[2,144,1024]{2,1,0:T(8,128)(2,1)S(1)} custom-call(s32[3]{0:T(128)S(1)} %pad_add_fusion.place, bf16[2,1024,128]{2,1,0:T(8,128)(2,1)S(1)} %collective-permute-done.10.q_ref, bf16[8,1024,128]{2,1,0:T(8,128)(2,1)S(1)} %slice_dynamic-update-slice_fusion.kv_ref), custom_call_target="tpu_custom_call" | custom-call | tf_op jit(solution)/shard_map/attend2/pallas_call | solution.py:199
  44.6 1.6 %collective-permute-start.11 = (bf16[2,144,1024]{2,1,0:T(8,128)(2,1)S(1)}, bf16[2,144,1024]{2,1,0:T(8,128)(2,1)S(1)}, u32[]{:S(2)}, u32[]{:S(2)}) collective-permute-start(bf16[2,144,1024]{2,1,0:T(8,128)(2,1)S(1)} %attend2.1), channel_id=1, source_target_pairs={{0,32},{16,48},{32,0},{48,16},{1,33},{17,49},{33,1},{49,17},{2,34}... | collective-permute-start | bytes 1769480 | tf_op jit(solution)/shard_map/ppermute | solution.py:246
  46.2 5.5 %attend3.1 = bf16[2,144,1024]{2,1,0:T(8,128)(2,1)S(1)} custom-call(s32[3]{0:T(128)S(1)} %pad_add_fusion.place, bf16[2,1024,128]{2,1,0:T(8,128)(2,1)S(1)} %pad_maximum_fusion.2.q_ref, bf16[8,1024,128]{2,1,0:T(8,128)(2,1)S(1)} %slice_dynamic-update-slice_fusion.kv_ref), custom_call_target="tpu_custom_call" | custom-call | tf_op jit(solution)/shard_map/attend3/pallas_call | solution.py:199
  51.7 3.1 %collective-permute-start.9 = (bf16[2,144,1024]{2,1,0:T(8,128)(2,1)S(1)}, bf16[2,144,1024]{2,1,0:T(8,128)(2,1)S(1)}, u32[]{:S(2)}, u32[]{:S(2)}) collective-permute-start(bf16[2,144,1024]{2,1,0:T(8,128)(2,1)S(1)} %attend3.1), channel_id=1, source_target_pairs={{0,16},{16,32},{32,48},{48,0},{1,17},{17,33},{33,49},{49,1},{2,18}... | collective-permute-start | bytes 1769480 | tf_op jit(solution)/shard_map/ppermute | solution.py:246
  54.9 0.0 collective-permute-done.2.q_ref
  54.9 6.8 %attend1.1 = bf16[2,144,1024]{2,1,0:T(8,128)(2,1)S(1)} custom-call(s32[3]{0:T(128)S(1)} %pad_add_fusion.place, bf16[2,1024,128]{2,1,0:T(8,128)(2,1)S(1)} %collective-permute-done.2.q_ref, bf16[8,1024,128]{2,1,0:T(8,128)(2,1)S(1)} %slice_dynamic-update-slice_fusion.kv_ref), custom_call_target="tpu_custom_call" | custom-call | tf_op jit(solution)/shard_map/attend1/pallas_call | solution.py:199
  61.7 0.1 collective-permute-start.7
  61.8 5.0 %attend0.1.refs_3_ = bf16[2,144,1024]{2,1,0:T(8,128)(2,1)S(1)} custom-call(s32[3]{0:T(128)S(1)} %pad_add_fusion.place, bf16[2,1024,128]{2,1,0:T(8,128)(2,1)S(1)} %pad_maximum_fusion.q_ref, bf16[8,1024,128]{2,1,0:T(8,128)(2,1)S(1)} %slice_dynamic-update-slice_fusion.kv_ref), custom_call_target="tpu_custom_call" | custom-call | tf_op jit(solution)/shard_map/attend0/pallas_call | solution.py:199
  66.8 12.1 %collective-permute-done.9.refs_1_ = bf16[2,144,1024]{2,1,0:T(8,128)(2,1)S(1)} collective-permute-done((bf16[2,144,1024]{2,1,0:T(8,128)(2,1)S(1)}, bf16[2,144,1024]{2,1,0:T(8,128)(2,1)S(1)}, u32[]{:S(2)}, u32[]{:S(2)}) %collective-permute-start.9) | collective-permute-done | bytes 589856 | tf_op jit(solution)/shard_map/ppermute | solution.py:246
  79.0 0.0 collective-permute-done.7.refs_0_
  79.0 1.1 %merge.1 = bf16[4,2,128,256]{3,2,1,0:T(8,128)(2,1)S(1)} custom-call(s32[3]{0:T(128)S(1)} %pad_add_fusion.place, bf16[2,144,1024]{2,1,0:T(8,128)(2,1)S(1)} %collective-permute-done.7.refs_0_, bf16[2,144,1024]{2,1,0:T(8,128)(2,1)S(1)} %collective-permute-done.9.refs_1_, bf16[2,144,1024]{2,1,0:T(8,128)(2,1)S(1)} %collective-permute-done.11.refs_2_, ...), custom_call_target="tpu_custom_call" | custom-call | tf_op jit(solution)/shard_map/merge/pallas_call | solution.py:293
  80.1 13.3 %all_to_all.5 = bf16[8,128,256]{2,1,0:T(8,128)(2,1)S(1)} all-to-all(bf16[8,128,256]{2,1,0:T(8,128)(2,1)S(1)} %bitcast.15), channel_id=1, replica_groups=mesh['xl'=2,'y'=4,'z'=4,'xh'=2,'core'=2] {'xh','core','xl'}, dimensions={0} | all-to-all | bytes 1048576 | tf_op jit(solution)/shard_map/all_to_all | solution.py:302
  93.4 0.8 copy.5
  (12 shorter events, 0.3 us)
Async XLA Ops:
  1.9 10.5 %collective-permute-start.3 = (bf16[1024,128]{1,0:T(8,128)(2,1)S(1)}, bf16[1024,128]{1,0:T(8,128)(2,1)S(1)}, u32[]{:S(2)}, u32[]{:S(2)}) collective-permute-start(bf16[1024,128]{1,0:T(8,128)(2,1)S(1)} %get-tuple-element.15), channel_id=1, source_target_pairs={{0,112},{16,96},{32,80},{48,64},{64,48},{80,32},{96,16},{112,0},{1... | collective-permute-start | bytes 786440 | tf_op jit(solution)/shard_map/ppermute | solution.py:255
  6.5 11.6 %collective-permute-start.1 = (bf16[1024,128]{1,0:T(8,128)(2,1)S(1)}, bf16[1024,128]{1,0:T(8,128)(2,1)S(1)}, u32[]{:S(2)}, u32[]{:S(2)}) collective-permute-start(bf16[1024,128]{1,0:T(8,128)(2,1)S(1)} %get-tuple-element.11), channel_id=1, source_target_pairs={{0,48},{16,0},{32,16},{48,32},{1,49},{17,1},{33,17},{49,33},{2,50}... | collective-permute-start | bytes 786440 | tf_op jit(solution)/shard_map/ppermute | solution.py:246
  6.5 11.6 %collective-permute-start = (bf16[1024,128]{1,0:T(8,128)(2,1)S(1)}, bf16[1024,128]{1,0:T(8,128)(2,1)S(1)}, u32[]{:S(2)}, u32[]{:S(2)}) collective-permute-start(bf16[1024,128]{1,0:T(8,128)(2,1)S(1)} %get-tuple-element.12), channel_id=1, source_target_pairs={{0,64},{64,0},{1,65},{65,1},{2,66},{66,2},{3,67},{67,3},{4,68},{68... | collective-permute-start | bytes 786440 | tf_op jit(solution)/shard_map/ppermute | solution.py:246
  12.5 25.4 %collective-permute-start.4 = (bf16[2,1024,128]{2,1,0:T(8,128)(2,1)S(1)}, bf16[2,1024,128]{2,1,0:T(8,128)(2,1)S(1)}, u32[]{:S(2)}, u32[]{:S(2)}) collective-permute-start(bf16[2,1024,128]{2,1,0:T(8,128)(2,1)S(1)} %pad_maximum_fusion.1), channel_id=1, source_target_pairs={{0,4},{4,8},{8,12},{12,0},{1,5},{5,9},{9,13},{13,1},{2,6},{6,10},{... | collective-permute-start | bytes 1572872 | tf_op jit(solution)/shard_map/ppermute | solution.py:246
  14.1 23.8 %collective-permute-start.5 = (bf16[2,1024,128]{2,1,0:T(8,128)(2,1)S(1)}, bf16[2,1024,128]{2,1,0:T(8,128)(2,1)S(1)}, u32[]{:S(2)}, u32[]{:S(2)}) collective-permute-start(bf16[2,1024,128]{2,1,0:T(8,128)(2,1)S(1)} %pad_maximum_fusion.1), channel_id=1, source_target_pairs={{0,12},{4,0},{8,4},{12,8},{1,13},{5,1},{9,5},{13,9},{2,14},{6,2},{... | collective-permute-start | bytes 1572872 | tf_op jit(solution)/shard_map/ppermute | solution.py:246
  18.1 19.7 %collective-permute-start.8 = (bf16[1024,128]{1,0:T(8,128)(2,1)S(1)}, bf16[1024,128]{1,0:T(8,128)(2,1)S(1)}, u32[]{:S(2)}, u32[]{:S(2)}) collective-permute-start(bf16[1024,128]{1,0:T(8,128)(2,1)S(1)} %collective-permute-done), channel_id=1, source_target_pairs={{0,48},{16,0},{32,16},{48,32},{1,49},{17,1},{33,17},{49,33},{2,50}... | collective-permute-start | bytes 786440 | tf_op jit(solution)/shard_map/ppermute | solution.py:246
  21.6 16.5 %collective-permute-start.6 = (bf16[2,1024,128]{2,1,0:T(8,128)(2,1)S(1)}, bf16[2,1024,128]{2,1,0:T(8,128)(2,1)S(1)}, u32[]{:S(2)}, u32[]{:S(2)}) collective-permute-start(bf16[2,1024,128]{2,1,0:T(8,128)(2,1)S(1)} %pad_maximum_fusion.1), channel_id=1, source_target_pairs={{0,8},{4,12},{8,0},{12,4},{1,9},{5,13},{9,1},{13,5},{2,10},{6,14},... | collective-permute-start | bytes 1572872 | tf_op jit(solution)/shard_map/ppermute | solution.py:246
  25.3 13.9 %collective-permute-start.10 = (bf16[2,1024,128]{2,1,0:T(8,128)(2,1)S(1)}, bf16[2,1024,128]{2,1,0:T(8,128)(2,1)S(1)}, u32[]{:S(2)}, u32[]{:S(2)}) collective-permute-start(bf16[2,1024,128]{2,1,0:T(8,128)(2,1)S(1)} %pad_maximum_fusion.q_ref), channel_id=1, source_target_pairs={{0,32},{16,48},{32,0},{48,16},{1,33},{17,49},{33,1},{49,17},{2,34}... | collective-permute-start | bytes 1572872 | tf_op jit(solution)/shard_map/ppermute | solution.py:246
  37.8 17.0 %collective-permute-start.2 = (bf16[2,1024,128]{2,1,0:T(8,128)(2,1)S(1)}, bf16[2,1024,128]{2,1,0:T(8,128)(2,1)S(1)}, u32[]{:S(2)}, u32[]{:S(2)}) collective-permute-start(bf16[2,1024,128]{2,1,0:T(8,128)(2,1)S(1)} %pad_maximum_fusion.q_ref), channel_id=1, source_target_pairs={{0,16},{16,32},{32,48},{48,0},{1,17},{17,33},{33,49},{49,1},{2,18}... | collective-permute-start | bytes 1572872 | tf_op jit(solution)/shard_map/ppermute | solution.py:246
  44.6 22.2 %collective-permute-start.11 = (bf16[2,144,1024]{2,1,0:T(8,128)(2,1)S(1)}, bf16[2,144,1024]{2,1,0:T(8,128)(2,1)S(1)}, u32[]{:S(2)}, u32[]{:S(2)}) collective-permute-start(bf16[2,144,1024]{2,1,0:T(8,128)(2,1)S(1)} %attend2.1), channel_id=1, source_target_pairs={{0,32},{16,48},{32,0},{48,16},{1,33},{17,49},{33,1},{49,17},{2,34}... | collective-permute-start | bytes 1769480 | tf_op jit(solution)/shard_map/ppermute | solution.py:246
  51.7 27.2 %collective-permute-start.9 = (bf16[2,144,1024]{2,1,0:T(8,128)(2,1)S(1)}, bf16[2,144,1024]{2,1,0:T(8,128)(2,1)S(1)}, u32[]{:S(2)}, u32[]{:S(2)}) collective-permute-start(bf16[2,144,1024]{2,1,0:T(8,128)(2,1)S(1)} %attend3.1), channel_id=1, source_target_pairs={{0,16},{16,32},{32,48},{48,0},{1,17},{17,33},{33,49},{49,1},{2,18}... | collective-permute-start | bytes 1769480 | tf_op jit(solution)/shard_map/ppermute | solution.py:246
  61.7 17.3 %collective-permute-start.7 = (bf16[2,144,1024]{2,1,0:T(8,128)(2,1)S(1)}, bf16[2,144,1024]{2,1,0:T(8,128)(2,1)S(1)}, u32[]{:S(2)}, u32[]{:S(2)}) collective-permute-start(bf16[2,144,1024]{2,1,0:T(8,128)(2,1)S(1)} %attend1.1), channel_id=1, source_target_pairs={{0,48},{16,0},{32,16},{48,32},{1,49},{17,1},{33,17},{49,33},{2,50}... | collective-permute-start | bytes 1769480 | tf_op jit(solution)/shard_map/ppermute | solution.py:246

commit v7 on v4

--- a/solution.py
+++ b/solution.py
@@ -275,6 +275,8 @@
     )(place, pinned(query_rows), pinned(key_rows), pinned(value_rows))
     kv_mirror = routed(kv_other, lambda h, r: (1 - h, 3 - r))
     q_swap = ring(q_other, "xl", 1)
+    q_early = ring(q_own, "y", 1)
+    q_swap, q_early = lax.optimization_barrier((q_swap, q_early))
     kv_pair = jnp.stack([kv_own, kv_mirror])
     pairs = {0: kv_pair}
     pairs |= {k: ring(kv_pair, "z", k) for k in (2, 3, 1)}
@@ -283,7 +285,9 @@
     )
     q_pair = jnp.stack([q_own, q_swap])
     queries = {0: q_pair}
-    queries |= {k: ring(q_pair, "y", k) for k in (3, 1, 2)}
+    queries[3] = ring(q_pair, "y", 3)
+    queries[1] = jnp.stack([q_early, ring(q_swap, "y", 1)])
+    queries[2] = ring(q_pair, "y", 2)
     parts = [ring(attend(k, place, queries[k], blocks), "y", 4 - k) for k in (3, 1, 2)]
     parts.append(attend(0, place, queries[0], blocks))
     merged = pl.pallas_call(

time: 95.6 us -> 93 us (0.973)
  the two profiles are of different devices: /device:TPU:72 before, /device:TPU:1 now
where the time goes in v7:
time: 93 us; the launch traced here: 91.3 us
  waiting for transfers between devices  31.5 us (34%)
  Pallas kernels  25.8 us (28%)
  starting transfers between devices  17.2 us (18%)
  blocking collectives  15.4 us (17%)
  local copies, waits for them, and re-layouts  1.12 us (1%)
    ppermute x11, waiting for transfers between devices, ring(): lax.ppermute(value, axis, [(at, (at + steps) % size) for at in range(size)])  25.8 us
    pallas_call x4, Pallas kernels, attend(): pl.pallas_call(functools.partial(attend_kernel, step), out_shape=jax.Shap...  22.8 us
    all_to_all x1, blocking collectives, on_device(): lax.all_to_all(merged, ('xh', 'core', 'xl'), split_axis=0, concat_axis=0,...  15.4 us
    ppermute x11, starting transfers between devices, ring(): lax.ppermute(value, axis, [(at, (at + steps) % size) for at in range(size)])  12.6 us
    ppermute x1, waiting for transfers between devices, routed(): return lax.ppermute(value, ('xl', 'y'), pairs)  5.7 us
    ppermute x1, starting transfers between devices, routed(): return lax.ppermute(value, ('xl', 'y'), pairs)  4.57 us
    pallas_call x1, Pallas kernels, on_device(): pl.pallas_call(pack_kernel, out_shape=(message,) * 4, in_specs=[smem()] +...  1.86 us
  transfers between devices with their start and end apart: 12, of which 5 were waited for; matrix products, arithmetic and copies ran while one was open for 0% of the time, Pallas kernels for 25%

profile of v7, /device:TPU:1, one launch (start us, length us, event | category | flops | bytes accessed | tf_op | source)
XLA Modules:
  0.0 91.3 jit_solution(18300982145009543295)
XLA Ops:
  0.0 0.1 pad_add_fusion.place
  0.1 1.9 %pack.1 = (bf16[1024,128]{1,0:T(8,128)(2,1)S(1)}, bf16[1024,128]{1,0:T(8,128)(2,1)S(1)}, bf16[1024,128]{1,0:T(8,128)(2,1)S(1)}, bf16[1024,128]{1,0:T(8,128)(2,1)S(1)}) custom-call(s32[3]{0:T(128)S(1)} %pad_add_fusion.place, bf16[512,512]{1,0:T(8,128)(2,1)} %query_in.1, bf16[512,256]{1,0:T(8,128)(2,1)} %key_in.1, bf16[512,256]{1,0:T(8,128)(2,1)} %value_in.1), custom_call_target="tpu_custom_call" | custom-call | tf_op jit(solution)/shard_map/pack/pallas_call | solution.py:262
  1.9 4.6 %collective-permute-start.3 = (bf16[1024,128]{1,0:T(8,128)(2,1)S(1)}, bf16[1024,128]{1,0:T(8,128)(2,1)S(1)}, u32[]{:S(2)}, u32[]{:S(2)}) collective-permute-start(bf16[1024,128]{1,0:T(8,128)(2,1)S(1)} %get-tuple-element.15), channel_id=1, source_target_pairs={{0,112},{16,96},{32,80},{48,64},{64,48},{80,32},{96,16},{112,0},{1... | collective-permute-start | bytes 786440 | tf_op jit(solution)/shard_map/ppermute | solution.py:255
  6.5 0.0 collective-permute-start.1
  6.5 0.3 collective-permute-start
  6.8 5.7 %collective-permute-done.3 = bf16[1024,128]{1,0:T(8,128)(2,1)S(1)} collective-permute-done((bf16[1024,128]{1,0:T(8,128)(2,1)S(1)}, bf16[1024,128]{1,0:T(8,128)(2,1)S(1)}, u32[]{:S(2)}, u32[]{:S(2)}) %collective-permute-start.3) | collective-permute-done | bytes 262176 | tf_op jit(solution)/shard_map/ppermute | solution.py:255
  12.5 0.1 pad_maximum_fusion.1
  12.5 1.6 %collective-permute-start.4 = (bf16[2,1024,128]{2,1,0:T(8,128)(2,1)S(1)}, bf16[2,1024,128]{2,1,0:T(8,128)(2,1)S(1)}, u32[]{:S(2)}, u32[]{:S(2)}) collective-permute-start(bf16[2,1024,128]{2,1,0:T(8,128)(2,1)S(1)} %pad_maximum_fusion.1), channel_id=1, source_target_pairs={{0,4},{4,8},{8,12},{12,0},{1,5},{5,9},{9,13},{13,1},{2,6},{6,10},{... | collective-permute-start | bytes 1572872 | tf_op jit(solution)/shard_map/ppermute | solution.py:246
  14.1 2.2 %collective-permute-start.5 = (bf16[2,1024,128]{2,1,0:T(8,128)(2,1)S(1)}, bf16[2,1024,128]{2,1,0:T(8,128)(2,1)S(1)}, u32[]{:S(2)}, u32[]{:S(2)}) collective-permute-start(bf16[2,1024,128]{2,1,0:T(8,128)(2,1)S(1)} %pad_maximum_fusion.1), channel_id=1, source_target_pairs={{0,12},{4,0},{8,4},{12,8},{1,13},{5,1},{9,5},{13,9},{2,14},{6,2},{... | collective-permute-start | bytes 1572872 | tf_op jit(solution)/shard_map/ppermute | solution.py:246
  16.3 2.6 %collective-permute-done.1 = bf16[1024,128]{1,0:T(8,128)(2,1)S(1)} collective-permute-done((bf16[1024,128]{1,0:T(8,128)(2,1)S(1)}, bf16[1024,128]{1,0:T(8,128)(2,1)S(1)}, u32[]{:S(2)}, u32[]{:S(2)}) %collective-permute-start.1) | collective-permute-done | bytes 262176 | tf_op jit(solution)/shard_map/ppermute | solution.py:246
  18.9 0.0 collective-permute-start.8
  18.9 3.7 %collective-permute-start.6 = (bf16[2,1024,128]{2,1,0:T(8,128)(2,1)S(1)}, bf16[2,1024,128]{2,1,0:T(8,128)(2,1)S(1)}, u32[]{:S(2)}, u32[]{:S(2)}) collective-permute-start(bf16[2,1024,128]{2,1,0:T(8,128)(2,1)S(1)} %pad_maximum_fusion.1), channel_id=1, source_target_pairs={{0,8},{4,12},{8,0},{12,4},{1,9},{5,13},{9,1},{13,5},{2,10},{6,14},... | collective-permute-start | bytes 1572872 | tf_op jit(solution)/shard_map/ppermute | solution.py:246
  22.6 0.1 pad_maximum_fusion.q_ref
  22.7 1.7 %collective-permute-start.10 = (bf16[2,1024,128]{2,1,0:T(8,128)(2,1)S(1)}, bf16[2,1024,128]{2,1,0:T(8,128)(2,1)S(1)}, u32[]{:S(2)}, u32[]{:S(2)}) collective-permute-start(bf16[2,1024,128]{2,1,0:T(8,128)(2,1)S(1)} %pad_maximum_fusion.q_ref), channel_id=1, source_target_pairs={{0,32},{16,48},{32,0},{48,16},{1,33},{17,49},{33,1},{49,17},{2,34}... | collective-permute-start | bytes 1572872 | tf_op jit(solution)/shard_map/ppermute | solution.py:246
  24.4 3.0 %collective-permute-done.8 = bf16[1024,128]{1,0:T(8,128)(2,1)S(1)} collective-permute-done((bf16[1024,128]{1,0:T(8,128)(2,1)S(1)}, bf16[1024,128]{1,0:T(8,128)(2,1)S(1)}, u32[]{:S(2)}, u32[]{:S(2)}) %collective-permute-start.8) | collective-permute-done | bytes 262176 | tf_op jit(solution)/shard_map/ppermute | solution.py:246
  27.4 0.0 collective-permute-start.2
  27.4 0.1 pad_maximum_fusion.2.q_ref
  27.5 0.0 collective-permute-done.4
  27.5 0.0 collective-permute-done.5
  27.6 10.6 %collective-permute-done.6 = bf16[2,1024,128]{2,1,0:T(8,128)(2,1)S(1)} collective-permute-done((bf16[2,1024,128]{2,1,0:T(8,128)(2,1)S(1)}, bf16[2,1024,128]{2,1,0:T(8,128)(2,1)S(1)}, u32[]{:S(2)}, u32[]{:S(2)}) %collective-permute-start.6) | collective-permute-done | bytes 524320 | tf_op jit(solution)/shard_map/ppermute | solution.py:246
  38.4 5.4 %attend2.1 = bf16[2,144,1024]{2,1,0:T(8,128)(2,1)S(1)} custom-call(s32[3]{0:T(128)S(1)} %pad_add_fusion.place, bf16[2,1024,128]{2,1,0:T(8,128)(2,1)S(1)} %collective-permute-done.10.q_ref, bf16[8,1024,128]{2,1,0:T(8,128)(2,1)S(1)} %slice_dynamic-update-slice_fusion.kv_ref), custom_call_target="tpu_custom_call" | custom-call | tf_op jit(solution)/shard_map/attend2/pallas_call | solution.py:199
  43.7 0.1 collective-permute-start.11
  43.8 7.0 %attend1.1 = bf16[2,144,1024]{2,1,0:T(8,128)(2,1)S(1)} custom-call(s32[3]{0:T(128)S(1)} %pad_add_fusion.place, bf16[2,1024,128]{2,1,0:T(8,128)(2,1)S(1)} %pad_maximum_fusion.2.q_ref, bf16[8,1024,128]{2,1,0:T(8,128)(2,1)S(1)} %slice_dynamic-update-slice_fusion.kv_ref), custom_call_target="tpu_custom_call" | custom-call | tf_op jit(solution)/shard_map/attend1/pallas_call | solution.py:199
  50.8 2.8 %collective-permute-start.9 = (bf16[2,144,1024]{2,1,0:T(8,128)(2,1)S(1)}, bf16[2,144,1024]{2,1,0:T(8,128)(2,1)S(1)}, u32[]{:S(2)}, u32[]{:S(2)}) collective-permute-start(bf16[2,144,1024]{2,1,0:T(8,128)(2,1)S(1)} %attend1.1), channel_id=1, source_target_pairs={{0,48},{16,0},{32,16},{48,32},{1,49},{17,1},{33,17},{49,33},{2,50}... | collective-permute-start | bytes 1769480 | tf_op jit(solution)/shard_map/ppermute | solution.py:246
  53.7 0.0 collective-permute-done.2.q_ref
  53.7 5.4 %attend3.1 = bf16[2,144,1024]{2,1,0:T(8,128)(2,1)S(1)} custom-call(s32[3]{0:T(128)S(1)} %pad_add_fusion.place, bf16[2,1024,128]{2,1,0:T(8,128)(2,1)S(1)} %collective-permute-done.2.q_ref, bf16[8,1024,128]{2,1,0:T(8,128)(2,1)S(1)} %slice_dynamic-update-slice_fusion.kv_ref), custom_call_target="tpu_custom_call" | custom-call | tf_op jit(solution)/shard_map/attend3/pallas_call | solution.py:199
  59.0 0.2 collective-permute-start.7
  59.3 5.0 %attend0.1.refs_3_ = bf16[2,144,1024]{2,1,0:T(8,128)(2,1)S(1)} custom-call(s32[3]{0:T(128)S(1)} %pad_add_fusion.place, bf16[2,1024,128]{2,1,0:T(8,128)(2,1)S(1)} %pad_maximum_fusion.q_ref, bf16[8,1024,128]{2,1,0:T(8,128)(2,1)S(1)} %slice_dynamic-update-slice_fusion.kv_ref), custom_call_target="tpu_custom_call" | custom-call | tf_op jit(solution)/shard_map/attend0/pallas_call | solution.py:199
  64.3 9.6 %collective-permute-done.9.refs_1_ = bf16[2,144,1024]{2,1,0:T(8,128)(2,1)S(1)} collective-permute-done((bf16[2,144,1024]{2,1,0:T(8,128)(2,1)S(1)}, bf16[2,144,1024]{2,1,0:T(8,128)(2,1)S(1)}, u32[]{:S(2)}, u32[]{:S(2)}) %collective-permute-start.9) | collective-permute-done | bytes 589856 | tf_op jit(solution)/shard_map/ppermute | solution.py:246
  73.9 1.1 %merge.1 = bf16[4,2,128,256]{3,2,1,0:T(8,128)(2,1)S(1)} custom-call(s32[3]{0:T(128)S(1)} %pad_add_fusion.place, bf16[2,144,1024]{2,1,0:T(8,128)(2,1)S(1)} %collective-permute-done.7.refs_0_, bf16[2,144,1024]{2,1,0:T(8,128)(2,1)S(1)} %collective-permute-done.9.refs_1_, bf16[2,144,1024]{2,1,0:T(8,128)(2,1)S(1)} %collective-permute-done.11.refs_2_, ...), custom_call_target="tpu_custom_call" | custom-call | tf_op jit(solution)/shard_map/merge/pallas_call | solution.py:293
  75.1 15.4 %all_to_all.5 = bf16[8,128,256]{2,1,0:T(8,128)(2,1)S(1)} all-to-all(bf16[8,128,256]{2,1,0:T(8,128)(2,1)S(1)} %bitcast.15), channel_id=1, replica_groups=mesh['xl'=2,'y'=4,'z'=4,'xh'=2,'core'=2] {'xh','core','xl'}, dimensions={0} | all-to-all | bytes 1048576 | tf_op jit(solution)/shard_map/all_to_all | solution.py:302
  90.5 0.8 copy.5
  (12 shorter events, 0.3 us)
Async XLA Ops:
  1.9 10.5 %collective-permute-start.3 = (bf16[1024,128]{1,0:T(8,128)(2,1)S(1)}, bf16[1024,128]{1,0:T(8,128)(2,1)S(1)}, u32[]{:S(2)}, u32[]{:S(2)}) collective-permute-start(bf16[1024,128]{1,0:T(8,128)(2,1)S(1)} %get-tuple-element.15), channel_id=1, source_target_pairs={{0,112},{16,96},{32,80},{48,64},{64,48},{80,32},{96,16},{112,0},{1... | collective-permute-start | bytes 786440 | tf_op jit(solution)/shard_map/ppermute | solution.py:255
  6.5 12.4 %collective-permute-start.1 = (bf16[1024,128]{1,0:T(8,128)(2,1)S(1)}, bf16[1024,128]{1,0:T(8,128)(2,1)S(1)}, u32[]{:S(2)}, u32[]{:S(2)}) collective-permute-start(bf16[1024,128]{1,0:T(8,128)(2,1)S(1)} %get-tuple-element.11), channel_id=1, source_target_pairs={{0,16},{16,32},{32,48},{48,0},{1,17},{17,33},{33,49},{49,1},{2,18}... | collective-permute-start | bytes 786440 | tf_op jit(solution)/shard_map/ppermute | solution.py:246
  6.5 12.4 %collective-permute-start = (bf16[1024,128]{1,0:T(8,128)(2,1)S(1)}, bf16[1024,128]{1,0:T(8,128)(2,1)S(1)}, u32[]{:S(2)}, u32[]{:S(2)}) collective-permute-start(bf16[1024,128]{1,0:T(8,128)(2,1)S(1)} %get-tuple-element.12), channel_id=1, source_target_pairs={{0,64},{64,0},{1,65},{65,1},{2,66},{66,2},{3,67},{67,3},{4,68},{68... | collective-permute-start | bytes 786440 | tf_op jit(solution)/shard_map/ppermute | solution.py:246
  12.5 14.9 %collective-permute-start.4 = (bf16[2,1024,128]{2,1,0:T(8,128)(2,1)S(1)}, bf16[2,1024,128]{2,1,0:T(8,128)(2,1)S(1)}, u32[]{:S(2)}, u32[]{:S(2)}) collective-permute-start(bf16[2,1024,128]{2,1,0:T(8,128)(2,1)S(1)} %pad_maximum_fusion.1), channel_id=1, source_target_pairs={{0,4},{4,8},{8,12},{12,0},{1,5},{5,9},{9,13},{13,1},{2,6},{6,10},{... | collective-permute-start | bytes 1572872 | tf_op jit(solution)/shard_map/ppermute | solution.py:246
  14.1 13.4 %collective-permute-start.5 = (bf16[2,1024,128]{2,1,0:T(8,128)(2,1)S(1)}, bf16[2,1024,128]{2,1,0:T(8,128)(2,1)S(1)}, u32[]{:S(2)}, u32[]{:S(2)}) collective-permute-start(bf16[2,1024,128]{2,1,0:T(8,128)(2,1)S(1)} %pad_maximum_fusion.1), channel_id=1, source_target_pairs={{0,12},{4,0},{8,4},{12,8},{1,13},{5,1},{9,5},{13,9},{2,14},{6,2},{... | collective-permute-start | bytes 1572872 | tf_op jit(solution)/shard_map/ppermute | solution.py:246
  18.9 8.5 %collective-permute-start.8 = (bf16[1024,128]{1,0:T(8,128)(2,1)S(1)}, bf16[1024,128]{1,0:T(8,128)(2,1)S(1)}, u32[]{:S(2)}, u32[]{:S(2)}) collective-permute-start(bf16[1024,128]{1,0:T(8,128)(2,1)S(1)} %collective-permute-done), channel_id=1, source_target_pairs={{0,16},{16,32},{32,48},{48,0},{1,17},{17,33},{33,49},{49,1},{2,18}... | collective-permute-start | bytes 786440 | tf_op jit(solution)/shard_map/ppermute | solution.py:246
  18.9 19.2 %collective-permute-start.6 = (bf16[2,1024,128]{2,1,0:T(8,128)(2,1)S(1)}, bf16[2,1024,128]{2,1,0:T(8,128)(2,1)S(1)}, u32[]{:S(2)}, u32[]{:S(2)}) collective-permute-start(bf16[2,1024,128]{2,1,0:T(8,128)(2,1)S(1)} %pad_maximum_fusion.1), channel_id=1, source_target_pairs={{0,8},{4,12},{8,0},{12,4},{1,9},{5,13},{9,1},{13,5},{2,10},{6,14},... | collective-permute-start | bytes 1572872 | tf_op jit(solution)/shard_map/ppermute | solution.py:246
  22.7 15.7 %collective-permute-start.10 = (bf16[2,1024,128]{2,1,0:T(8,128)(2,1)S(1)}, bf16[2,1024,128]{2,1,0:T(8,128)(2,1)S(1)}, u32[]{:S(2)}, u32[]{:S(2)}) collective-permute-start(bf16[2,1024,128]{2,1,0:T(8,128)(2,1)S(1)} %pad_maximum_fusion.q_ref), channel_id=1, source_target_pairs={{0,32},{16,48},{32,0},{48,16},{1,33},{17,49},{33,1},{49,17},{2,34}... | collective-permute-start | bytes 1572872 | tf_op jit(solution)/shard_map/ppermute | solution.py:246
  27.4 26.3 %collective-permute-start.2 = (bf16[2,1024,128]{2,1,0:T(8,128)(2,1)S(1)}, bf16[2,1024,128]{2,1,0:T(8,128)(2,1)S(1)}, u32[]{:S(2)}, u32[]{:S(2)}) collective-permute-start(bf16[2,1024,128]{2,1,0:T(8,128)(2,1)S(1)} %pad_maximum_fusion.q_ref), channel_id=1, source_target_pairs={{0,48},{16,0},{32,16},{48,32},{1,49},{17,1},{33,17},{49,33},{2,50}... | collective-permute-start | bytes 1572872 | tf_op jit(solution)/shard_map/ppermute | solution.py:246
  43.7 20.6 %collective-permute-start.11 = (bf16[2,144,1024]{2,1,0:T(8,128)(2,1)S(1)}, bf16[2,144,1024]{2,1,0:T(8,128)(2,1)S(1)}, u32[]{:S(2)}, u32[]{:S(2)}) collective-permute-start(bf16[2,144,1024]{2,1,0:T(8,128)(2,1)S(1)} %attend2.1), channel_id=1, source_target_pairs={{0,32},{16,48},{32,0},{48,16},{1,33},{17,49},{33,1},{49,17},{2,34}... | collective-permute-start | bytes 1769480 | tf_op jit(solution)/shard_map/ppermute | solution.py:246
  50.8 23.1 %collective-permute-start.9 = (bf16[2,144,1024]{2,1,0:T(8,128)(2,1)S(1)}, bf16[2,144,1024]{2,1,0:T(8,128)(2,1)S(1)}, u32[]{:S(2)}, u32[]{:S(2)}) collective-permute-start(bf16[2,144,1024]{2,1,0:T(8,128)(2,1)S(1)} %attend1.1), channel_id=1, source_target_pairs={{0,48},{16,0},{32,16},{48,32},{1,49},{17,1},{33,17},{49,33},{2,50}... | collective-permute-start | bytes 1769480 | tf_op jit(solution)/shard_map/ppermute | solution.py:246
  59.0 14.9 %collective-permute-start.7 = (bf16[2,144,1024]{2,1,0:T(8,128)(2,1)S(1)}, bf16[2,144,1024]{2,1,0:T(8,128)(2,1)S(1)}, u32[]{:S(2)}, u32[]{:S(2)}) collective-permute-start(bf16[2,144,1024]{2,1,0:T(8,128)(2,1)S(1)} %attend3.1), channel_id=1, source_target_pairs={{0,16},{16,32},{32,48},{48,0},{1,17},{17,33},{33,49},{49,1},{2,18}... | collective-permute-start | bytes 1769480 | tf_op jit(solution)/shard_map/ppermute | solution.py:246

commit v8 on v7

--- a/solution.py
+++ b/solution.py
@@ -161,16 +161,26 @@
                 [jnp.where(z >= 3, part[:BLOCK], LOWEST), part[BLOCK:]], axis=0
             )
 
-        def alone(pair, mask):
-            tile = (slot, row, pair)
-            keys, values = keys_of(tile), values_of(tile)
+        near_tile, far_tile = (slot, row, 0), (slot, row, 1)
+        keys = keys_of(near_tile)
+        for strip in range(STRIPS):
+            score(near_tile, keys, strip, causal)
+
+        @pl.when(z >= 2)
+        def _():
+            values, keys = values_of(near_tile), keys_of(far_tile)
             for strip in range(STRIPS):
-                score(tile, keys, strip, mask)
+                update(near_tile, values, strip)
+                score(far_tile, keys, strip, far)
+            values = values_of(far_tile)
             for strip in range(STRIPS):
-                update(tile, values, strip)
-
-        alone(0, causal)
-        pl.when(z >= 2)(lambda: alone(1, far))
+                update(far_tile, values, strip)
+
+        @pl.when(z < 2)
+        def _():
+            values = values_of(near_tile)
+            for strip in range(STRIPS):
+                update(near_tile, values, strip)
 
     if step == 0:
         on_the_diagonal(0, 0)

time: 93 us -> 93 us (level)
  no operation moved by 1% of the time
where the time goes in v8:
time: 93 us; the launch traced here: 91.3 us
  waiting for transfers between devices  31 us (33%)
  Pallas kernels  26.1 us (28%)
  starting transfers between devices  17.3 us (19%)
  blocking collectives  15.4 us (17%)
  local copies, waits for them, and re-layouts  1.12 us (1%)
    ppermute x11, waiting for transfers between devices, ring(): lax.ppermute(value, axis, [(at, (at + steps) % size) for at in range(size)])  25.3 us
    pallas_call x4, Pallas kernels, attend(): pl.pallas_call(functools.partial(attend_kernel, step), out_shape=jax.Shap...  23.1 us
    all_to_all x1, blocking collectives, on_device(): lax.all_to_all(merged, ('xh', 'core', 'xl'), split_axis=0, concat_axis=0,...  15.4 us
    ppermute x11, starting transfers between devices, ring(): lax.ppermute(value, axis, [(at, (at + steps) % size) for at in range(size)])  12.7 us
    ppermute x1, waiting for transfers between devices, routed(): return lax.ppermute(value, ('xl', 'y'), pairs)  5.7 us
    ppermute x1, starting transfers between devices, routed(): return lax.ppermute(value, ('xl', 'y'), pairs)  4.57 us
    pallas_call x1, Pallas kernels, on_device(): pl.pallas_call(pack_kernel, out_shape=(message,) * 4, in_specs=[smem()] +...  1.86 us
  transfers between devices with their start and end apart: 12, of which 5 were waited for; matrix products, arithmetic and copies ran while one was open for 0% of the time, Pallas kernels for 25%

profile of v8, /device:TPU:1, one launch (start us, length us, event | category | flops | bytes accessed | tf_op | source)
XLA Modules:
  0.0 91.3 jit_solution(13946586404118607035)
XLA Ops:
  0.0 0.1 pad_add_fusion.place
  0.1 1.9 %pack.1 = (bf16[1024,128]{1,0:T(8,128)(2,1)S(1)}, bf16[1024,128]{1,0:T(8,128)(2,1)S(1)}, bf16[1024,128]{1,0:T(8,128)(2,1)S(1)}, bf16[1024,128]{1,0:T(8,128)(2,1)S(1)}) custom-call(s32[3]{0:T(128)S(1)} %pad_add_fusion.place, bf16[512,512]{1,0:T(8,128)(2,1)} %query_in.1, bf16[512,256]{1,0:T(8,128)(2,1)} %key_in.1, bf16[512,256]{1,0:T(8,128)(2,1)} %value_in.1), custom_call_target="tpu_custom_call" | custom-call | tf_op jit(solution)/shard_map/pack/pallas_call | solution.py:272
  1.9 4.6 %collective-permute-start.3 = (bf16[1024,128]{1,0:T(8,128)(2,1)S(1)}, bf16[1024,128]{1,0:T(8,128)(2,1)S(1)}, u32[]{:S(2)}, u32[]{:S(2)}) collective-permute-start(bf16[1024,128]{1,0:T(8,128)(2,1)S(1)} %get-tuple-element.15), channel_id=1, source_target_pairs={{0,112},{16,96},{32,80},{48,64},{64,48},{80,32},{96,16},{112,0},{1... | collective-permute-start | bytes 786440 | tf_op jit(solution)/shard_map/ppermute | solution.py:265
  6.5 0.0 collective-permute-start.1
  6.5 0.3 collective-permute-start
  6.8 5.7 %collective-permute-done.3 = bf16[1024,128]{1,0:T(8,128)(2,1)S(1)} collective-permute-done((bf16[1024,128]{1,0:T(8,128)(2,1)S(1)}, bf16[1024,128]{1,0:T(8,128)(2,1)S(1)}, u32[]{:S(2)}, u32[]{:S(2)}) %collective-permute-start.3) | collective-permute-done | bytes 262176 | tf_op jit(solution)/shard_map/ppermute | solution.py:265
  12.5 0.1 pad_maximum_fusion.1
  12.5 1.6 %collective-permute-start.4 = (bf16[2,1024,128]{2,1,0:T(8,128)(2,1)S(1)}, bf16[2,1024,128]{2,1,0:T(8,128)(2,1)S(1)}, u32[]{:S(2)}, u32[]{:S(2)}) collective-permute-start(bf16[2,1024,128]{2,1,0:T(8,128)(2,1)S(1)} %pad_maximum_fusion.1), channel_id=1, source_target_pairs={{0,4},{4,8},{8,12},{12,0},{1,5},{5,9},{9,13},{13,1},{2,6},{6,10},{... | collective-permute-start | bytes 1572872 | tf_op jit(solution)/shard_map/ppermute | solution.py:256
  14.1 2.2 %collective-permute-start.5 = (bf16[2,1024,128]{2,1,0:T(8,128)(2,1)S(1)}, bf16[2,1024,128]{2,1,0:T(8,128)(2,1)S(1)}, u32[]{:S(2)}, u32[]{:S(2)}) collective-permute-start(bf16[2,1024,128]{2,1,0:T(8,128)(2,1)S(1)} %pad_maximum_fusion.1), channel_id=1, source_target_pairs={{0,12},{4,0},{8,4},{12,8},{1,13},{5,1},{9,5},{13,9},{2,14},{6,2},{... | collective-permute-start | bytes 1572872 | tf_op jit(solution)/shard_map/ppermute | solution.py:256
  16.3 2.6 %collective-permute-done.1 = bf16[1024,128]{1,0:T(8,128)(2,1)S(1)} collective-permute-done((bf16[1024,128]{1,0:T(8,128)(2,1)S(1)}, bf16[1024,128]{1,0:T(8,128)(2,1)S(1)}, u32[]{:S(2)}, u32[]{:S(2)}) %collective-permute-start.1) | collective-permute-done | bytes 262176 | tf_op jit(solution)/shard_map/ppermute | solution.py:256
  18.9 0.0 collective-permute-start.8
  18.9 3.7 %collective-permute-start.6 = (bf16[2,1024,128]{2,1,0:T(8,128)(2,1)S(1)}, bf16[2,1024,128]{2,1,0:T(8,128)(2,1)S(1)}, u32[]{:S(2)}, u32[]{:S(2)}) collective-permute-start(bf16[2,1024,128]{2,1,0:T(8,128)(2,1)S(1)} %pad_maximum_fusion.1), channel_id=1, source_target_pairs={{0,8},{4,12},{8,0},{12,4},{1,9},{5,13},{9,1},{13,5},{2,10},{6,14},... | collective-permute-start | bytes 1572872 | tf_op jit(solution)/shard_map/ppermute | solution.py:256
  22.6 0.1 pad_maximum_fusion.q_ref
  22.7 1.7 %collective-permute-start.10 = (bf16[2,1024,128]{2,1,0:T(8,128)(2,1)S(1)}, bf16[2,1024,128]{2,1,0:T(8,128)(2,1)S(1)}, u32[]{:S(2)}, u32[]{:S(2)}) collective-permute-start(bf16[2,1024,128]{2,1,0:T(8,128)(2,1)S(1)} %pad_maximum_fusion.q_ref), channel_id=1, source_target_pairs={{0,32},{16,48},{32,0},{48,16},{1,33},{17,49},{33,1},{49,17},{2,34}... | collective-permute-start | bytes 1572872 | tf_op jit(solution)/shard_map/ppermute | solution.py:256
  24.4 3.0 %collective-permute-done.8 = bf16[1024,128]{1,0:T(8,128)(2,1)S(1)} collective-permute-done((bf16[1024,128]{1,0:T(8,128)(2,1)S(1)}, bf16[1024,128]{1,0:T(8,128)(2,1)S(1)}, u32[]{:S(2)}, u32[]{:S(2)}) %collective-permute-start.8) | collective-permute-done | bytes 262176 | tf_op jit(solution)/shard_map/ppermute | solution.py:256
  27.4 0.0 collective-permute-start.2
  27.4 0.1 pad_maximum_fusion.2.q_ref
  27.5 0.0 collective-permute-done.4
  27.5 0.0 collective-permute-done.5
  27.6 10.6 %collective-permute-done.6 = bf16[2,1024,128]{2,1,0:T(8,128)(2,1)S(1)} collective-permute-done((bf16[2,1024,128]{2,1,0:T(8,128)(2,1)S(1)}, bf16[2,1024,128]{2,1,0:T(8,128)(2,1)S(1)}, u32[]{:S(2)}, u32[]{:S(2)}) %collective-permute-start.6) | collective-permute-done | bytes 524320 | tf_op jit(solution)/shard_map/ppermute | solution.py:256
  38.4 5.4 %attend2.1 = bf16[2,144,1024]{2,1,0:T(8,128)(2,1)S(1)} custom-call(s32[3]{0:T(128)S(1)} %pad_add_fusion.place, bf16[2,1024,128]{2,1,0:T(8,128)(2,1)S(1)} %collective-permute-done.10.q_ref, bf16[8,1024,128]{2,1,0:T(8,128)(2,1)S(1)} %slice_dynamic-update-slice_fusion.kv_ref), custom_call_target="tpu_custom_call" | custom-call | tf_op jit(solution)/shard_map/attend2/pallas_call | solution.py:209
  43.7 0.1 collective-permute-start.11
  43.8 7.1 %attend1.1 = bf16[2,144,1024]{2,1,0:T(8,128)(2,1)S(1)} custom-call(s32[3]{0:T(128)S(1)} %pad_add_fusion.place, bf16[2,1024,128]{2,1,0:T(8,128)(2,1)S(1)} %pad_maximum_fusion.2.q_ref, bf16[8,1024,128]{2,1,0:T(8,128)(2,1)S(1)} %slice_dynamic-update-slice_fusion.kv_ref), custom_call_target="tpu_custom_call" | custom-call | tf_op jit(solution)/shard_map/attend1/pallas_call | solution.py:209
  51.0 2.7 %collective-permute-start.9 = (bf16[2,144,1024]{2,1,0:T(8,128)(2,1)S(1)}, bf16[2,144,1024]{2,1,0:T(8,128)(2,1)S(1)}, u32[]{:S(2)}, u32[]{:S(2)}) collective-permute-start(bf16[2,144,1024]{2,1,0:T(8,128)(2,1)S(1)} %attend1.1), channel_id=1, source_target_pairs={{0,48},{16,0},{32,16},{48,32},{1,49},{17,1},{33,17},{49,33},{2,50}... | collective-permute-start | bytes 1769480 | tf_op jit(solution)/shard_map/ppermute | solution.py:256
  53.7 0.0 collective-permute-done.2.q_ref
  53.7 5.4 %attend3.1 = bf16[2,144,1024]{2,1,0:T(8,128)(2,1)S(1)} custom-call(s32[3]{0:T(128)S(1)} %pad_add_fusion.place, bf16[2,1024,128]{2,1,0:T(8,128)(2,1)S(1)} %collective-permute-done.2.q_ref, bf16[8,1024,128]{2,1,0:T(8,128)(2,1)S(1)} %slice_dynamic-update-slice_fusion.kv_ref), custom_call_target="tpu_custom_call" | custom-call | tf_op jit(solution)/shard_map/attend3/pallas_call | solution.py:209
  59.0 0.5 collective-permute-start.7
  59.5 5.2 %attend0.1.refs_3_ = bf16[2,144,1024]{2,1,0:T(8,128)(2,1)S(1)} custom-call(s32[3]{0:T(128)S(1)} %pad_add_fusion.place, bf16[2,1024,128]{2,1,0:T(8,128)(2,1)S(1)} %pad_maximum_fusion.q_ref, bf16[8,1024,128]{2,1,0:T(8,128)(2,1)S(1)} %slice_dynamic-update-slice_fusion.kv_ref), custom_call_target="tpu_custom_call" | custom-call | tf_op jit(solution)/shard_map/attend0/pallas_call | solution.py:209
  64.8 9.1 %collective-permute-done.9.refs_1_ = bf16[2,144,1024]{2,1,0:T(8,128)(2,1)S(1)} collective-permute-done((bf16[2,144,1024]{2,1,0:T(8,128)(2,1)S(1)}, bf16[2,144,1024]{2,1,0:T(8,128)(2,1)S(1)}, u32[]{:S(2)}, u32[]{:S(2)}) %collective-permute-start.9) | collective-permute-done | bytes 589856 | tf_op jit(solution)/shard_map/ppermute | solution.py:256
  73.9 1.1 %merge.1 = bf16[4,2,128,256]{3,2,1,0:T(8,128)(2,1)S(1)} custom-call(s32[3]{0:T(128)S(1)} %pad_add_fusion.place, bf16[2,144,1024]{2,1,0:T(8,128)(2,1)S(1)} %collective-permute-done.7.refs_0_, bf16[2,144,1024]{2,1,0:T(8,128)(2,1)S(1)} %collective-permute-done.9.refs_1_, bf16[2,144,1024]{2,1,0:T(8,128)(2,1)S(1)} %collective-permute-done.11.refs_2_, ...), custom_call_target="tpu_custom_call" | custom-call | tf_op jit(solution)/shard_map/merge/pallas_call | solution.py:303
  75.1 15.4 %all_to_all.5 = bf16[8,128,256]{2,1,0:T(8,128)(2,1)S(1)} all-to-all(bf16[8,128,256]{2,1,0:T(8,128)(2,1)S(1)} %bitcast.15), channel_id=1, replica_groups=mesh['xl'=2,'y'=4,'z'=4,'xh'=2,'core'=2] {'xh','core','xl'}, dimensions={0} | all-to-all | bytes 1048576 | tf_op jit(solution)/shard_map/all_to_all | solution.py:312
  90.5 0.8 copy.5
  (12 shorter events, 0.3 us)
Async XLA Ops:
  1.9 10.5 %collective-permute-start.3 = (bf16[1024,128]{1,0:T(8,128)(2,1)S(1)}, bf16[1024,128]{1,0:T(8,128)(2,1)S(1)}, u32[]{:S(2)}, u32[]{:S(2)}) collective-permute-start(bf16[1024,128]{1,0:T(8,128)(2,1)S(1)} %get-tuple-element.15), channel_id=1, source_target_pairs={{0,112},{16,96},{32,80},{48,64},{64,48},{80,32},{96,16},{112,0},{1... | collective-permute-start | bytes 786440 | tf_op jit(solution)/shard_map/ppermute | solution.py:265
  6.5 12.4 %collective-permute-start.1 = (bf16[1024,128]{1,0:T(8,128)(2,1)S(1)}, bf16[1024,128]{1,0:T(8,128)(2,1)S(1)}, u32[]{:S(2)}, u32[]{:S(2)}) collective-permute-start(bf16[1024,128]{1,0:T(8,128)(2,1)S(1)} %get-tuple-element.11), channel_id=1, source_target_pairs={{0,16},{16,32},{32,48},{48,0},{1,17},{17,33},{33,49},{49,1},{2,18}... | collective-permute-start | bytes 786440 | tf_op jit(solution)/shard_map/ppermute | solution.py:256
  6.5 12.4 %collective-permute-start = (bf16[1024,128]{1,0:T(8,128)(2,1)S(1)}, bf16[1024,128]{1,0:T(8,128)(2,1)S(1)}, u32[]{:S(2)}, u32[]{:S(2)}) collective-permute-start(bf16[1024,128]{1,0:T(8,128)(2,1)S(1)} %get-tuple-element.12), channel_id=1, source_target_pairs={{0,64},{64,0},{1,65},{65,1},{2,66},{66,2},{3,67},{67,3},{4,68},{68... | collective-permute-start | bytes 786440 | tf_op jit(solution)/shard_map/ppermute | solution.py:256
  12.5 14.9 %collective-permute-start.4 = (bf16[2,1024,128]{2,1,0:T(8,128)(2,1)S(1)}, bf16[2,1024,128]{2,1,0:T(8,128)(2,1)S(1)}, u32[]{:S(2)}, u32[]{:S(2)}) collective-permute-start(bf16[2,1024,128]{2,1,0:T(8,128)(2,1)S(1)} %pad_maximum_fusion.1), channel_id=1, source_target_pairs={{0,4},{4,8},{8,12},{12,0},{1,5},{5,9},{9,13},{13,1},{2,6},{6,10},{... | collective-permute-start | bytes 1572872 | tf_op jit(solution)/shard_map/ppermute | solution.py:256
  14.1 13.4 %collective-permute-start.5 = (bf16[2,1024,128]{2,1,0:T(8,128)(2,1)S(1)}, bf16[2,1024,128]{2,1,0:T(8,128)(2,1)S(1)}, u32[]{:S(2)}, u32[]{:S(2)}) collective-permute-start(bf16[2,1024,128]{2,1,0:T(8,128)(2,1)S(1)} %pad_maximum_fusion.1), channel_id=1, source_target_pairs={{0,12},{4,0},{8,4},{12,8},{1,13},{5,1},{9,5},{13,9},{2,14},{6,2},{... | collective-permute-start | bytes 1572872 | tf_op jit(solution)/shard_map/ppermute | solution.py:256
  18.9 8.5 %collective-permute-start.8 = (bf16[1024,128]{1,0:T(8,128)(2,1)S(1)}, bf16[1024,128]{1,0:T(8,128)(2,1)S(1)}, u32[]{:S(2)}, u32[]{:S(2)}) collective-permute-start(bf16[1024,128]{1,0:T(8,128)(2,1)S(1)} %collective-permute-done), channel_id=1, source_target_pairs={{0,16},{16,32},{32,48},{48,0},{1,17},{17,33},{33,49},{49,1},{2,18}... | collective-permute-start | bytes 786440 | tf_op jit(solution)/shard_map/ppermute | solution.py:256
  18.9 19.2 %collective-permute-start.6 = (bf16[2,1024,128]{2,1,0:T(8,128)(2,1)S(1)}, bf16[2,1024,128]{2,1,0:T(8,128)(2,1)S(1)}, u32[]{:S(2)}, u32[]{:S(2)}) collective-permute-start(bf16[2,1024,128]{2,1,0:T(8,128)(2,1)S(1)} %pad_maximum_fusion.1), channel_id=1, source_target_pairs={{0,8},{4,12},{8,0},{12,4},{1,9},{5,13},{9,1},{13,5},{2,10},{6,14},... | collective-permute-start | bytes 1572872 | tf_op jit(solution)/shard_map/ppermute | solution.py:256
  22.7 15.7 %collective-permute-start.10 = (bf16[2,1024,128]{2,1,0:T(8,128)(2,1)S(1)}, bf16[2,1024,128]{2,1,0:T(8,128)(2,1)S(1)}, u32[]{:S(2)}, u32[]{:S(2)}) collective-permute-start(bf16[2,1024,128]{2,1,0:T(8,128)(2,1)S(1)} %pad_maximum_fusion.q_ref), channel_id=1, source_target_pairs={{0,32},{16,48},{32,0},{48,16},{1,33},{17,49},{33,1},{49,17},{2,34}... | collective-permute-start | bytes 1572872 | tf_op jit(solution)/shard_map/ppermute | solution.py:256
  27.4 26.3 %collective-permute-start.2 = (bf16[2,1024,128]{2,1,0:T(8,128)(2,1)S(1)}, bf16[2,1024,128]{2,1,0:T(8,128)(2,1)S(1)}, u32[]{:S(2)}, u32[]{:S(2)}) collective-permute-start(bf16[2,1024,128]{2,1,0:T(8,128)(2,1)S(1)} %pad_maximum_fusion.q_ref), channel_id=1, source_target_pairs={{0,48},{16,0},{32,16},{48,32},{1,49},{17,1},{33,17},{49,33},{2,50}... | collective-permute-start | bytes 1572872 | tf_op jit(solution)/shard_map/ppermute | solution.py:256
  43.7 21.0 %collective-permute-start.11 = (bf16[2,144,1024]{2,1,0:T(8,128)(2,1)S(1)}, bf16[2,144,1024]{2,1,0:T(8,128)(2,1)S(1)}, u32[]{:S(2)}, u32[]{:S(2)}) collective-permute-start(bf16[2,144,1024]{2,1,0:T(8,128)(2,1)S(1)} %attend2.1), channel_id=1, source_target_pairs={{0,32},{16,48},{32,0},{48,16},{1,33},{17,49},{33,1},{49,17},{2,34}... | collective-permute-start | bytes 1769480 | tf_op jit(solution)/shard_map/ppermute | solution.py:256
  51.0 23.0 %collective-permute-start.9 = (bf16[2,144,1024]{2,1,0:T(8,128)(2,1)S(1)}, bf16[2,144,1024]{2,1,0:T(8,128)(2,1)S(1)}, u32[]{:S(2)}, u32[]{:S(2)}) collective-permute-start(bf16[2,144,1024]{2,1,0:T(8,128)(2,1)S(1)} %attend1.1), channel_id=1, source_target_pairs={{0,48},{16,0},{32,16},{48,32},{1,49},{17,1},{33,17},{49,33},{2,50}... | collective-permute-start | bytes 1769480 | tf_op jit(solution)/shard_map/ppermute | solution.py:256
  59.0 14.9 %collective-permute-start.7 = (bf16[2,144,1024]{2,1,0:T(8,128)(2,1)S(1)}, bf16[2,144,1024]{2,1,0:T(8,128)(2,1)S(1)}, u32[]{:S(2)}, u32[]{:S(2)}) collective-permute-start(bf16[2,144,1024]{2,1,0:T(8,128)(2,1)S(1)} %attend3.1), channel_id=1, source_target_pairs={{0,16},{16,32},{32,48},{48,0},{1,17},{17,33},{33,49},{49,1},{2,18}... | collective-permute-start | bytes 1769480 | tf_op jit(solution)/shard_map/ppermute | solution.py:256

commit v9 on v8

--- a/solution.py
+++ b/solution.py
@@ -188,27 +188,29 @@
         pl.when(kv_rows[1] == q_rows[1])(lambda: on_the_diagonal(1, 1))
 
     index = lax.broadcasted_iota(jnp.int32, (EXT - HEAD_DIM, STRIP), 0)
-    for slot in range(2):
-        for strip in range(STRIPS):
-            at = slice(strip * STRIP, (strip + 1) * STRIP)
+    for strip in range(STRIPS):
+        at = slice(strip * STRIP, (strip + 1) * STRIP)
+        rows = jnp.zeros((EXT - HEAD_DIM, STRIP), jnp.float32)
+        for slot in range(2):
             total = acc[slot, strip, HEAD_DIM : HEAD_DIM + 1]
             empty = total == 0.0
             inverse = 1.0 / jnp.where(empty, 1.0, total)
-            out_ref[slot, :HEAD_DIM, at] = (acc[slot, strip, :HEAD_DIM] * inverse).astype(
-                jnp.bfloat16
-            )
+            out_ref[slot * HEAD_DIM : (slot + 1) * HEAD_DIM, at] = (
+                acc[slot, strip, :HEAD_DIM] * inverse
+            ).astype(jnp.bfloat16)
             level = best[slot, strip] * SCALE + jnp.log2(jnp.where(empty, 1.0, total))
             high = level.astype(jnp.bfloat16).astype(jnp.float32)
             middle = (level - high).astype(jnp.bfloat16).astype(jnp.float32)
             low = level - high - middle
-            rows = jnp.where(index == 0, high, jnp.where(index == 1, middle, low))
-            out_ref[slot, HEAD_DIM:, at] = rows.astype(jnp.bfloat16)
+            for place_at, value in enumerate((high, middle, low)):
+                rows = jnp.where(index == 3 * slot + place_at, value, rows)
+        out_ref[2 * HEAD_DIM :, at] = rows.astype(jnp.bfloat16)
 
 
 def attend(step, place, queries, blocks):
     return pl.pallas_call(
         functools.partial(attend_kernel, step),
-        out_shape=jax.ShapeDtypeStruct((2, EXT, ROWS), jnp.bfloat16),
+        out_shape=jax.ShapeDtypeStruct((HEAD_DIM + EXT, ROWS), jnp.bfloat16),
         in_specs=[smem()] + vmem(2),
         out_specs=vmem(1)[0],
         scratch_shapes=[
@@ -229,13 +231,13 @@
     for slot in range(2):
         levels = []
         for part in parts:
-            tail = part[slot, HEAD_DIM:].astype(jnp.float32)
-            levels.append(tail[0:1] + tail[1:2] + tail[2:3])
+            tail = part[2 * HEAD_DIM :].astype(jnp.float32)
+            levels.append(sum(tail[3 * slot + at : 3 * slot + at + 1] for at in range(3)))
         top = jnp.maximum(jnp.maximum(levels[0], levels[1]), jnp.maximum(levels[2], levels[3]))
         shares = [jnp.exp2(level - top) for level in levels]
         inverse = 1.0 / (shares[0] + shares[1] + shares[2] + shares[3])
         mixed = sum(
-            part[slot, :HEAD_DIM].astype(jnp.float32) * (share * inverse)
+            part[slot * HEAD_DIM : (slot + 1) * HEAD_DIM].astype(jnp.float32) * (share * inverse)
             for part, share in zip(parts, shares)
         )
         row_half = half if slot == 0 else 1 - half

time: 93 us -> 92.3 us (level)
  waiting for transfers between devices: 31 us -> 29.2 us
  blocking collectives: 15.4 us -> 16.5 us
    ppermute x11, waiting for transfers between devices: 25.3 us -> 23.5 us  [ring(): lax.ppermute(value, axis, [(at, (at + steps) % size) for at in range(size)])]
    all_to_all x1, blocking collectives: 15.4 us -> 16.5 us  [on_device(): lax.all_to_all(merged, ('xh', 'core', 'xl'), split_axis=0, concat_axis=0,...]
where the time goes in v9:
time: 92.3 us; the launch traced here: 90.7 us
  waiting for transfers between devices  29.2 us (32%)
  Pallas kernels  26.1 us (28%)
  starting transfers between devices  17.3 us (19%)
  blocking collectives  16.5 us (18%)
  local copies, waits for them, and re-layouts  1.12 us (1%)
    ppermute x11, waiting for transfers between devices, ring(): lax.ppermute(value, axis, [(at, (at + steps) % size) for at in range(size)])  23.5 us
    pallas_call x4, Pallas kernels, attend(): pl.pallas_call(functools.partial(attend_kernel, step), out_shape=jax.Shap...  23.1 us
    all_to_all x1, blocking collectives, on_device(): lax.all_to_all(merged, ('xh', 'core', 'xl'), split_axis=0, concat_axis=0,...  16.5 us
    ppermute x11, starting transfers between devices, ring(): lax.ppermute(value, axis, [(at, (at + steps) % size) for at in range(size)])  12.7 us
    ppermute x1, waiting for transfers between devices, routed(): return lax.ppermute(value, ('xl', 'y'), pairs)  5.7 us
    ppermute x1, starting transfers between devices, routed(): return lax.ppermute(value, ('xl', 'y'), pairs)  4.57 us
    pallas_call x1, Pallas kernels, on_device(): pl.pallas_call(pack_kernel, out_shape=(message,) * 4, in_specs=[smem()] +...  1.86 us
  transfers between devices with their start and end apart: 12, of which 5 were waited for; matrix products, arithmetic and copies ran while one was open for 0% of the time, Pallas kernels for 25%

profile of v9, /device:TPU:1, one launch (start us, length us, event | category | flops | bytes accessed | tf_op | source)
XLA Modules:
  0.0 90.7 jit_solution(12967071827601798825)
XLA Ops:
  0.0 0.1 pad_add_fusion.place
  0.1 1.9 %pack.1 = (bf16[1024,128]{1,0:T(8,128)(2,1)S(1)}, bf16[1024,128]{1,0:T(8,128)(2,1)S(1)}, bf16[1024,128]{1,0:T(8,128)(2,1)S(1)}, bf16[1024,128]{1,0:T(8,128)(2,1)S(1)}) custom-call(s32[3]{0:T(128)S(1)} %pad_add_fusion.place, bf16[512,512]{1,0:T(8,128)(2,1)} %query_in.1, bf16[512,256]{1,0:T(8,128)(2,1)} %key_in.1, bf16[512,256]{1,0:T(8,128)(2,1)} %value_in.1), custom_call_target="tpu_custom_call" | custom-call | tf_op jit(solution)/shard_map/pack/pallas_call | solution.py:274
  1.9 4.6 %collective-permute-start.3 = (bf16[1024,128]{1,0:T(8,128)(2,1)S(1)}, bf16[1024,128]{1,0:T(8,128)(2,1)S(1)}, u32[]{:S(2)}, u32[]{:S(2)}) collective-permute-start(bf16[1024,128]{1,0:T(8,128)(2,1)S(1)} %get-tuple-element.15), channel_id=1, source_target_pairs={{0,112},{16,96},{32,80},{48,64},{64,48},{80,32},{96,16},{112,0},{1... | collective-permute-start | bytes 786440 | tf_op jit(solution)/shard_map/ppermute | solution.py:267
  6.5 0.0 collective-permute-start.1
  6.5 0.3 collective-permute-start
  6.8 5.7 %collective-permute-done.3 = bf16[1024,128]{1,0:T(8,128)(2,1)S(1)} collective-permute-done((bf16[1024,128]{1,0:T(8,128)(2,1)S(1)}, bf16[1024,128]{1,0:T(8,128)(2,1)S(1)}, u32[]{:S(2)}, u32[]{:S(2)}) %collective-permute-start.3) | collective-permute-done | bytes 262176 | tf_op jit(solution)/shard_map/ppermute | solution.py:267
  12.5 0.1 pad_maximum_fusion.1
  12.5 1.6 %collective-permute-start.4 = (bf16[2,1024,128]{2,1,0:T(8,128)(2,1)S(1)}, bf16[2,1024,128]{2,1,0:T(8,128)(2,1)S(1)}, u32[]{:S(2)}, u32[]{:S(2)}) collective-permute-start(bf16[2,1024,128]{2,1,0:T(8,128)(2,1)S(1)} %pad_maximum_fusion.1), channel_id=1, source_target_pairs={{0,4},{4,8},{8,12},{12,0},{1,5},{5,9},{9,13},{13,1},{2,6},{6,10},{... | collective-permute-start | bytes 1572872 | tf_op jit(solution)/shard_map/ppermute | solution.py:258
  14.1 2.2 %collective-permute-start.5 = (bf16[2,1024,128]{2,1,0:T(8,128)(2,1)S(1)}, bf16[2,1024,128]{2,1,0:T(8,128)(2,1)S(1)}, u32[]{:S(2)}, u32[]{:S(2)}) collective-permute-start(bf16[2,1024,128]{2,1,0:T(8,128)(2,1)S(1)} %pad_maximum_fusion.1), channel_id=1, source_target_pairs={{0,12},{4,0},{8,4},{12,8},{1,13},{5,1},{9,5},{13,9},{2,14},{6,2},{... | collective-permute-start | bytes 1572872 | tf_op jit(solution)/shard_map/ppermute | solution.py:258
  16.3 2.6 %collective-permute-done.1 = bf16[1024,128]{1,0:T(8,128)(2,1)S(1)} collective-permute-done((bf16[1024,128]{1,0:T(8,128)(2,1)S(1)}, bf16[1024,128]{1,0:T(8,128)(2,1)S(1)}, u32[]{:S(2)}, u32[]{:S(2)}) %collective-permute-start.1) | collective-permute-done | bytes 262176 | tf_op jit(solution)/shard_map/ppermute | solution.py:258
  18.9 0.0 collective-permute-done
  18.9 0.0 collective-permute-start.8
  18.9 3.7 %collective-permute-start.6 = (bf16[2,1024,128]{2,1,0:T(8,128)(2,1)S(1)}, bf16[2,1024,128]{2,1,0:T(8,128)(2,1)S(1)}, u32[]{:S(2)}, u32[]{:S(2)}) collective-permute-start(bf16[2,1024,128]{2,1,0:T(8,128)(2,1)S(1)} %pad_maximum_fusion.1), channel_id=1, source_target_pairs={{0,8},{4,12},{8,0},{12,4},{1,9},{5,13},{9,1},{13,5},{2,10},{6,14},... | collective-permute-start | bytes 1572872 | tf_op jit(solution)/shard_map/ppermute | solution.py:258
  22.6 0.1 pad_maximum_fusion.q_ref
  22.7 1.7 %collective-permute-start.10 = (bf16[2,1024,128]{2,1,0:T(8,128)(2,1)S(1)}, bf16[2,1024,128]{2,1,0:T(8,128)(2,1)S(1)}, u32[]{:S(2)}, u32[]{:S(2)}) collective-permute-start(bf16[2,1024,128]{2,1,0:T(8,128)(2,1)S(1)} %pad_maximum_fusion.q_ref), channel_id=1, source_target_pairs={{0,32},{16,48},{32,0},{48,16},{1,33},{17,49},{33,1},{49,17},{2,34}... | collective-permute-start | bytes 1572872 | tf_op jit(solution)/shard_map/ppermute | solution.py:258
  24.4 3.0 %collective-permute-done.8 = bf16[1024,128]{1,0:T(8,128)(2,1)S(1)} collective-permute-done((bf16[1024,128]{1,0:T(8,128)(2,1)S(1)}, bf16[1024,128]{1,0:T(8,128)(2,1)S(1)}, u32[]{:S(2)}, u32[]{:S(2)}) %collective-permute-start.8) | collective-permute-done | bytes 262176 | tf_op jit(solution)/shard_map/ppermute | solution.py:258
  27.4 0.0 collective-permute-start.2
  27.4 0.1 pad_maximum_fusion.2.q_ref
  27.6 10.6 %collective-permute-done.6 = bf16[2,1024,128]{2,1,0:T(8,128)(2,1)S(1)} collective-permute-done((bf16[2,1024,128]{2,1,0:T(8,128)(2,1)S(1)}, bf16[2,1024,128]{2,1,0:T(8,128)(2,1)S(1)}, u32[]{:S(2)}, u32[]{:S(2)}) %collective-permute-start.6) | collective-permute-done | bytes 524320 | tf_op jit(solution)/shard_map/ppermute | solution.py:258
  38.4 5.4 %attend2.1 = bf16[272,1024]{1,0:T(8,128)(2,1)S(1)} custom-call(s32[3]{0:T(128)S(1)} %pad_add_fusion.place, bf16[2,1024,128]{2,1,0:T(8,128)(2,1)S(1)} %collective-permute-done.10.q_ref, bf16[8,1024,128]{2,1,0:T(8,128)(2,1)S(1)} %slice_dynamic-update-slice_fusion.kv_ref), custom_call_target="tpu_custom_call" | custom-call | tf_op jit(solution)/shard_map/attend2/pallas_call | solution.py:211
  43.7 0.1 collective-permute-start.11
  43.8 7.1 %attend1.1 = bf16[272,1024]{1,0:T(8,128)(2,1)S(1)} custom-call(s32[3]{0:T(128)S(1)} %pad_add_fusion.place, bf16[2,1024,128]{2,1,0:T(8,128)(2,1)S(1)} %pad_maximum_fusion.2.q_ref, bf16[8,1024,128]{2,1,0:T(8,128)(2,1)S(1)} %slice_dynamic-update-slice_fusion.kv_ref), custom_call_target="tpu_custom_call" | custom-call | tf_op jit(solution)/shard_map/attend1/pallas_call | solution.py:211
  51.0 2.7 %collective-permute-start.9 = (bf16[272,1024]{1,0:T(8,128)(2,1)S(1)}, bf16[272,1024]{1,0:T(8,128)(2,1)S(1)}, u32[]{:S(2)}, u32[]{:S(2)}) collective-permute-start(bf16[272,1024]{1,0:T(8,128)(2,1)S(1)} %attend1.1), channel_id=1, source_target_pairs={{0,48},{16,0},{32,16},{48,32},{1,49},{17,1},{33,17},{49,33},{2,50}... | collective-permute-start | bytes 1671176 | tf_op jit(solution)/shard_map/ppermute | solution.py:258
  53.7 0.0 collective-permute-done.2.q_ref
  53.7 5.4 %attend3.1 = bf16[272,1024]{1,0:T(8,128)(2,1)S(1)} custom-call(s32[3]{0:T(128)S(1)} %pad_add_fusion.place, bf16[2,1024,128]{2,1,0:T(8,128)(2,1)S(1)} %collective-permute-done.2.q_ref, bf16[8,1024,128]{2,1,0:T(8,128)(2,1)S(1)} %slice_dynamic-update-slice_fusion.kv_ref), custom_call_target="tpu_custom_call" | custom-call | tf_op jit(solution)/shard_map/attend3/pallas_call | solution.py:211
  59.1 0.5 collective-permute-start.7
  59.6 5.2 %attend0.1.refs_3_ = bf16[272,1024]{1,0:T(8,128)(2,1)S(1)} custom-call(s32[3]{0:T(128)S(1)} %pad_add_fusion.place, bf16[2,1024,128]{2,1,0:T(8,128)(2,1)S(1)} %pad_maximum_fusion.q_ref, bf16[8,1024,128]{2,1,0:T(8,128)(2,1)S(1)} %slice_dynamic-update-slice_fusion.kv_ref), custom_call_target="tpu_custom_call" | custom-call | tf_op jit(solution)/shard_map/attend0/pallas_call | solution.py:211
  64.8 0.0 collective-permute-done.11.refs_2_
  64.8 7.3 %collective-permute-done.9.refs_1_ = bf16[272,1024]{1,0:T(8,128)(2,1)S(1)} collective-permute-done((bf16[272,1024]{1,0:T(8,128)(2,1)S(1)}, bf16[272,1024]{1,0:T(8,128)(2,1)S(1)}, u32[]{:S(2)}, u32[]{:S(2)}) %collective-permute-start.9) | collective-permute-done | bytes 557088 | tf_op jit(solution)/shard_map/ppermute | solution.py:258
  72.1 1.1 %merge.1 = bf16[4,2,128,256]{3,2,1,0:T(8,128)(2,1)S(1)} custom-call(s32[3]{0:T(128)S(1)} %pad_add_fusion.place, bf16[272,1024]{1,0:T(8,128)(2,1)S(1)} %collective-permute-done.7.refs_0_, bf16[272,1024]{1,0:T(8,128)(2,1)S(1)} %collective-permute-done.9.refs_1_, bf16[272,1024]{1,0:T(8,128)(2,1)S(1)} %collective-permute-done.11.refs_2_, ...), custom_call_target="tpu_custom_call" | custom-call | tf_op jit(solution)/shard_map/merge/pallas_call | solution.py:305
  73.3 16.5 %all_to_all.5 = bf16[8,128,256]{2,1,0:T(8,128)(2,1)S(1)} all-to-all(bf16[8,128,256]{2,1,0:T(8,128)(2,1)S(1)} %bitcast.15), channel_id=1, replica_groups=mesh['xl'=2,'y'=4,'z'=4,'xh'=2,'core'=2] {'xh','core','xl'}, dimensions={0} | all-to-all | bytes 1048576 | tf_op jit(solution)/shard_map/all_to_all | solution.py:314
  89.8 0.8 copy.5
  (12 shorter events, 0.3 us)
Async XLA Ops:
  1.9 10.5 %collective-permute-start.3 = (bf16[1024,128]{1,0:T(8,128)(2,1)S(1)}, bf16[1024,128]{1,0:T(8,128)(2,1)S(1)}, u32[]{:S(2)}, u32[]{:S(2)}) collective-permute-start(bf16[1024,128]{1,0:T(8,128)(2,1)S(1)} %get-tuple-element.15), channel_id=1, source_target_pairs={{0,112},{16,96},{32,80},{48,64},{64,48},{80,32},{96,16},{112,0},{1... | collective-permute-start | bytes 786440 | tf_op jit(solution)/shard_map/ppermute | solution.py:267
  6.5 12.4 %collective-permute-start.1 = (bf16[1024,128]{1,0:T(8,128)(2,1)S(1)}, bf16[1024,128]{1,0:T(8,128)(2,1)S(1)}, u32[]{:S(2)}, u32[]{:S(2)}) collective-permute-start(bf16[1024,128]{1,0:T(8,128)(2,1)S(1)} %get-tuple-element.11), channel_id=1, source_target_pairs={{0,16},{16,32},{32,48},{48,0},{1,17},{17,33},{33,49},{49,1},{2,18}... | collective-permute-start | bytes 786440 | tf_op jit(solution)/shard_map/ppermute | solution.py:258
  6.5 12.4 %collective-permute-start = (bf16[1024,128]{1,0:T(8,128)(2,1)S(1)}, bf16[1024,128]{1,0:T(8,128)(2,1)S(1)}, u32[]{:S(2)}, u32[]{:S(2)}) collective-permute-start(bf16[1024,128]{1,0:T(8,128)(2,1)S(1)} %get-tuple-element.12), channel_id=1, source_target_pairs={{0,64},{64,0},{1,65},{65,1},{2,66},{66,2},{3,67},{67,3},{4,68},{68... | collective-permute-start | bytes 786440 | tf_op jit(solution)/shard_map/ppermute | solution.py:258
  12.5 14.9 %collective-permute-start.4 = (bf16[2,1024,128]{2,1,0:T(8,128)(2,1)S(1)}, bf16[2,1024,128]{2,1,0:T(8,128)(2,1)S(1)}, u32[]{:S(2)}, u32[]{:S(2)}) collective-permute-start(bf16[2,1024,128]{2,1,0:T(8,128)(2,1)S(1)} %pad_maximum_fusion.1), channel_id=1, source_target_pairs={{0,4},{4,8},{8,12},{12,0},{1,5},{5,9},{9,13},{13,1},{2,6},{6,10},{... | collective-permute-start | bytes 1572872 | tf_op jit(solution)/shard_map/ppermute | solution.py:258
  14.1 13.4 %collective-permute-start.5 = (bf16[2,1024,128]{2,1,0:T(8,128)(2,1)S(1)}, bf16[2,1024,128]{2,1,0:T(8,128)(2,1)S(1)}, u32[]{:S(2)}, u32[]{:S(2)}) collective-permute-start(bf16[2,1024,128]{2,1,0:T(8,128)(2,1)S(1)} %pad_maximum_fusion.1), channel_id=1, source_target_pairs={{0,12},{4,0},{8,4},{12,8},{1,13},{5,1},{9,5},{13,9},{2,14},{6,2},{... | collective-permute-start | bytes 1572872 | tf_op jit(solution)/shard_map/ppermute | solution.py:258
  18.9 8.5 %collective-permute-start.8 = (bf16[1024,128]{1,0:T(8,128)(2,1)S(1)}, bf16[1024,128]{1,0:T(8,128)(2,1)S(1)}, u32[]{:S(2)}, u32[]{:S(2)}) collective-permute-start(bf16[1024,128]{1,0:T(8,128)(2,1)S(1)} %collective-permute-done), channel_id=1, source_target_pairs={{0,16},{16,32},{32,48},{48,0},{1,17},{17,33},{33,49},{49,1},{2,18}... | collective-permute-start | bytes 786440 | tf_op jit(solution)/shard_map/ppermute | solution.py:258
  18.9 19.2 %collective-permute-start.6 = (bf16[2,1024,128]{2,1,0:T(8,128)(2,1)S(1)}, bf16[2,1024,128]{2,1,0:T(8,128)(2,1)S(1)}, u32[]{:S(2)}, u32[]{:S(2)}) collective-permute-start(bf16[2,1024,128]{2,1,0:T(8,128)(2,1)S(1)} %pad_maximum_fusion.1), channel_id=1, source_target_pairs={{0,8},{4,12},{8,0},{12,4},{1,9},{5,13},{9,1},{13,5},{2,10},{6,14},... | collective-permute-start | bytes 1572872 | tf_op jit(solution)/shard_map/ppermute | solution.py:258
  22.7 15.7 %collective-permute-start.10 = (bf16[2,1024,128]{2,1,0:T(8,128)(2,1)S(1)}, bf16[2,1024,128]{2,1,0:T(8,128)(2,1)S(1)}, u32[]{:S(2)}, u32[]{:S(2)}) collective-permute-start(bf16[2,1024,128]{2,1,0:T(8,128)(2,1)S(1)} %pad_maximum_fusion.q_ref), channel_id=1, source_target_pairs={{0,32},{16,48},{32,0},{48,16},{1,33},{17,49},{33,1},{49,17},{2,34}... | collective-permute-start | bytes 1572872 | tf_op jit(solution)/shard_map/ppermute | solution.py:258
  27.4 26.3 %collective-permute-start.2 = (bf16[2,1024,128]{2,1,0:T(8,128)(2,1)S(1)}, bf16[2,1024,128]{2,1,0:T(8,128)(2,1)S(1)}, u32[]{:S(2)}, u32[]{:S(2)}) collective-permute-start(bf16[2,1024,128]{2,1,0:T(8,128)(2,1)S(1)} %pad_maximum_fusion.q_ref), channel_id=1, source_target_pairs={{0,48},{16,0},{32,16},{48,32},{1,49},{17,1},{33,17},{49,33},{2,50}... | collective-permute-start | bytes 1572872 | tf_op jit(solution)/shard_map/ppermute | solution.py:258
  43.7 21.1 %collective-permute-start.11 = (bf16[272,1024]{1,0:T(8,128)(2,1)S(1)}, bf16[272,1024]{1,0:T(8,128)(2,1)S(1)}, u32[]{:S(2)}, u32[]{:S(2)}) collective-permute-start(bf16[272,1024]{1,0:T(8,128)(2,1)S(1)} %attend2.1), channel_id=1, source_target_pairs={{0,32},{16,48},{32,0},{48,16},{1,33},{17,49},{33,1},{49,17},{2,34}... | collective-permute-start | bytes 1671176 | tf_op jit(solution)/shard_map/ppermute | solution.py:258
  51.0 21.1 %collective-permute-start.9 = (bf16[272,1024]{1,0:T(8,128)(2,1)S(1)}, bf16[272,1024]{1,0:T(8,128)(2,1)S(1)}, u32[]{:S(2)}, u32[]{:S(2)}) collective-permute-start(bf16[272,1024]{1,0:T(8,128)(2,1)S(1)} %attend1.1), channel_id=1, source_target_pairs={{0,48},{16,0},{32,16},{48,32},{1,49},{17,1},{33,17},{49,33},{2,50}... | collective-permute-start | bytes 1671176 | tf_op jit(solution)/shard_map/ppermute | solution.py:258
  59.1 13.1 %collective-permute-start.7 = (bf16[272,1024]{1,0:T(8,128)(2,1)S(1)}, bf16[272,1024]{1,0:T(8,128)(2,1)S(1)}, u32[]{:S(2)}, u32[]{:S(2)}) collective-permute-start(bf16[272,1024]{1,0:T(8,128)(2,1)S(1)} %attend3.1), channel_id=1, source_target_pairs={{0,16},{16,32},{32,48},{48,0},{1,17},{17,33},{33,49},{49,1},{2,18}... | collective-permute-start | bytes 1671176 | tf_op jit(solution)/shard_map/ppermute | solution.py:258
